TPU v7x, 32 devices: a whole 2x2x4 slice. The times are simulated.
32 devices in a mesh: dp: 4 (over y, core), rep: 2 (over x), tensor: 4 (over z).
Axes of the slice: x: 2, y: 2, z: 4, core: 2. Of those that a mesh axis runs over, the one named last changes fastest.
Arguments:
- query_tokens: bfloat16 [2, 8, 256, 768], P(None, ('dp', 'rep')), may hold values from -6 to 6
- query_drop: int32 [2, 8, 256], P(None, ('dp', 'rep')), may hold values 0 or 1
- query_length: int32 [2, 8], P(None, ('dp', 'rep')), may hold values from 1 to 256, 1280 in all within a row
- key_tokens: bfloat16 [2, 8, 256, 768], P(None, ('dp', 'rep')), may hold values from -6 to 6
- key_drop: int32 [2, 8, 256], P(None, ('dp', 'rep')), may hold values 0 or 1
- key_length: int32 [2, 8], P(None, ('dp', 'rep')), may hold values from 1 to 256, 1280 in all within a row
- negatives: bfloat16 [8192, 768], P(('rep', 'tensor')), may hold values from -0.59765625 to 0.59765625
- attend_weight: bfloat16 [2, 2, 768, 3, 768], P(None, None, None, None, 'tensor'), may hold values from -0.21875 to 0.21875
- attend_bias: bfloat16 [2, 2, 2, 768], P(None, None, None, 'tensor'), may hold values from -1.5 to 1.5
- merge_weight: bfloat16 [2, 2, 768, 768], P(None, None, 'tensor'), may hold values from -0.875 to 0.875
- merge_bias: bfloat16 [2, 2, 768], replicated, may hold values from -1.5 to 1.5
- expand_weight: bfloat16 [2, 2, 768, 3072], P(None, None, None, 'tensor'), may hold values from -0.21875 to 0.21875
- expand_bias: bfloat16 [2, 2, 3072], P(None, None, 'tensor'), may hold values from -1.5 to 1.5
- shrink_weight: bfloat16 [2, 2, 3072, 768], P(None, None, 'tensor'), may hold values from -0.109375 to 0.109375
- shrink_bias: bfloat16 [2, 2, 768], replicated, may hold values from -1.5 to 1.5
- norm_gain: bfloat16 [2, 2, 2, 768], replicated, may hold values from 0.5 to 1.5
- norm_shift: bfloat16 [2, 2, 2, 768], replicated, may hold values from -1.5 to 1.5
Outputs:
- activations: bfloat16 [2, 8, 256, 768], P(None, ('dp', 'rep'), 'tensor')
- input_grad: bfloat16 [2, 8, 256, 768], P(None, ('dp', 'rep'), 'tensor')
- attend_weight_grad: float32 [2, 768, 3, 768], P(None, ('dp', 'rep'), None, 'tensor')
- attend_bias_grad: float32 [2, 2, 768], P(None, None, 'tensor')
- merge_weight_grad: float32 [2, 768, 768], P(None, 'tensor', ('dp', 'rep'))
- merge_bias_grad: float32 [2, 768], P(None, ('dp', 'rep'))
- expand_weight_grad: float32 [2, 768, 3072], P(None, ('dp', 'rep'), 'tensor')
- expand_bias_grad: float32 [2, 3072], P(None, 'tensor')
- shrink_weight_grad: float32 [2, 3072, 768], P(None, 'tensor', ('dp', 'rep'))
- shrink_bias_grad: float32 [2, 768], P(None, ('dp', 'rep'))
- norm_gain_grad: float32 [2, 2, 768], P(None, None, ('dp', 'rep'))
- norm_shift_grad: float32 [2, 2, 768], P(None, None, ('dp', 'rep'))
- loss: float32 [], replicated
Inputs may be any that keep to these rules, and one draw needn't show every extreme that they name: `query_length`: in each micro-batch the lengths of the 8 query crops sum to 1280 and the longest is exactly 256. `key_length`: in each micro-batch the lengths of the 8 key crops sum to 1280 and the longest is exactly 256.
All inputs are finite; a program needn't handle non-finite values. No bound on the sum of `query_drop` or of `query_length` or of `key_drop` or of `key_length` on one device may be relied on, other than what follows from the above.
Results may differ from a plain program's by a relative error of at most 0.018.
Values may be sent and summed in bfloat16 or wider, within the bound.
A program may use at most 192 MiB of HBM per device.

v0:
```python
import jax
import jax.numpy as jnp
from jax import lax
from jax.sharding import PartitionSpec as P

HEAD_DIM = 64
CROP_SLOTS = 256


SOFTMAX_WARMTH = 0.05
NORM_EPS = 1e-12
UNIT_EPS = 1e-06
MASKED = -1e30
TOP_PRECISION = lax.Precision.HIGHEST
ROOT_HALF = 0.7071067811865476
INV_ROOT_TAU = 0.3989422804014327


def packing_plan(dropped_flags, crop_lengths):
    position = lax.broadcasted_iota(jnp.int32, dropped_flags.shape, dropped_flags.ndim - 1)
    retained_flag = (
        (position < crop_lengths[..., None]) & ((dropped_flags == 0) | (position == 0))
    ).astype(jnp.int32)
    slot_lookup = jnp.cumsum(retained_flag, axis=-1) - 1
    token_counts = jnp.sum(retained_flag, axis=-1)
    matches = (slot_lookup[..., None, :] == position[..., :, None]) & (
        retained_flag[..., None, :] == 1
    )
    source_index = jnp.sum(jnp.where(matches, position[..., None, :], 0), axis=-1)
    return (retained_flag, slot_lookup, source_index, token_counts)


def branch_total(partial_value):
    return lax.psum_scatter(partial_value, "tensor", scatter_dimension=1, tiled=True)


def rows_gather(piece):
    return lax.all_gather(piece, "tensor", axis=1, tiled=True)


def grad_gather(piece):
    return lax.all_gather(piece, "tensor", axis=1, tiled=True)


def grad_total(partial_value):
    return lax.psum_scatter(partial_value, "tensor", scatter_dimension=1, tiled=True)


def apply_matrix(rows_three, matrix):
    result = jnp.dot(
        rows_three.reshape(-1, rows_three.shape[-1]), matrix, preferred_element_type=jnp.float32
    )
    return result.reshape(rows_three.shape[:-1] + (matrix.shape[-1],))


def apply_transposed(rows_three, matrix):
    result = lax.dot_general(
        rows_three.reshape(-1, rows_three.shape[-1]),
        matrix,
        (((1,), (1,)), ((), ())),
        preferred_element_type=jnp.float32,
    )
    return result.reshape(rows_three.shape[:-1] + (matrix.shape[0],))


def rows_product(left_rows, right_rows):
    return lax.dot_general(
        left_rows.reshape(-1, left_rows.shape[-1]),
        right_rows.reshape(-1, right_rows.shape[-1]),
        (((0,), (0,)), ((), ())),
        preferred_element_type=jnp.float32,
    )


def norm_forward(total_rows, gain_row, shift_row):
    mean_row = jnp.mean(total_rows, axis=-1, keepdims=True)
    centered = total_rows - mean_row
    inverse = lax.rsqrt(jnp.mean(centered * centered, axis=-1, keepdims=True) + NORM_EPS)
    normed = centered * inverse
    return (normed * gain_row + shift_row, normed, inverse)


def norm_backward(grad_rows_in, normed, inverse, gain_row):
    scaled = grad_rows_in * gain_row
    back = inverse * (
        scaled
        - jnp.mean(scaled, axis=-1, keepdims=True)
        - normed * jnp.mean(scaled * normed, axis=-1, keepdims=True)
    )
    return (back, jnp.sum(grad_rows_in * normed, axis=(0, 1)), jnp.sum(grad_rows_in, axis=(0, 1)))


def gelu_slope(inner_pre):
    return (
        0.5 * (1.0 + lax.erf(inner_pre * ROOT_HALF))
        + inner_pre * jnp.exp(-0.5 * inner_pre * inner_pre) * INV_ROOT_TAU
    )


def layer_pass(hidden_share, hidden_full, params, valid_keys):
    (
        heads_matrix,
        heads_offset,
        merge_matrix,
        merge_offset,
        expand_matrix,
        expand_offset,
        shrink_matrix,
        shrink_offset,
        gain_rows,
        shift_rows,
    ) = params
    crop_count, row_count, model_width = hidden_full.shape
    local_width = heads_matrix.shape[-1]
    head_count = local_width // HEAD_DIM
    head_shape = (crop_count, row_count, head_count, HEAD_DIM)
    project = apply_matrix(hidden_full, heads_matrix.reshape(model_width, 3 * local_width)).reshape(
        crop_count, row_count, 3, local_width
    )
    queries = (project[:, :, 0] + heads_offset[0]).astype(jnp.bfloat16).reshape(head_shape)
    key_rows = project[:, :, 1].astype(jnp.bfloat16).reshape(head_shape)
    values = (project[:, :, 2] + heads_offset[1]).astype(jnp.bfloat16).reshape(head_shape)
    raw_scores = jnp.einsum(
        "cqhe,ckhe->chqk", queries, key_rows, preferred_element_type=jnp.float32
    )
    scores = jnp.where(valid_keys[:, None, None, :], raw_scores * HEAD_DIM ** (-0.5), MASKED)
    row_top = jnp.max(scores, axis=-1, keepdims=True)
    exponent = jnp.exp(scores - row_top)
    chances = exponent / jnp.sum(exponent, axis=-1, keepdims=True)
    chances_low = chances.astype(jnp.bfloat16)
    mixed_heads = (
        jnp.einsum("chqk,ckhe->cqhe", chances_low, values, preferred_element_type=jnp.float32)
        .astype(jnp.bfloat16)
        .reshape(crop_count, row_count, local_width)
    )
    branch = branch_total(apply_matrix(mixed_heads, merge_matrix))
    first_norm, normed_one, inverse_one = norm_forward(
        hidden_share + branch + merge_offset, gain_rows[0], shift_rows[0]
    )
    first_full = rows_gather(first_norm.astype(jnp.bfloat16))
    inner_pre = apply_matrix(first_full, expand_matrix) + expand_offset
    active = jax.nn.gelu(inner_pre, approximate=False).astype(jnp.bfloat16)
    second = branch_total(apply_matrix(active, shrink_matrix))
    output, normed_two, inverse_two = norm_forward(
        first_norm + second + shrink_offset, gain_rows[1], shift_rows[1]
    )
    kept_state = (
        queries,
        key_rows,
        values,
        chances,
        chances_low,
        mixed_heads,
        normed_one,
        inverse_one,
        first_full,
        inner_pre,
        active,
        normed_two,
        inverse_two,
    )
    return (output, kept_state)


def layer_back(grad_out, kept_state, hidden_full, params):
    (
        queries,
        key_rows,
        values,
        chances,
        chances_low,
        mixed_heads,
        normed_one,
        inverse_one,
        first_full,
        inner_pre,
        active,
        normed_two,
        inverse_two,
    ) = kept_state
    (
        heads_matrix,
        heads_offset,
        merge_matrix,
        merge_offset,
        expand_matrix,
        expand_offset,
        shrink_matrix,
        shrink_offset,
        gain_rows,
        shift_rows,
    ) = params
    crop_count, row_count, model_width = hidden_full.shape
    local_width = heads_matrix.shape[-1]
    head_count = local_width // HEAD_DIM
    total_two, gain_two, shift_two = norm_backward(grad_out, normed_two, inverse_two, gain_rows[1])
    shrink_bias_part = jnp.sum(total_two, axis=(0, 1))
    second_low = grad_gather(total_two.astype(jnp.bfloat16))
    shrink_grad = rows_product(active, second_low)
    inner_grad = apply_transposed(second_low, shrink_matrix) * gelu_slope(inner_pre)
    expand_bias_part = jnp.sum(inner_grad, axis=(0, 1))
    inner_low = inner_grad.astype(jnp.bfloat16)
    expand_grad = rows_product(first_full, inner_low)
    first_grad = grad_total(apply_transposed(inner_low, expand_matrix)) + total_two
    total_one, gain_one, shift_one = norm_backward(
        first_grad, normed_one, inverse_one, gain_rows[0]
    )
    merge_bias_part = jnp.sum(total_one, axis=(0, 1))
    branch_low = grad_gather(total_one.astype(jnp.bfloat16))
    merge_grad = rows_product(mixed_heads, branch_low)
    mixed_grad = (
        apply_transposed(branch_low, merge_matrix)
        .astype(jnp.bfloat16)
        .reshape(crop_count, row_count, head_count, HEAD_DIM)
    )
    value_grad = jnp.einsum(
        "chqk,cqhe->ckhe", chances_low, mixed_grad, preferred_element_type=jnp.float32
    )
    chance_grad = jnp.einsum(
        "cqhe,ckhe->chqk", mixed_grad, values, preferred_element_type=jnp.float32
    )
    score_grad = chances * (chance_grad - jnp.sum(chances * chance_grad, axis=-1, keepdims=True))
    raw_grad = (score_grad * HEAD_DIM ** (-0.5)).astype(jnp.bfloat16)
    query_grad = jnp.einsum(
        "chqk,ckhe->cqhe", raw_grad, key_rows, preferred_element_type=jnp.float32
    )
    key_grad = jnp.einsum("chqk,cqhe->ckhe", raw_grad, queries, preferred_element_type=jnp.float32)
    flat_shape = (crop_count, row_count, local_width)
    query_grad = query_grad.reshape(flat_shape)
    key_grad = key_grad.reshape(flat_shape)
    value_grad = value_grad.reshape(flat_shape)
    heads_bias_part = jnp.stack(
        [jnp.sum(query_grad, axis=(0, 1)), jnp.sum(value_grad, axis=(0, 1))]
    )
    project_low = (
        jnp.stack([query_grad, key_grad, value_grad], axis=2)
        .astype(jnp.bfloat16)
        .reshape(crop_count, row_count, 3 * local_width)
    )
    heads_grad = rows_product(hidden_full, project_low).reshape(model_width, 3, local_width)
    input_part = apply_transposed(project_low, heads_matrix.reshape(model_width, 3 * local_width))
    grads = (
        heads_grad,
        heads_bias_part,
        merge_grad,
        merge_bias_part,
        expand_grad,
        expand_bias_part,
        shrink_grad,
        shrink_bias_part,
        jnp.stack([gain_one, gain_two]),
        jnp.stack([shift_one, shift_two]),
    )
    return (input_part, total_one, grads)


def queue_part(query_low, piece):
    logits = (
        lax.dot_general(
            query_low, piece, (((1,), (1,)), ((), ())), preferred_element_type=jnp.float32
        )
        / SOFTMAX_WARMTH
    )
    row_top = jnp.max(logits, axis=-1)
    exponent = jnp.exp(logits - row_top[:, None])
    weighted_keys = jnp.dot(exponent, piece.astype(jnp.float32), precision=TOP_PRECISION)
    return (row_top, jnp.sum(exponent, axis=-1), weighted_keys)


def combine_parts(first_part, later_part):
    top_first, total_first, weighted_first = first_part
    top_later, total_later, weighted_later = later_part
    row_top = jnp.maximum(top_first, top_later)
    factor_first = jnp.exp(top_first - row_top)
    factor_later = jnp.exp(top_later - row_top)
    return (
        row_top,
        total_first * factor_first + total_later * factor_later,
        weighted_first * factor_first[:, None] + weighted_later * factor_later[:, None],
    )


def per_device(
    query_tokens,
    query_drop,
    query_length,
    key_tokens,
    key_drop,
    key_length,
    negatives,
    attend_weight,
    attend_bias,
    merge_weight,
    merge_bias,
    expand_weight,
    expand_bias,
    shrink_weight,
    shrink_bias,
    norm_gain,
    norm_shift,
):
    stacked = (
        attend_weight,
        attend_bias,
        merge_weight,
        merge_bias,
        expand_weight,
        expand_bias,
        shrink_weight,
        shrink_bias,
        norm_gain,
        norm_shift,
    )
    micro_count = query_tokens.shape[0]
    crop_count = query_tokens.shape[1]
    crop_rows = query_tokens.shape[2]
    model_width = query_tokens.shape[3]
    share_rows = crop_rows // lax.axis_size("tensor")
    share_start = lax.axis_index("tensor") * share_rows
    layer_count = attend_weight.shape[1]

    def layer_params(encoder_at, layer_at):
        return tuple((item[encoder_at, layer_at] for item in stacked))

    def prepare(tokens, dropped_flags, crop_lengths):
        retained_flag, slot_lookup, source_index, token_counts = packing_plan(
            dropped_flags, crop_lengths
        )
        position = lax.broadcasted_iota(jnp.int32, dropped_flags.shape, 1)
        valid_keys = position < token_counts[:, None]
        picked = jnp.take_along_axis(tokens, source_index[..., None], axis=1)
        compact = jnp.where(valid_keys[..., None], picked, jnp.zeros_like(picked))
        return (retained_flag, slot_lookup, token_counts, valid_keys, compact)

    def encode(compact, valid_keys, encoder_at):
        hidden_share = lax.dynamic_slice_in_dim(compact, share_start, share_rows, 1).astype(
            jnp.float32
        )
        hidden_full = compact
        inputs = []
        for layer_at in range(layer_count):
            if layer_at > 0:
                hidden_full = rows_gather(hidden_share.astype(jnp.bfloat16))
            inputs.append(hidden_share)
            hidden_share, unused_state = layer_pass(
                hidden_share, hidden_full, layer_params(encoder_at, layer_at), valid_keys
            )
        share_valid = lax.dynamic_slice_in_dim(valid_keys, share_start, share_rows, 1)
        pooled_part = jnp.sum(jnp.where(share_valid[..., None], hidden_share, 0.0), axis=1)
        return (hidden_share, pooled_part, inputs)

    prepared = []
    stored = []
    final_rows = []
    query_parts = []
    key_parts = []
    key_counts = []
    for micro_at in range(micro_count):
        key_prep = prepare(key_tokens[micro_at], key_drop[micro_at], key_length[micro_at])
        unused_rows, key_part, unused_inputs = encode(key_prep[4], key_prep[3], 1)
        query_prep = prepare(query_tokens[micro_at], query_drop[micro_at], query_length[micro_at])
        last_rows, query_part, inputs = encode(query_prep[4], query_prep[3], 0)
        prepared.append(query_prep)
        stored.append(inputs)
        final_rows.append(last_rows)
        query_parts.append(query_part)
        key_parts.append(key_part)
        key_counts.append(key_prep[2])
    pooled_query, pooled_key = lax.psum((jnp.stack(query_parts), jnp.stack(key_parts)), "tensor")
    query_counts = jnp.stack([item[2] for item in prepared]).astype(jnp.float32)
    key_mean = pooled_key / jnp.stack(key_counts).astype(jnp.float32)[..., None]
    key_direction = key_mean * lax.rsqrt(
        jnp.sum(key_mean * key_mean, axis=-1, keepdims=True) + UNIT_EPS
    )
    query_mean = pooled_query / query_counts[..., None]
    query_scale = lax.rsqrt(jnp.sum(query_mean * query_mean, axis=-1, keepdims=True) + UNIT_EPS)
    query_direction = query_mean * query_scale
    unit_flattened = query_direction.reshape(-1, model_width)
    key_flattened = key_direction.reshape(-1, model_width)
    query_low = unit_flattened.astype(jnp.bfloat16)
    positive_score = jnp.sum(unit_flattened * key_flattened, axis=-1) / SOFTMAX_WARMTH
    start_state = (positive_score, jnp.ones_like(positive_score), key_flattened)
    row_top, exponent_sum, weighted_keys = combine_parts(
        start_state,
        queue_part(query_low, lax.all_gather(negatives, ("rep", "tensor"), axis=0, tiled=True)),
    )
    per_query = row_top + jnp.log(exponent_sum) - positive_score
    direction_gradient = (
        (weighted_keys / exponent_sum[:, None] - key_flattened) * (CROP_SLOTS / SOFTMAX_WARMTH)
    ).reshape(query_direction.shape)
    mean_grad = query_scale * (
        direction_gradient
        - query_direction * jnp.sum(query_direction * direction_gradient, axis=-1, keepdims=True)
    )
    pooled_grad = mean_grad / query_counts[..., None]
    running = []
    for layer_at in range(layer_count):
        running.append(tuple((jnp.zeros(item.shape[2:], jnp.float32) for item in stacked)))
    token_grads = []
    for micro_at in range(micro_count):
        retained_flag, slot_lookup, token_counts, valid_keys, compact = prepared[micro_at]
        inputs = stored[micro_at]
        share_valid = lax.dynamic_slice_in_dim(valid_keys, share_start, share_rows, 1)
        grad_now = jnp.where(share_valid[..., None], pooled_grad[micro_at][:, None, :], 0.0)
        for layer_at in reversed(range(layer_count)):
            hidden_share = inputs[layer_at]
            if layer_at == 0:
                hidden_full = compact
            else:
                hidden_full = rows_gather(hidden_share.astype(jnp.bfloat16))
            params = layer_params(0, layer_at)
            unused_out, kept_state = layer_pass(hidden_share, hidden_full, params, valid_keys)
            input_part, residual_grad, grads = layer_back(grad_now, kept_state, hidden_full, params)
            running[layer_at] = tuple((old + new for old, new in zip(running[layer_at], grads)))
            if layer_at > 0:
                grad_now = grad_total(input_part) + residual_grad
            else:
                placed = lax.dynamic_update_slice_in_dim(
                    jnp.zeros_like(input_part), residual_grad, share_start, 1
                )
                combined = input_part + placed
                moved = jnp.take_along_axis(
                    combined, jnp.maximum(slot_lookup, 0)[..., None], axis=1
                )
                moved = jnp.where(retained_flag[..., None] == 1, moved, 0.0)
                token_grads.append(grad_total(moved).astype(jnp.bfloat16))
    layer_grads = [
        jnp.stack([running[layer_at][which] for layer_at in range(layer_count)])
        for which in range(len(stacked))
    ]
    summed = (
        lax.psum_scatter(layer_grads[0], ("dp", "rep"), scatter_dimension=1, tiled=True),
        lax.psum_scatter(layer_grads[2], ("dp", "rep"), scatter_dimension=2, tiled=True),
        lax.psum_scatter(layer_grads[4], ("dp", "rep"), scatter_dimension=1, tiled=True),
        lax.psum_scatter(layer_grads[6], ("dp", "rep"), scatter_dimension=2, tiled=True),
    )
    attend_bias_total, expand_bias_total, loss_total = lax.psum(
        (layer_grads[1], layer_grads[5], jnp.sum(per_query)), ("dp", "rep")
    )
    group_shared = lax.psum(
        (layer_grads[3], layer_grads[7], layer_grads[8], layer_grads[9]), "tensor"
    )
    merge_bias_total, shrink_bias_total, gain_total, shift_total = (
        lax.psum_scatter(group_shared[0], ("dp", "rep"), scatter_dimension=1, tiled=True),
        lax.psum_scatter(group_shared[1], ("dp", "rep"), scatter_dimension=1, tiled=True),
        lax.psum_scatter(group_shared[2], ("dp", "rep"), scatter_dimension=2, tiled=True),
        lax.psum_scatter(group_shared[3], ("dp", "rep"), scatter_dimension=2, tiled=True),
    )
    loss = loss_total / (micro_count * crop_count * lax.axis_size("dp") * lax.axis_size("rep"))
    activations = jnp.stack(final_rows).astype(jnp.bfloat16)
    input_grad = jnp.stack(token_grads)
    return (
        activations,
        input_grad,
        summed[0],
        attend_bias_total,
        summed[1],
        merge_bias_total,
        summed[2],
        expand_bias_total,
        summed[3],
        shrink_bias_total,
        gain_total,
        shift_total,
        loss,
    )


def solution(mesh):
    return jax.shard_map(
        per_device,
        mesh=mesh,
        in_specs=(
            P(None, ("dp", "rep"), None, None),
            P(None, ("dp", "rep"), None),
            P(None, ("dp", "rep")),
            P(None, ("dp", "rep"), None, None),
            P(None, ("dp", "rep"), None),
            P(None, ("dp", "rep")),
            P(("rep", "tensor"), None),
            P(None, None, None, None, "tensor"),
            P(None, None, None, "tensor"),
            P(None, None, "tensor", None),
            P(),
            P(None, None, None, "tensor"),
            P(None, None, "tensor"),
            P(None, None, "tensor", None),
            P(),
            P(),
            P(),
        ),
        out_specs=(
            P(None, ("dp", "rep"), "tensor", None),
            P(None, ("dp", "rep"), "tensor", None),
            P(None, ("dp", "rep"), None, "tensor"),
            P(None, None, "tensor"),
            P(None, "tensor", ("dp", "rep")),
            P(None, ("dp", "rep")),
            P(None, ("dp", "rep"), "tensor"),
            P(None, "tensor"),
            P(None, "tensor", ("dp", "rep")),
            P(None, ("dp", "rep")),
            P(None, None, ("dp", "rep")),
            P(None, None, ("dp", "rep")),
            P(),
        ),
        check_vma=False,
    )
```

profile of v0, /device:TPU:0, one launch (start us, length us, event | category | flops | bytes accessed | tf_op | source)
XLA Modules:
  0.0 1306.2 jit_solution(2965534976636865572)
XLA Ops:
  18.5 4.1 fusion.583
  74.0 12.2 reduce-scatter.52.cloned.1.call-done
  88.3 17.7 %all_gather.69 = bf16[1,256,768]{2,1,0:T(8,128)(2,1)S(1)} all-gather(bf16[1,64,768]{2,1,0:T(8,128)(2,1)S(1)} %get-tuple-element.282), channel_id=1, replica_groups=mesh['dp'=4,'rep'=2,'tensor'=4] {'tensor'}, dimensions={1}, use_global_device_ids=true | all-gather | bytes 491520 | tf_op jit(solution)/shard_map/all_gather | solution.py:38
  106.0 4.2 fusion.125
  111.0 2.7 convolution_bitcast_fusion.13
  113.8 25.0 %reduce-scatter.68.cloned.1.call-done = f32[1,64,768]{2,1,0:T(8,128)} async-done(((f32[1,256,768]{2,1,0:T(8,128)}), f32[1,64,768]{2,1,0:T(8,128)}) %reduce-scatter.68.cloned.1.call-update) | async-done | bytes 196624 | tf_op jit(solution)/shard_map/reduce_scatter | solution.py:34
  140.1 17.5 %all_gather.72 = bf16[1,256,768]{2,1,0:T(8,128)(2,1)S(1)} all-gather(bf16[1,64,768]{2,1,0:T(8,128)(2,1)S(1)} %get-tuple-element.283), channel_id=1, replica_groups=mesh['dp'=4,'rep'=2,'tensor'=4] {'tensor'}, dimensions={1}, use_global_device_ids=true | all-gather | bytes 491520 | tf_op jit(solution)/shard_map/all_gather | solution.py:38
  157.5 4.3 fusion.131
  165.8 16.2 %all_gather.78 = bf16[1,256,768]{2,1,0:T(8,128)(2,1)S(1)} all-gather(bf16[1,64,768]{2,1,0:T(8,128)(2,1)S(1)} %get-tuple-element.266), channel_id=1, replica_groups=mesh['dp'=4,'rep'=2,'tensor'=4] {'tensor'}, dimensions={1}, use_global_device_ids=true | all-gather | bytes 491520 | tf_op jit(solution)/shard_map/all_gather | solution.py:38
  182.0 5.1 convolution_bitcast_fusion.7
  190.4 16.6 %all_gather.75 = bf16[1,256,768]{2,1,0:T(8,128)(2,1)} all-gather(bf16[1,64,768]{2,1,0:T(8,128)(2,1)S(1)} %get-tuple-element.267), channel_id=1, replica_groups=mesh['dp'=4,'rep'=2,'tensor'=4] {'tensor'}, dimensions={1}, use_global_device_ids=true | all-gather | bytes 491520 | tf_op jit(solution)/shard_map/all_gather | solution.py:38
  207.1 5.3 convolution_bitcast_fusion.9
  215.4 15.0 %all_gather.70 = bf16[1,256,768]{2,1,0:T(8,128)(2,1)S(1)} all-gather(bf16[1,64,768]{2,1,0:T(8,128)(2,1)S(1)} %get-tuple-element.280), channel_id=1, replica_groups=mesh['dp'=4,'rep'=2,'tensor'=4] {'tensor'}, dimensions={1}, use_global_device_ids=true | all-gather | bytes 491520 | tf_op jit(solution)/shard_map/all_gather | solution.py:38
  231.1 17.4 %all_gather.73 = bf16[1,256,768]{2,1,0:T(8,128)(2,1)S(1)} all-gather(bf16[1,64,768]{2,1,0:T(8,128)(2,1)S(1)} %get-tuple-element.281), channel_id=1, replica_groups=mesh['dp'=4,'rep'=2,'tensor'=4] {'tensor'}, dimensions={1}, use_global_device_ids=true | all-gather | bytes 491520 | tf_op jit(solution)/shard_map/all_gather | solution.py:38
  252.0 2.8 fusion.779
  264.2 2.9 fusion.780
  275.8 16.4 %all_gather.79 = bf16[1,256,768]{2,1,0:T(8,128)(2,1)S(1)} all-gather(bf16[1,64,768]{2,1,0:T(8,128)(2,1)S(1)} %get-tuple-element.276), channel_id=1, replica_groups=mesh['dp'=4,'rep'=2,'tensor'=4] {'tensor'}, dimensions={1}, use_global_device_ids=true | all-gather | bytes 491520 | tf_op jit(solution)/shard_map/all_gather | solution.py:38
  303.1 16.4 %all_gather.76 = bf16[1,256,768]{2,1,0:T(8,128)(2,1)S(1)} all-gather(bf16[1,64,768]{2,1,0:T(8,128)(2,1)} %get-tuple-element.277), channel_id=1, replica_groups=mesh['dp'=4,'rep'=2,'tensor'=4] {'tensor'}, dimensions={1}, use_global_device_ids=true | all-gather | bytes 491520 | tf_op jit(solution)/shard_map/all_gather | solution.py:38
  332.7 16.3 %all_gather.71 = bf16[1,256,768]{2,1,0:T(8,128)(2,1)S(1)} all-gather(bf16[1,64,768]{2,1,0:T(8,128)(2,1)S(1)} %get-tuple-element.278), channel_id=1, replica_groups=mesh['dp'=4,'rep'=2,'tensor'=4] {'tensor'}, dimensions={1}, use_global_device_ids=true | all-gather | bytes 491520 | tf_op jit(solution)/shard_map/all_gather | solution.py:38
  349.0 17.3 %all_gather.74 = bf16[1,256,768]{2,1,0:T(8,128)(2,1)} all-gather(bf16[1,64,768]{2,1,0:T(8,128)(2,1)S(1)} %get-tuple-element.279), channel_id=1, replica_groups=mesh['dp'=4,'rep'=2,'tensor'=4] {'tensor'}, dimensions={1}, use_global_device_ids=true | all-gather | bytes 491520 | tf_op jit(solution)/shard_map/all_gather | solution.py:38
  366.4 4.2 fusion.128
  371.3 2.6 convolution_bitcast_fusion.12
  374.2 4.3 fusion.134
  389.5 17.1 %all_gather.80 = bf16[1,256,768]{2,1,0:T(8,128)(2,1)} all-gather(bf16[1,64,768]{2,1,0:T(8,128)(2,1)S(1)} %get-tuple-element.274), channel_id=1, replica_groups=mesh['dp'=4,'rep'=2,'tensor'=4] {'tensor'}, dimensions={1}, use_global_device_ids=true | all-gather | bytes 491520 | tf_op jit(solution)/shard_map/all_gather | solution.py:38
  406.6 5.1 convolution_bitcast_fusion.6
  411.8 17.3 %all_gather.77 = bf16[1,256,768]{2,1,0:T(8,128)(2,1)} all-gather(bf16[1,64,768]{2,1,0:T(8,128)(2,1)} %get-tuple-element.275), channel_id=1, replica_groups=mesh['dp'=4,'rep'=2,'tensor'=4] {'tensor'}, dimensions={1}, use_global_device_ids=true | all-gather | bytes 491520 | tf_op jit(solution)/shard_map/all_gather | solution.py:38
  429.1 5.1 convolution_bitcast_fusion.8
  450.8 63.9 %reduce-scatter.66.cloned.1.call-done = f32[1,64,768]{2,1,0:T(8,128)} async-done(((f32[1,256,768]{2,1,0:T(8,128)}), f32[1,64,768]{2,1,0:T(8,128)}) %reduce-scatter.66.cloned.1.call-update) | async-done | bytes 196624 | tf_op jit(solution)/shard_map/reduce_scatter | solution.py:34
  519.2 19.1 %all-reduce.3 = (f32[2,1,768]{2,0,1:T(2,128)}, f32[2,1,768]{2,0,1:T(2,128)}) all-reduce(f32[2,1,768]{2,0,1:T(2,128)S(1)} %pad_maximum_fusion.8, f32[2,1,768]{2,0,1:T(2,128)} %pad_maximum_fusion.9), channel_id=1, replica_groups=mesh['dp'=4,'rep'=2,'tensor'=4] {'tensor'}, use_global_device_ids=true, to_apply=%region_42.44 | all-reduce | flops 3072 | bytes 24576 | tf_op jit(solution)/shard_map/psum | solution.py:369
  541.3 80.2 %all-gather.2.cloned.1.call-done = bf16[8192,768]{1,0:T(8,128)(2,1)} async-done(((bf16[1024,768]{1,0:T(8,128)(2,1)}), bf16[8192,768]{1,0:T(8,128)(2,1)}) %all-gather.2.cloned.1.call-update) | async-done | bytes 12582928 | tf_op jit(solution)/shard_map/all_gather | solution.py:385
  621.6 8.2 fusion.785
  630.9 5.1 multiply_reduce_fusion.38
  637.9 15.0 %all_gather.82 = bf16[1,256,768]{2,1,0:T(8,128)(2,1)S(1)} all-gather(bf16[1,64,768]{2,1,0:T(8,128)(2,1)S(1)} %convert_element_type.1189), channel_id=1, replica_groups=mesh['dp'=4,'rep'=2,'tensor'=4] {'tensor'}, dimensions={1}, use_global_device_ids=true | all-gather | bytes 491520 | tf_op jit(solution)/shard_map/all_gather | solution.py:42
  656.3 2.7 convolution_bitcast_fusion.5
  662.6 17.9 %all_gather.86 = bf16[1,256,768]{2,1,0:T(8,128)(2,1)S(1)} all-gather(bf16[1,64,768]{2,1,0:T(8,128)(2,1)S(1)} %convert_element_type.1205), channel_id=1, replica_groups=mesh['dp'=4,'rep'=2,'tensor'=4] {'tensor'}, dimensions={1}, use_global_device_ids=true | all-gather | bytes 491520 | tf_op jit(solution)/shard_map/all_gather | solution.py:42
  681.3 2.7 fusion.795
  684.7 2.7 convolution_bitcast_fusion.2
  690.8 18.7 %reduce-scatter.84.cloned.1.call-done = f32[1,64,768]{2,1,0:T(8,128)} async-done(((f32[1,256,768]{2,1,0:T(8,128)}), f32[1,64,768]{2,1,0:T(8,128)}) %reduce-scatter.84.cloned.1.call-update) | async-done | bytes 196624 | tf_op jit(solution)/shard_map/reduce_scatter | solution.py:46
  711.7 15.2 %all_gather.83 = bf16[1,256,768]{2,1,0:T(8,128)(2,1)S(1)} all-gather(bf16[1,64,768]{2,1,0:T(8,128)(2,1)S(1)} %convert_element_type.1191), channel_id=1, replica_groups=mesh['dp'=4,'rep'=2,'tensor'=4] {'tensor'}, dimensions={1}, use_global_device_ids=true | all-gather | bytes 491520 | tf_op jit(solution)/shard_map/all_gather | solution.py:42
  732.1 3.0 bitcast_reduce_fusion.3
  738.4 17.0 %all_gather.87 = bf16[1,256,768]{2,1,0:T(8,128)(2,1)S(1)} all-gather(bf16[1,64,768]{2,1,0:T(8,128)(2,1)S(1)} %convert_element_type.1207), channel_id=1, replica_groups=mesh['dp'=4,'rep'=2,'tensor'=4] {'tensor'}, dimensions={1}, use_global_device_ids=true | all-gather | bytes 491520 | tf_op jit(solution)/shard_map/all_gather | solution.py:42
  766.4 20.9 %reduce-scatter.86.cloned.1.call-done = f32[1,64,768]{2,1,0:T(8,128)} async-done(((f32[1,256,768]{2,1,0:T(8,128)}), f32[1,64,768]{2,1,0:T(8,128)}) %reduce-scatter.86.cloned.1.call-update) | async-done | bytes 196624 | tf_op jit(solution)/shard_map/reduce_scatter | solution.py:46
  789.1 14.9 %all_gather.84 = bf16[1,256,768]{2,1,0:T(8,128)(2,1)S(1)} all-gather(bf16[1,64,768]{2,1,0:T(8,128)(2,1)S(1)} %convert_element_type.1196), channel_id=1, replica_groups=mesh['dp'=4,'rep'=2,'tensor'=4] {'tensor'}, dimensions={1}, use_global_device_ids=true | all-gather | bytes 491520 | tf_op jit(solution)/shard_map/all_gather | solution.py:42
  804.0 2.7 fusion.796
  806.7 2.8 convolution_bitcast_fusion.3
  812.3 17.3 %all_gather.88 = bf16[1,256,768]{2,1,0:T(8,128)(2,1)S(1)} all-gather(bf16[1,64,768]{2,1,0:T(8,128)(2,1)S(1)} %convert_element_type.1212), channel_id=1, replica_groups=mesh['dp'=4,'rep'=2,'tensor'=4] {'tensor'}, dimensions={1}, use_global_device_ids=true | all-gather | bytes 491520 | tf_op jit(solution)/shard_map/all_gather | solution.py:42
  829.6 2.8 fusion.797
  832.5 2.8 convolution_bitcast_fusion
  851.8 9.1 reduce-scatter.88.cloned.1.call-done
  873.8 4.1 pad_maximum_fusion.1
  877.9 8.2 copy.117
  886.2 15.2 %all_gather.89 = bf16[1,256,768]{2,1,0:T(8,128)(2,1)S(1)} all-gather(bf16[1,64,768]{2,1,0:T(8,128)(2,1)S(1)} %convert_element_type.1214), channel_id=1, replica_groups=mesh['dp'=4,'rep'=2,'tensor'=4] {'tensor'}, dimensions={1}, use_global_device_ids=true | all-gather | bytes 491520 | tf_op jit(solution)/shard_map/all_gather | solution.py:42
  913.0 14.5 %all_gather.85 = bf16[1,256,768]{2,1,0:T(8,128)(2,1)S(1)} all-gather(bf16[1,64,768]{2,1,0:T(8,128)(2,1)S(1)} %copy-done.95), channel_id=1, replica_groups=mesh['dp'=4,'rep'=2,'tensor'=4] {'tensor'}, dimensions={1}, use_global_device_ids=true | all-gather | bytes 491520 | tf_op jit(solution)/shard_map/all_gather | solution.py:42
  946.3 4.8 copy.140
  951.1 8.0 reshape.5096
  970.2 24.0 %all-reduce.1 = (f32[2,2,192]{2,1,0:T(2,128)}, f32[2,768]{1,0:T(2,128)}, f32[]{:T(128)}) all-reduce(f32[2,2,192]{2,1,0:T(2,128)S(1)} %pad_maximum_fusion.13, f32[2,768]{1,0:T(2,128)S(1)} %pad_maximum_fusion.11, f32[]{:T(128)} %get-tuple-element.182), channel_id=1, replica_groups=mesh['dp'=4,'rep'=2,'tensor'=4] {'dp','rep'}, use_global_device_ids=true, to_apply=%region_129.132 | all-reduce | flops 2305 | bytes 18440 | tf_op jit(solution)/shard_map/psum | solution.py:437
  996.7 10.9 reduce-scatter.104.cloned.1.call-done
  1008.6 12.4 all-reduce.2
  1021.0 76.6 %all-reduce.6.cloned.1.call-done = f32[2,768,768]{1,0,2:T(2,128)} async-done(((f32[2,768,768]{1,0,2:T(2,128)}), f32[2,768,768]{1,0,2:T(2,128)}) %all-reduce.6.cloned.1.call-update) | async-done | bytes 4718608
  1099.6 23.8 %reduce-scatter.90.cloned.1.call-done = f32[1,64,768]{2,1,0:T(8,128)} async-done(((f32[1,256,768]{2,1,0:T(8,128)}), f32[1,64,768]{2,1,0:T(8,128)}) %reduce-scatter.90.cloned.1.call-update) | async-done | bytes 196624 | tf_op jit(solution)/shard_map/reduce_scatter | solution.py:46
  1124.4 24.1 %reduce-scatter.82.cloned.1.call-done = f32[1,64,768]{2,1,0:T(8,128)} async-done(((f32[1,256,768]{2,1,0:T(8,128)}), f32[1,64,768]{2,1,0:T(8,128)}) %reduce-scatter.82.cloned.1.call-update) | async-done | bytes 196624 | tf_op jit(solution)/shard_map/reduce_scatter | solution.py:46
  1150.1 37.9 %reduce-scatter.96.cloned.1.call-done = f32[96,384]{1,0:T(8,128)} async-done(((f32[768,384]{1,0:T(8,128)}), f32[96,384]{1,0:T(8,128)}) %reduce-scatter.96.cloned.1.call-update) | async-done | bytes 147472
  1189.8 49.7 %reduce-scatter.94.cloned.1.call-done = f32[96,1152]{1,0:T(8,128)} async-done(((f32[768,1152]{1,0:T(8,128)}), f32[96,1152]{1,0:T(8,128)}) %reduce-scatter.94.cloned.1.call-update) | async-done | bytes 442384
  1242.1 55.4 %reduce-scatter.92.cloned.1.call-done = f32[2,96,768]{2,1,0:T(8,128)} async-done(((f32[2,768,768]{2,1,0:T(8,128)}), f32[2,96,768]{2,1,0:T(8,128)}) %reduce-scatter.92.cloned.1.call-update) | async-done | bytes 589840 | tf_op jit(solution)/shard_map/reduce_scatter | solution.py:434
  (992 shorter events, 278.5 us)
Async XLA Ops:
  8.0 66.0 %reduce-scatter.44.cloned.1.call-start = ((), (), s32[]{:S(2)}) async-start(), calls=%async_computation.31 | async-start | bytes 983040 | tf_op jit(solution)/shard_map/reduce_scatter | solution.py:34
  24.7 61.6 %copy-start.22 = (bf16[1,256,768]{2,1,0:T(8,128)(2,1)}, bf16[1,256,768]{2,1,0:T(8,128)(2,1)S(1)}, u32[]{:S(2)}) copy-start(bf16[1,256,768]{2,1,0:T(8,128)(2,1)S(1)} %fusion.312) | copy-start | bytes 1179652
  29.3 57.0 %copy-start.24 = (bf16[1,256,768]{2,1,0:T(8,128)(2,1)}, bf16[1,256,768]{2,1,0:T(8,128)(2,1)S(1)}, u32[]{:S(2)}) copy-start(bf16[1,256,768]{2,1,0:T(8,128)(2,1)S(1)} %fusion.299) | copy-start | bytes 1179652
  35.1 51.2 %reduce-scatter.52.cloned.1.call-start = ((), (), s32[]{:S(2)}) async-start(), calls=%async_computation.35 | async-start | bytes 983040 | tf_op jit(solution)/shard_map/reduce_scatter | solution.py:34
  39.4 74.4 %reduce-scatter.60.cloned.1.call-start = ((), (), s32[]{:S(2)}) async-start(), calls=%async_computation.39 | async-start | bytes 983040 | tf_op jit(solution)/shard_map/reduce_scatter | solution.py:34
  48.2 117.4 %copy-start.30 = (bf16[1,256,768]{2,1,0:T(8,128)(2,1)}, bf16[1,256,768]{2,1,0:T(8,128)(2,1)S(1)}, u32[]{:S(2)}) copy-start(bf16[1,256,768]{2,1,0:T(8,128)(2,1)S(1)} %fusion.290) | copy-start | bytes 1179652
  58.9 80.0 %reduce-scatter.68.cloned.1.call-start = ((), (), s32[]{:S(2)}) async-start(), calls=%async_computation.43 | async-start | bytes 983040 | tf_op jit(solution)/shard_map/reduce_scatter | solution.py:34
  60.9 104.7 %copy-start.31 = (bf16[1,256,768]{2,1,0:T(8,128)(2,1)}, bf16[1,256,768]{2,1,0:T(8,128)(2,1)S(1)}, u32[]{:S(2)}) copy-start(bf16[1,256,768]{2,1,0:T(8,128)(2,1)S(1)} %fusion.283) | copy-start | bytes 1179652
  70.6 141.9 %reduce-scatter.46.cloned.1.call-start = ((), (), s32[]{:S(2)}) async-start(), calls=%async_computation.32 | async-start | bytes 983040 | tf_op jit(solution)/shard_map/reduce_scatter | solution.py:34
  71.7 110.3 %copy-start.216 = (f32[768]{0:T(1024)}, f32[768]{0:T(1024)S(1)}, u32[]{:S(2)}) copy-start(f32[768]{0:T(1024)S(1)} %get-tuple-element.126) | copy-start | bytes 9220
  74.0 36.3 %copy-start.138 = (f32[768]{0:T(1024)}, f32[768]{0:T(1024)S(1)}, u32[]{:S(2)}) copy-start(f32[768]{0:T(1024)S(1)} %get-tuple-element.109) | copy-start | bytes 9220
  74.0 91.6 %copy-start.136 = (f32[768]{0:T(1024)}, f32[768]{0:T(1024)S(1)}, u32[]{:S(2)}) copy-start(f32[768]{0:T(1024)S(1)} %get-tuple-element.105) | copy-start | bytes 9220
  74.0 91.6 %copy-start.137 = (f32[768]{0:T(1024)}, f32[768]{0:T(1024)S(1)}, u32[]{:S(2)}) copy-start(f32[768]{0:T(1024)S(1)} %get-tuple-element.370) | copy-start | bytes 9220
  74.0 369.4 %copy-start.109 = (f32[768]{0:T(1024)}, f32[768]{0:T(1024)S(1)}, u32[]{:S(2)}) copy-start(f32[768]{0:T(1024)S(1)} %get-tuple-element.368) | copy-start | bytes 9220
  87.5 22.8 %copy-start.165 = (f32[64]{0:T(128)}, f32[64]{0:T(128)S(1)}, u32[]{:S(2)}) copy-start(f32[64]{0:T(128)S(1)} %broadcast_multiply_fusion.33) | copy-start | bytes 772
  113.7 98.8 %reduce-scatter.54.cloned.1.call-start = ((), (), s32[]{:S(2)}) async-start(), calls=%async_computation.36 | async-start | bytes 983040 | tf_op jit(solution)/shard_map/reduce_scatter | solution.py:34
  165.3 94.1 %reduce-scatter.70.cloned.1.call-start = ((), (), s32[]{:S(2)}) async-start(), calls=%async_computation.44 | async-start | bytes 983040 | tf_op jit(solution)/shard_map/reduce_scatter | solution.py:34
  187.1 72.3 %reduce-scatter.62.cloned.1.call-start = ((), (), s32[]{:S(2)}) async-start(), calls=%async_computation.40 | async-start | bytes 983040 | tf_op jit(solution)/shard_map/reduce_scatter | solution.py:34
  207.1 23.3 %copy-start.1 = (bf16[2,2,768,3,192]{2,4,3,1,0:T(8,128)(2,1)S(1)}, bf16[2,2,768,3,192]{2,4,3,1,0:T(8,128)(2,1)}, u32[]{:S(2)}) copy-start(bf16[2,2,768,3,192]{2,4,3,1,0:T(8,128)(2,1)} %param.28) | copy-start | bytes 10616836
  212.4 118.0 %reduce-scatter.48.cloned.1.call-start = ((), (), s32[]{:S(2)}) async-start(), calls=%async_computation.33 | async-start | bytes 983040 | tf_op jit(solution)/shard_map/reduce_scatter | solution.py:34
  214.0 35.6 %copy-start.8 = (f32[1,64,768]{2,1,0:T(8,128)}, f32[1,64,768]{2,1,0:T(8,128)S(1)}, u32[]{:S(2)}) copy-start(f32[1,64,768]{2,1,0:T(8,128)S(1)} %get-tuple-element.273) | copy-start | bytes 589828
  214.1 35.6 %copy-start.10 = (f32[1,64,768]{2,1,0:T(8,128)}, f32[1,64,768]{2,1,0:T(8,128)S(1)}, u32[]{:S(2)}) copy-start(f32[1,64,768]{2,1,0:T(8,128)S(1)} %get-tuple-element.221) | copy-start | bytes 589828
  259.3 71.1 %reduce-scatter.56.cloned.1.call-start = ((), (), s32[]{:S(2)}) async-start(), calls=%async_computation.37 | async-start | bytes 983040 | tf_op jit(solution)/shard_map/reduce_scatter | solution.py:34
  274.0 107.9 %reduce-scatter.72.cloned.1.call-start = ((), (), s32[]{:S(2)}) async-start(), calls=%async_computation.45 | async-start | bytes 983040 | tf_op jit(solution)/shard_map/reduce_scatter | solution.py:34
  303.1 78.8 %reduce-scatter.64.cloned.1.call-start = ((), (), s32[]{:S(2)}) async-start(), calls=%async_computation.41 | async-start | bytes 983040 | tf_op jit(solution)/shard_map/reduce_scatter | solution.py:34
  330.4 113.0 %reduce-scatter.50.cloned.1.call-start = ((), (), s32[]{:S(2)}) async-start(), calls=%async_computation.34 | async-start | bytes 983040 | tf_op jit(solution)/shard_map/reduce_scatter | solution.py:34
  330.5 35.9 %copy-start.214 = (f32[768]{0:T(1024)S(1)}, f32[768]{0:T(1024)}, u32[]{:S(2)}) copy-start(f32[768]{0:T(1024)} %get-tuple-element.124) | copy-start | bytes 9220
  332.0 38.5 %copy-start.12 = (f32[1,64,768]{2,1,0:T(8,128)}, f32[1,64,768]{2,1,0:T(8,128)S(1)}, u32[]{:S(2)}) copy-start(f32[1,64,768]{2,1,0:T(8,128)S(1)} %get-tuple-element.271) | copy-start | bytes 589828
  332.0 38.5 %copy-start.14 = (f32[1,64,768]{2,1,0:T(8,128)}, f32[1,64,768]{2,1,0:T(8,128)S(1)}, u32[]{:S(2)}) copy-start(f32[1,64,768]{2,1,0:T(8,128)S(1)} %get-tuple-element.219) | copy-start | bytes 589828
  332.1 34.3 %copy-start.174 = (f32[64]{0:T(128)}, f32[64]{0:T(128)S(1)}, u32[]{:S(2)}) copy-start(f32[64]{0:T(128)S(1)} %broadcast_multiply_fusion.31) | copy-start | bytes 772
  332.3 34.1 %copy-start.190 = (f32[64]{0:T(128)}, f32[64]{0:T(128)S(1)}, u32[]{:S(2)}) copy-start(f32[64]{0:T(128)S(1)} %add_rsqrt_fusion.15) | copy-start | bytes 772
  332.3 34.0 %copy-start.171 = (f32[64]{0:T(128)}, f32[64]{0:T(128)S(1)}, u32[]{:S(2)}) copy-start(f32[64]{0:T(128)S(1)} %broadcast_multiply_fusion.27) | copy-start | bytes 772
  332.5 33.8 %copy-start.188 = (f32[64]{0:T(128)}, f32[64]{0:T(128)S(1)}, u32[]{:S(2)}) copy-start(f32[64]{0:T(128)S(1)} %add_rsqrt_fusion.11) | copy-start | bytes 772
  373.9 69.5 %reduce-scatter.58.cloned.1.call-start = ((), (), s32[]{:S(2)}) async-start(), calls=%async_computation.38 | async-start | bytes 983040 | tf_op jit(solution)/shard_map/reduce_scatter | solution.py:34
  385.3 65.5 %reduce-scatter.74.cloned.1.call-start = ((), (), s32[]{:S(2)}) async-start(), calls=%async_computation.46 | async-start | bytes 983040 | tf_op jit(solution)/shard_map/reduce_scatter | solution.py:34
  411.7 103.0 %reduce-scatter.66.cloned.1.call-start = ((), (), s32[]{:S(2)}) async-start(), calls=%async_computation.42 | async-start | bytes 983040 | tf_op jit(solution)/shard_map/reduce_scatter | solution.py:34
  434.3 187.3 %all-gather.2.cloned.1.call-start = ((), (), s32[]{:S(2)}) async-start(), calls=%async_computation.47 | async-start | bytes 14155776 | tf_op jit(solution)/shard_map/all_gather | solution.py:385
  434.8 254.0 %reduce-scatter.76.cloned.1.call-start = ((), (), s32[]{:S(2)}) async-start(), calls=%async_computation.48 | async-start | bytes 983040 | tf_op jit(solution)/shard_map/reduce_scatter | solution.py:46
  445.2 71.8 %copy-start.146 = (f32[768]{0:T(1024)S(1)}, f32[768]{0:T(1024)}, u32[]{:S(2)}) copy-start(f32[768]{0:T(1024)} %get-tuple-element.103) | copy-start | bytes 9220
  659.0 50.5 %reduce-scatter.84.cloned.1.call-start = ((), (), s32[]{:S(2)}) async-start(), calls=%async_computation.52 | async-start | bytes 983040 | tf_op jit(solution)/shard_map/reduce_scatter | solution.py:46
  687.4 77.4 %reduce-scatter.78.cloned.1.call-start = ((), (), s32[]{:S(2)}) async-start(), calls=%async_computation.49 | async-start | bytes 983040 | tf_op jit(solution)/shard_map/reduce_scatter | solution.py:46
  688.8 38.9 %copy-start.20 = (bf16[2,2,192,768]{3,2,1,0:T(8,128)(2,1)S(1)}, bf16[2,2,192,768]{3,2,1,0:T(8,128)(2,1)}, u32[]{:S(2)}) copy-start(bf16[2,2,192,768]{3,2,1,0:T(8,128)(2,1)} %param.30) | copy-start | bytes 3538948
  688.8 39.2 %copy-start.121 = (bf16[256,3,64]{0,2,1:T(8,128)(2,1)S(1)}, bf16[256,3,64]{0,2,1:T(8,128)(2,1)}, u32[]{:S(2)}) copy-start(bf16[256,3,64]{0,2,1:T(8,128)(2,1)} %get-tuple-element.305) | copy-start | bytes 294916
  688.8 39.2 %copy-start.129 = (bf16[1,256,1,192]{1,3,2,0:T(8,128)(2,1)S(1)}, bf16[1,256,1,192]{1,3,2,0:T(8,128)(2,1)}, u32[]{:S(2)}) copy-start(bf16[1,256,1,192]{1,3,2,0:T(8,128)(2,1)} %slice.922) | copy-start | bytes 294916
  688.8 39.2 %copy-start.243 = (pred[256]{0:T(512)(128)(4,1)S(1)}, pred[256]{0:T(512)(128)(4,1)}, u32[]{:S(2)}) copy-start(pred[256]{0:T(512)(128)(4,1)} %copy-done.242) | copy-start | bytes 772
  688.8 39.2 %copy-start.263 = (f32[3,256]{1,0:T(4,128)S(1)}, f32[3,256]{1,0:T(4,128)}, u32[]{:S(2)}) copy-start(f32[3,256]{1,0:T(4,128)} %get-tuple-element.321) | copy-start | bytes 9220
  737.6 49.8 %reduce-scatter.86.cloned.1.call-start = ((), (), s32[]{:S(2)}) async-start(), calls=%async_computation.53 | async-start | bytes 983040 | tf_op jit(solution)/shard_map/reduce_scatter | solution.py:46
  762.1 27.0 %copy-start.100 = (bf16[3,64,256]{2,1,0:T(8,128)(2,1)}, bf16[3,64,256]{2,1,0:T(8,128)(2,1)S(1)}, u32[]{:S(2)}) copy-start(bf16[3,64,256]{2,1,0:T(8,128)(2,1)S(1)} %get-tuple-element.338) | copy-start | bytes 294916
  762.1 25.3 %copy-start.9 = (f32[1,64,768]{2,1,0:T(8,128)S(1)}, f32[1,64,768]{2,1,0:T(8,128)}, u32[]{:S(2)}) copy-start(f32[1,64,768]{2,1,0:T(8,128)} %copy-done.8) | copy-start | bytes 589828
  762.1 25.2 %copy-start.168 = (f32[64]{0:T(128)S(1)}, f32[64]{0:T(128)}, u32[]{:S(2)}) copy-start(f32[64]{0:T(128)} %copy-done.167) | copy-start | bytes 772
  762.1 25.2 %copy-start.185 = (f32[64]{0:T(128)S(1)}, f32[64]{0:T(128)}, u32[]{:S(2)}) copy-start(f32[64]{0:T(128)} %copy-done.184) | copy-start | bytes 772
  763.6 85.5 %reduce-scatter.80.cloned.1.call-start = ((), (), s32[]{:S(2)}) async-start(), calls=%async_computation.50 | async-start | bytes 983040 | tf_op jit(solution)/shard_map/reduce_scatter | solution.py:46
  806.7 25.7 %copy-start.46 = (bf16[256,768]{1,0:T(8,128)(2,1)}, bf16[256,768]{1,0:T(8,128)(2,1)S(1)}, u32[]{:S(2)}) copy-start(bf16[256,768]{1,0:T(8,128)(2,1)S(1)} %get-tuple-element.354) | copy-start | bytes 1179652
  809.5 51.3 %reduce-scatter.88.cloned.1.call-start = ((), (), s32[]{:S(2)}) async-start(), calls=%async_computation.54 | async-start | bytes 983040 | tf_op jit(solution)/shard_map/reduce_scatter | solution.py:46
  835.4 133.6 %reduce-scatter.100.cloned.1.call-start = ((), (), s32[]{:S(2)}) async-start(), calls=%async_computation.60 | async-start | bytes 442368
  849.0 145.9 %reduce-scatter.98.cloned.1.call-start = ((), (), s32[]{:S(2)}) async-start(), calls=%async_computation.59 | async-start | bytes 442368
  866.4 129.3 %reduce-scatter.102.cloned.1.call-start = ((), (), s32[]{:S(2)}) async-start(), calls=%async_computation.61 | async-start | bytes 442368
  870.3 137.3 %reduce-scatter.104.cloned.1.call-start = ((), (), s32[]{:S(2)}) async-start(), calls=%async_computation.62 | async-start | bytes 442368
  873.5 224.1 %all-reduce.6.cloned.1.call-start = ((), (), s32[]{:S(2)}) async-start(), calls=%async_computation.63 | async-start | bytes 9437184
  886.1 237.3 %reduce-scatter.90.cloned.1.call-start = ((), (), s32[]{:S(2)}) async-start(), calls=%async_computation.55 | async-start | bytes 983040 | tf_op jit(solution)/shard_map/reduce_scatter | solution.py:46
  930.8 217.6 %reduce-scatter.82.cloned.1.call-start = ((), (), s32[]{:S(2)}) async-start(), calls=%async_computation.51 | async-start | bytes 983040 | tf_op jit(solution)/shard_map/reduce_scatter | solution.py:46
  938.5 249.4 %reduce-scatter.96.cloned.1.call-start = ((), (), s32[]{:S(2)}) async-start(), calls=%async_computation.58 | async-start | bytes 1327104
  943.1 296.5 %reduce-scatter.94.cloned.1.call-start = ((), (), s32[]{:S(2)}) async-start(), calls=%async_computation.57 | async-start | bytes 3981312
  959.1 338.3 %reduce-scatter.92.cloned.1.call-start = ((), (), s32[]{:S(2)}) async-start(), calls=%async_computation.56 | async-start | bytes 5308416 | tf_op jit(solution)/shard_map/reduce_scatter | solution.py:434
  (234 other events, 1240.2 us)
Sparse Core Ops, SparseCore 0:
  35.2 26.0 reduce-scatter.43
  63.6 22.5 reduce-scatter.51
  88.5 25.2 reduce-scatter.59
  116.0 22.8 reduce-scatter.67
  141.0 24.6 reduce-scatter.45
  167.9 24.8 reduce-scatter.53
  195.1 26.4 reduce-scatter.69
  223.8 26.3 reduce-scatter.61
  259.5 26.8 reduce-scatter.47
  288.5 25.8 reduce-scatter.55
  316.8 25.9 reduce-scatter.71
  345.0 25.1 reduce-scatter.63
  374.1 25.6 reduce-scatter.49
  401.9 23.8 reduce-scatter.57
  428.0 22.8 reduce-scatter.73
  453.0 61.6 reduce-scatter.65
  659.1 26.2 reduce-scatter.75
  687.5 21.9 reduce-scatter.83
  737.7 24.6 reduce-scatter.77
  764.6 22.7 reduce-scatter.85
  809.7 25.8 reduce-scatter.79
  837.9 22.9 reduce-scatter.87
  863.9 33.0 reduce-scatter.99
  900.0 33.8 reduce-scatter.97
  936.9 33.8 reduce-scatter.101
  973.7 33.8 reduce-scatter.103
  1010.8 86.7 all-reduce.5
  1100.0 23.3 reduce-scatter.89
  1125.8 22.5 reduce-scatter.81
  1151.8 36.0 reduce-scatter.95
  1191.4 48.0 reduce-scatter.93
  1243.6 53.8 reduce-scatter.91
Sparse Core Ops, SparseCore 1:
  436.8 184.7 all-gather.1
where the time goes:
time: 1320 us; the launch traced here: 1310 us
  waiting for transfers between devices  512 us (39%)
  blocking collectives  384 us (29%)
  matrix products  185 us (14%)
  other arithmetic  107 us (8%)
  local copies, waits for them, and re-layouts  93.8 us (7%)
  between operations  22.1 us (2%)
    all_gather x12, blocking collectives, rows_gather(): return lax.all_gather(piece, 'tensor', axis=1, tiled=True)  201 us
    unnamed x40, waiting for transfers between devices  176 us
    all_gather x8, blocking collectives, grad_gather(): return lax.all_gather(piece, 'tensor', axis=1, tiled=True)  127 us
    reduce_scatter x16, waiting for transfers between devices, branch_total(): lax.psum_scatter(partial_value, 'tensor', scatter_dimension=1, tiled=True)  104 us
    reduce_scatter x8, waiting for transfers between devices, grad_total(): lax.psum_scatter(partial_value, 'tensor', scatter_dimension=1, tiled=True)  96.6 us
    all_gather x1, waiting for transfers between devices, per_device(): lax.all_gather(negatives, ('rep', 'tensor'), axis=0, tiled=True)  80.2 us
    dot_general x28, matrix products, apply_matrix(): jnp.dot(rows_three.reshape(-1, rows_three.shape[-1]), matrix, preferred_e...  72.2 us
    reduce_scatter x1, waiting for transfers between devices, per_device(): lax.psum_scatter(layer_grads[4], ('dp', 'rep'), scatter_dimension=1, tile...  55.4 us
  transfers between devices with their start and end apart: 33, of which 15 were waited for; matrix products, arithmetic and copies ran while one was open for 23% of the time, Pallas kernels for 0%

commit v1 on v0

v1 whole, which is shorter than its diff:
```python
import jax
import jax.numpy as jnp
from jax import lax
from jax.experimental import pallas as pl
from jax.experimental.pallas import tpu as pltpu
from jax.sharding import PartitionSpec as P

HEAD_DIM = 64
CROP_SLOTS = 256
SOFTMAX_WARMTH = 0.05
NORM_EPS = 1e-12
UNIT_EPS = 1e-06
MASKED = -1e30
TOP_PRECISION = lax.Precision.HIGHEST
ROOT_HALF = 0.7071067811865476
INV_ROOT_TAU = 0.3989422804014327

MESH = pl.DeviceIdType.MESH
BF = jnp.bfloat16
F32 = jnp.float32
CHUNKS = 4
TILE = 64
VMEM_LIMIT = 62 * 1024 * 1024


def nn(a, b):
    return jnp.dot(a, b, preferred_element_type=F32)


def nt(a, b):
    return lax.dot_general(a, b, (((1,), (1,)), ((), ())), preferred_element_type=F32)


def tn(a, b):
    return lax.dot_general(a, b, (((0,), (0,)), ((), ())), preferred_element_type=F32)


def greet_line():
    z = lax.axis_index("tensor")
    sem = pltpu.get_barrier_semaphore()
    for d in (1, 2, 3):
        pl.semaphore_signal(sem, inc=1, device_id={"tensor": (z + d) % 4}, device_id_type=MESH)
    pl.semaphore_wait(sem, 3)


class Line:
    def __init__(self, part, sbuf, tbuf, x1, x2, s_sem, t_sem, r1, r2):
        z = lax.axis_index("tensor")
        self.mid = (z + 1) // 2 == 1
        self.end = (z + 1) // 2 != 1
        self.inner = 1 + z // 2
        self.outer = 3 * (z // 2)
        self.cross = 3 - z
        self.part, self.sbuf, self.tbuf, self.x1, self.x2 = part, sbuf, tbuf, x1, x2
        self.s_sem, self.t_sem, self.r1, self.r2 = s_sem, t_sem, r1, r2
        self.size = part.shape[1] // CHUNKS

    def rows(self, c):
        return pl.ds(c * self.size, self.size)

    def to_inner(self, s, c):
        return pltpu.make_async_remote_copy(
            src_ref=self.sbuf.at[s, self.rows(c)], dst_ref=self.x2.at[s, self.rows(c)],
            send_sem=self.s_sem.at[s, c], recv_sem=self.r2.at[s, c],
            device_id={"tensor": self.inner}, device_id_type=MESH)

    def to_cross(self, s, c, slot):
        return pltpu.make_async_remote_copy(
            src_ref=self.sbuf.at[s, self.rows(c)], dst_ref=self.x1.at[slot, s, self.rows(c)],
            send_sem=self.s_sem.at[s, c], recv_sem=self.r1.at[slot, s, c],
            device_id={"tensor": self.cross}, device_id_type=MESH)

    def to_outer(self, s, c, slot):
        return pltpu.make_async_remote_copy(
            src_ref=self.tbuf.at[s, self.rows(c)], dst_ref=self.x1.at[slot, s, self.rows(c)],
            send_sem=self.t_sem.at[s, c], recv_sem=self.r1.at[slot, s, c],
            device_id={"tensor": self.outer}, device_id_type=MESH)

    def begin(self, s):
        @pl.when(self.end)
        def _():
            for c in range(CHUNKS):
                rows = self.rows(c)
                self.sbuf[s, rows] = self.part[s, rows].astype(BF)
                self.to_inner(s, c).start()

    def inward(self, s, c, slot, live):
        @pl.when(self.mid & live)
        def _():
            rows = self.rows(c)
            self.to_inner(s, c).wait_recv()
            self.sbuf[s, rows] = (self.part[s, rows] + self.x2[s, rows].astype(F32)).astype(BF)
            self.to_cross(s, c, slot).start()

    def outward(self, s, c, slot, live):
        @pl.when(self.mid & live)
        def _():
            rows = self.rows(c)
            self.to_cross(s, c, slot).wait_recv()
            joint = self.part[s, rows] + self.x1[slot, s, rows].astype(F32)
            self.part[s, rows] = joint + self.x2[s, rows].astype(F32)
            self.tbuf[s, rows] = joint.astype(BF)
            self.to_outer(s, c, slot).start()

    def finish(self, s, slot):
        @pl.when(self.end)
        def _():
            for c in range(CHUNKS):
                rows = self.rows(c)
                self.to_outer(s, c, slot).wait_recv()
                self.part[s, rows] = self.part[s, rows] + self.x1[slot, s, rows].astype(F32)
            for c in range(CHUNKS):
                self.to_inner(s, c).wait_send()

        @pl.when(self.mid)
        def _():
            for c in range(CHUNKS):
                self.to_cross(s, c, slot).wait_send()
                self.to_outer(s, c, slot).wait_send()


def line_scratch(streams, rows, width):
    return [
        pltpu.VMEM((streams, rows, width), F32),
        pltpu.VMEM((streams, rows, width), BF),
        pltpu.VMEM((streams, rows, width), BF),
        pltpu.VMEM((2, streams, rows, width), BF),
        pltpu.VMEM((streams, rows, width), BF),
        pltpu.SemaphoreType.DMA((streams, CHUNKS)),
        pltpu.SemaphoreType.DMA((streams, CHUNKS)),
        pltpu.SemaphoreType.DMA((2, streams, CHUNKS)),
        pltpu.SemaphoreType.DMA((streams, CHUNKS)),
    ]


def tiles(rows, body):
    def step(c, carry):
        body(pl.ds(pl.multiple_of(c * TILE, TILE), TILE))
        return carry

    lax.fori_loop(0, rows // TILE, step, 0)


def normalize(total, gain, shift):
    mean = jnp.mean(total, axis=-1, keepdims=True)
    centered = total - mean
    inverse = lax.rsqrt(jnp.mean(centered * centered, axis=-1, keepdims=True) + NORM_EPS)
    normed = centered * inverse
    return normed * gain + shift, normed, inverse


def head_masks(width, scale):
    lane = lax.broadcasted_iota(jnp.int32, (1, width), 1)
    return [
        jnp.where((lane >= h * HEAD_DIM) & (lane < (h + 1) * HEAD_DIM), scale, 0.0).astype(BF)
        for h in range(width // HEAD_DIM)
    ]


def forward_kernel(
    q_tok, q_drop, q_len, k_tok, k_drop, k_len,
    wqkv, abias, wm, mbias, we, ebias, ws, sbias, gains, shifts,
    acts, pooled, slots, xin, proj, probs, mixed, n1, i1, first, slope, active, n2, i2,
    h, hb, qkv, pb, mx, inner, act, vbias, valid, part, sbuf, tbuf, x1, x2, s_sem, t_sem, r1, r2,
):
    micro = q_tok.shape[0]
    rows, width = q_tok.shape[2:]
    layers = we.shape[1]
    local = wm.shape[2]
    heads = local // HEAD_DIM
    streams = 2 * micro
    last = 2 * layers * streams
    greet_line()
    line = Line(part, sbuf, tbuf, x1, x2, s_sem, t_sem, r1, r2)

    def compact(tok, drop, length, slots_out, s, m):
        pos = lax.broadcasted_iota(jnp.int32, (1, rows), 1)
        kept = (pos < length) & ((drop[m] == 0) | (pos == 0))
        kept_f = jnp.broadcast_to(jnp.where(kept, 1.0, 0.0), (16, rows))
        down = lax.broadcasted_iota(jnp.int32, (rows, rows), 0)
        along = lax.broadcasted_iota(jnp.int32, (rows, rows), 1)
        tri = jnp.where(down <= along, 1.0, 0.0).astype(BF)
        order = nn(kept_f.astype(BF), tri)[0:1] - 1.0
        order = jnp.where(kept, order, -1.0)
        count = jnp.sum(kept_f[0:1], axis=-1, keepdims=True)
        pick = jnp.where(order == down.astype(F32), 1.0, 0.0).astype(BF)
        rows_now = nn(pick, tok[m, 0])
        h[s] = rows_now
        hb[...] = rows_now.astype(BF)
        fits = pos.astype(F32) < count
        vbias[s] = jnp.broadcast_to(jnp.where(fits, 0.0, MASKED), (8, rows))
        valid[s] = jnp.broadcast_to(jnp.where(fits, 1.0, 0.0), (8, rows))
        pooled[s, 1:2] = jnp.broadcast_to(count, (1, width))
        if slots_out:
            slots[m] = jnp.broadcast_to(order, (8, rows))

    def at(i):
        j = jnp.maximum(i, 0)
        return j % streams, (j // streams) % 2, (i >= 0) & (i < last)

    def serve(i, *which):
        s1, slot1, live1 = at(i - 1)
        s2, slot2, live2 = at(i - 2)
        for kind, c in which:
            if kind == 1:
                line.inward(s1, c, slot1, live1)
            else:
                line.outward(s2, c, slot2, live2)

    def attention_pass(layer, s):
        i = layer * 2 * streams + s
        e, m = 1 - s // micro, s % micro
        is_q = s >= micro
        serve(i, (1, 0))

        @pl.when(layer == 0)
        def _():
            @pl.when(s < micro)
            def _():
                compact(k_tok, k_drop, k_len[m, 0], False, s, m)

            @pl.when(is_q)
            def _():
                compact(q_tok, q_drop, q_len[m, 0], True, s, m)

        @pl.when(layer > 0)
        def _():
            line.finish(s, 1)
            lp = layer - 1
            bias = sbias[e, lp].astype(F32)
            gain = gains[e, lp, 1:2].astype(F32)
            shift = shifts[e, lp, 1:2].astype(F32)

            def norm(r):
                out, normed, inverse = normalize(h[s, r] + part[s, r] + bias, gain, shift)
                h[s, r] = out
                hb[r] = out.astype(BF)

                @pl.when(is_q)
                def _():
                    n2[lp, m, r] = normed
                    i2[lp, m, r] = jnp.broadcast_to(inverse, (TILE, 128))

            tiles(rows, norm)

        serve(i, (1, 1))

        @pl.when(layer < layers)
        def _():
            @pl.when(is_q)
            def _():
                xin[layer, m] = hb[...]

            rows_now = hb[...]
            for j in range(3):
                bias = 0.0 if j == 1 else abias[e, layer, j // 2 : j // 2 + 1].astype(F32)
                qkv[j] = (nn(rows_now, wqkv[e, layer, j]) + bias).astype(BF)

            @pl.when(is_q)
            def _():
                for j in range(3):
                    proj[layer, m, j] = qkv[j]

        serve(i, (1, 2), (2, 0))
        q_masks = head_masks(local, HEAD_DIM**-0.5)
        v_masks = head_masks(local, 1.0)

        def one_head(hd):
            @pl.when(layer < layers)
            def _():
                scores = nt(qkv[0] * q_masks[hd], qkv[1]) + vbias[s, 0:1]
                expo = jnp.exp(scores - jnp.max(scores, axis=-1, keepdims=True))
                chance = (expo / jnp.sum(expo, axis=-1, keepdims=True)).astype(BF)
                pb[hd] = chance

                @pl.when(is_q)
                def _():
                    probs[layer, m, hd] = chance

                out = nn(chance, qkv[2] * v_masks[hd])
                if hd == 0:
                    mx[...] = out
                else:
                    mx[...] += out

        for hd in range(heads):
            one_head(hd)
            if hd == 0:
                serve(i, (1, 3), (2, 1))
            elif hd == 1:
                serve(i, (2, 2))

        @pl.when(layer < layers)
        def _():
            mixed_now = mx[...].astype(BF)

            @pl.when(is_q)
            def _():
                mixed[layer, m] = mixed_now

            part[s] = nn(mixed_now, wm[e, layer])
            line.begin(s)

        serve(i, (2, 3))

        @pl.when(layer == layers)
        def _():
            pooled[s, 0:1] = jnp.dot(valid[s], h[s], precision=TOP_PRECISION, preferred_element_type=F32)[0:1]

            @pl.when(is_q)
            def _():
                acts[m] = hb[...]

    def forward_pass(layer, s):
        i = (layer * 2 + 1) * streams + s
        e, m = 1 - s // micro, s % micro
        is_q = s >= micro
        serve(i, (1, 0))
        line.finish(s, 0)
        bias = mbias[e, layer].astype(F32)
        gain = gains[e, layer, 0:1].astype(F32)
        shift = shifts[e, layer, 0:1].astype(F32)

        def norm(r):
            out, normed, inverse = normalize(h[s, r] + part[s, r] + bias, gain, shift)
            h[s, r] = out
            hb[r] = out.astype(BF)

            @pl.when(is_q)
            def _():
                n1[layer, m, r] = normed
                i1[layer, m, r] = jnp.broadcast_to(inverse, (TILE, 128))
                first[layer, m, r] = out.astype(BF)

        tiles(rows, norm)
        serve(i, (1, 1), (2, 0))
        inner[...] = nn(hb[...], we[e, layer])
        serve(i, (1, 2), (2, 1))
        bias_e = ebias[e, layer].astype(F32)

        def gelu(r):
            u = inner[r] + bias_e
            phi = 0.5 * (1.0 + lax.erf(u * ROOT_HALF))
            out = (u * phi).astype(BF)
            act[r] = out

            @pl.when(is_q)
            def _():
                active[layer, m, r] = out
                slope[layer, m, r] = phi + u * jnp.exp(-0.5 * u * u) * INV_ROOT_TAU

        tiles(rows, gelu)
        serve(i, (1, 3), (2, 2))
        part[s] = nn(act[...], ws[e, layer])
        line.begin(s)
        serve(i, (2, 3))

    def layer_step(layer, carry):
        def a_step(s, c):
            attention_pass(layer, s)
            return c

        lax.fori_loop(0, streams, a_step, 0)

        @pl.when(layer < layers)
        def _():
            def f_step(s, c):
                forward_pass(layer, s)
                return c

            lax.fori_loop(0, streams, f_step, 0)

        return carry

    lax.fori_loop(0, layers + 1, layer_step, 0)


def run_forward(q_tok, q_drop, q_len, k_tok, k_drop, k_len, weights):
    micro, _, rows, width = q_tok.shape
    wqkv, abias, wm, mbias, we, ebias, ws, sbias, gains, shifts = weights
    layers, local, units = we.shape[1], wm.shape[2], we.shape[3]
    heads = local // HEAD_DIM
    streams = 2 * micro
    lm = (layers, micro)
    shapes = [
        ((micro, rows, width), BF),
        ((streams, 8, width), F32),
        ((micro, 8, rows), F32),
        (lm + (rows, width), BF),
        (lm + (3, rows, local), BF),
        (lm + (heads, rows, rows), BF),
        (lm + (rows, local), BF),
        (lm + (rows, width), F32),
        (lm + (rows, 128), F32),
        (lm + (rows, width), BF),
        (lm + (rows, units), F32),
        (lm + (rows, units), BF),
        (lm + (rows, width), F32),
        (lm + (rows, 128), F32),
    ]
    vm = pl.BlockSpec(memory_space=pltpu.VMEM)
    sm = pl.BlockSpec(memory_space=pltpu.SMEM)
    return pl.pallas_call(
        forward_kernel,
        out_shape=[jax.ShapeDtypeStruct(*s) for s in shapes],
        in_specs=[vm, vm, sm, vm, vm, sm] + [vm] * 10,
        out_specs=[vm] * len(shapes),
        scratch_shapes=[
            pltpu.VMEM((streams, rows, width), F32),
            pltpu.VMEM((rows, width), BF),
            pltpu.VMEM((3, rows, local), BF),
            pltpu.VMEM((heads, rows, rows), BF),
            pltpu.VMEM((rows, local), F32),
            pltpu.VMEM((rows, units), F32),
            pltpu.VMEM((rows, units), BF),
            pltpu.VMEM((streams, 8, rows), F32),
            pltpu.VMEM((streams, 8, rows), F32),
        ]
        + line_scratch(streams, rows, width),
        compiler_params=pltpu.CompilerParams(
            collective_id=0, has_side_effects=True, vmem_limit_bytes=VMEM_LIMIT
        ),
        name="encoders_forward",
    )(q_tok, q_drop, q_len, k_tok, k_drop, k_len, *weights)


def norm_back(g, normed, inverse, gain):
    scaled = g * gain
    return inverse * (
        scaled
        - jnp.mean(scaled, axis=-1, keepdims=True)
        - normed * jnp.mean(scaled * normed, axis=-1, keepdims=True)
    )


def fold(x):
    return jnp.sum(x.reshape(x.shape[0] // 8, 8, x.shape[1]), axis=0)


def backward_kernel(
    pgrad, slots, xin, proj, probs, mixed, n1, i1, first, slope, active, n2, i2,
    wqkv, wm, we, ws, gains,
    g_in, g_attend, g_merge, g_expand, g_shrink, g_vec, g_abias,
    dr, low, dinner, tmp, dqkv, dsc, dpart, part, sbuf, tbuf, x1, x2, s_sem, t_sem, r1, r2,
):
    layers, micro, rows, width = xin.shape
    local = wm.shape[1]
    heads = local // HEAD_DIM
    streams = micro
    last = 2 * layers * streams
    greet_line()
    line = Line(part, sbuf, tbuf, x1, x2, s_sem, t_sem, r1, r2)
    g_vec[...] = jnp.zeros_like(g_vec)
    g_abias[...] = jnp.zeros_like(g_abias)

    def serve(i, *which):
        j = jnp.maximum(i - 1, 0)
        s, slot, live = j % streams, (j // streams) % 2, (i >= 1) & (i <= last)
        for kind, c in which:
            if kind == 1:
                line.inward(s, c, slot, live)
            else:
                line.outward(s, c, slot, live)

    def add_to(ref, s, value):
        @pl.when(s == 0)
        def _():
            ref[...] = value

        @pl.when(s > 0)
        def _():
            ref[...] += value

    def mlp_back(step, s):
        layer = layers - 1 - step
        i = step * 2 * streams + s

        @pl.when(step == 0)
        def _():
            def seed(c, carry):
                r = pl.ds(pl.multiple_of(c * TILE, TILE), TILE)
                pos = (lax.broadcasted_iota(jnp.int32, (TILE, 1), 0) + c * TILE).astype(F32)
                part[s, r] = jnp.where(pos < pgrad[s, 1:2, 0:1], pgrad[s, 0:1], 0.0)
                dr[s, r] = jnp.zeros((TILE, width), F32)
                return carry

            lax.fori_loop(0, rows // TILE, seed, 0)

        @pl.when(step > 0)
        def _():
            line.finish(s, 1)

        gain = gains[layer, 1:2].astype(F32)

        def back(r):
            g = part[s, r] + dr[s, r]
            normed = n2[layer, s, r]
            out = norm_back(g, normed, i2[layer, s, r][:, 0:1], gain)
            dr[s, r] = out
            low[s, r] = out.astype(BF)
            g_vec[layer, 1] += fold(g * normed)
            g_vec[layer, 3] += fold(g)
            g_vec[layer, 4] += fold(out)

        tiles(rows, back)
        serve(i, (1, 0))
        tmp[...] = nt(low[s], ws[layer])
        serve(i, (1, 1))

        def slopes(r):
            out = tmp[r] * slope[layer, s, r]
            dinner[r] = out.astype(BF)
            g_vec[layer, 6] += fold(out)

        tiles(rows, slopes)
        part[s] = nt(dinner[...], we[layer])
        line.begin(s)
        serve(i, (1, 2), (2, 0))
        add_to(g_shrink.at[layer], s, tn(active[layer, s], low[s]))
        serve(i, (1, 3), (2, 1))
        add_to(g_expand.at[layer], s, tn(first[layer, s], dinner[...]))
        serve(i, (2, 2), (2, 3))

    def attention_back(step, s):
        layer = layers - 1 - step
        i = (step * 2 + 1) * streams + s
        line.finish(s, 0)
        gain = gains[layer, 0:1].astype(F32)

        def back(r):
            g = part[s, r] + dr[s, r]
            normed = n1[layer, s, r]
            out = norm_back(g, normed, i1[layer, s, r][:, 0:1], gain)
            dr[s, r] = out
            low[s, r] = out.astype(BF)
            g_vec[layer, 0] += fold(g * normed)
            g_vec[layer, 2] += fold(g)
            g_vec[layer, 5] += fold(out)

        tiles(rows, back)
        serve(i, (1, 0))
        dmix = nt(low[s], wm[layer]).astype(BF)
        serve(i, (1, 1))
        masks = head_masks(local, 1.0)
        for hd in range(heads):
            chance_b = probs[layer, s, hd]
            chance = chance_b.astype(F32)
            dm = dmix * masks[hd]
            dch = nt(dm, proj[layer, s, 2])
            ds = chance * (dch - jnp.sum(chance * dch, axis=-1, keepdims=True))
            draw = (ds * HEAD_DIM**-0.5).astype(BF)
            dq = nn(draw, proj[layer, s, 1] * masks[hd])
            dk = tn(draw, proj[layer, s, 0] * masks[hd])
            dv = tn(chance_b, dm)
            if hd == 0:
                dqkv[0] = dq
                dqkv[1] = dk
                dqkv[2] = dv
            else:
                dqkv[0] += dq
                dqkv[1] += dk
                dqkv[2] += dv
            if hd == 0:
                serve(i, (1, 2), (2, 0))
            elif hd == 1:
                serve(i, (1, 3), (2, 1))
        g_abias[layer, 0] += fold(dqkv[0])
        g_abias[layer, 1] += fold(dqkv[2])
        for j in range(3):
            dsc[j] = dqkv[j].astype(BF)
        part[s] = nt(dsc[0], wqkv[layer, 0]) + nt(dsc[1], wqkv[layer, 1]) + nt(dsc[2], wqkv[layer, 2])
        line.begin(s)
        serve(i, (2, 2), (2, 3))
        add_to(g_merge.at[layer], s, tn(mixed[layer, s], low[s]))
        for j in range(3):
            add_to(g_attend.at[layer, j], s, tn(xin[layer, s], dsc[j]))

    def layer_step(step, carry):
        def m_step(s, c):
            mlp_back(step, s)
            return c

        def a_step(s, c):
            attention_back(step, s)
            return c

        lax.fori_loop(0, streams, m_step, 0)
        lax.fori_loop(0, streams, a_step, 0)
        return carry

    lax.fori_loop(0, layers, layer_step, 0)

    def tail(s, carry):
        @pl.when(s == 0)
        def _():
            for c in range(CHUNKS):
                serve(last, (1, c), (2, c))

        line.finish(s, 1)

        def back(r):
            low[s, r] = (part[s, r] + dr[s, r]).astype(BF)

        tiles(rows, back)
        down = lax.broadcasted_iota(jnp.int32, (rows, rows), 0).astype(F32)
        pick = jnp.where(slots[s, 0:1] == down, 1.0, 0.0).astype(BF)
        g_in[s] = tn(pick, low[s]).astype(BF)
        return carry

    lax.fori_loop(0, streams, tail, 0)


def run_backward(pgrad, slots, saved, weights):
    wqkv, abias, wm, mbias, we, ebias, ws, sbias, gains, shifts = weights
    layers, micro, rows, width = saved[0].shape
    local, units = wm.shape[2], we.shape[3]
    heads = local // HEAD_DIM
    shapes = [
        ((micro, rows, width), BF),
        ((layers, 3, width, local), F32),
        ((layers, local, width), F32),
        ((layers, width, units), F32),
        ((layers, units, width), F32),
        ((layers, 7, 8, width), F32),
        ((layers, 2, 8, local), F32),
    ]
    vm = pl.BlockSpec(memory_space=pltpu.VMEM)
    return pl.pallas_call(
        backward_kernel,
        out_shape=[jax.ShapeDtypeStruct(*s) for s in shapes],
        in_specs=[vm] * 18,
        out_specs=[vm] * len(shapes),
        scratch_shapes=[
            pltpu.VMEM((micro, rows, width), F32),
            pltpu.VMEM((micro, rows, width), BF),
            pltpu.VMEM((rows, units), BF),
            pltpu.VMEM((rows, units), F32),
            pltpu.VMEM((3, rows, local), F32),
            pltpu.VMEM((3, rows, local), BF),
            pltpu.VMEM((8, 128), F32),
        ]
        + line_scratch(micro, rows, width),
        compiler_params=pltpu.CompilerParams(
            collective_id=1, has_side_effects=True, vmem_limit_bytes=VMEM_LIMIT
        ),
        name="encoder_backward",
    )(pgrad, slots, *saved, wqkv[0], wm[0], we[0], ws[0], gains[0])


def contrast(mean_q, mean_k, negatives):
    key_dir = mean_k * lax.rsqrt(jnp.sum(mean_k * mean_k, axis=-1, keepdims=True) + UNIT_EPS)
    scale = lax.rsqrt(jnp.sum(mean_q * mean_q, axis=-1, keepdims=True) + UNIT_EPS)
    direction = mean_q * scale
    positive = jnp.sum(direction * key_dir, axis=-1) / SOFTMAX_WARMTH
    micro, width = mean_q.shape
    asked = lax.all_gather(direction.astype(BF), "rep", axis=0, tiled=True)
    logits = nt(asked, negatives) / SOFTMAX_WARMTH
    top = jnp.max(logits, axis=-1, keepdims=True)
    expo = jnp.exp(logits - top)
    total = jnp.sum(expo, axis=-1, keepdims=True)
    keys = jnp.dot(expo, negatives.astype(F32), precision=TOP_PRECISION)
    packed = jnp.concatenate([keys, jnp.broadcast_to(top, (top.shape[0], 128)), jnp.broadcast_to(total, (top.shape[0], 128))], axis=1)
    pieces = lax.all_gather(packed, ("rep", "tensor"), axis=0, tiled=False)
    mine = lax.dynamic_slice_in_dim(pieces, lax.axis_index("rep") * micro, micro, 1)
    keys, top, total = mine[..., :width], mine[..., width], mine[..., width + 128]
    best = jnp.maximum(jnp.max(top, axis=0), positive)
    weight = jnp.exp(top - best)
    own = jnp.exp(positive - best)
    total = jnp.sum(total * weight, axis=0) + own
    keys = jnp.sum(keys * weight[..., None], axis=0) + own[:, None] * key_dir
    per_query = best + jnp.log(total) - positive
    dqn = (keys / total[:, None] - key_dir) * (CROP_SLOTS / SOFTMAX_WARMTH)
    mean_grad = scale * (dqn - direction * jnp.sum(direction * dqn, axis=-1, keepdims=True))
    return per_query, mean_grad


def per_device(
    query_tokens, query_drop, query_length, key_tokens, key_drop, key_length, negatives,
    attend_weight, attend_bias, merge_weight, merge_bias, expand_weight, expand_bias,
    shrink_weight, shrink_bias, norm_gain, norm_shift,
):
    micro, _, rows, width = query_tokens.shape
    weights = (
        jnp.transpose(attend_weight, (0, 1, 3, 2, 4)),
        attend_bias,
        merge_weight,
        merge_bias[:, :, None],
        expand_weight,
        expand_bias[:, :, None],
        shrink_weight,
        shrink_bias[:, :, None],
        norm_gain,
        norm_shift,
    )
    acts, pooled, slots, *saved = run_forward(
        query_tokens, query_drop, query_length, key_tokens, key_drop, key_length, weights
    )
    counts = pooled[:, 1]
    means = pooled[:, 0] / counts
    per_query, mean_grad = contrast(means[micro:], means[:micro], negatives)
    pgrad = jnp.concatenate(
        [(mean_grad / counts[micro:])[:, None], counts[micro:, None], jnp.zeros((micro, 6, width), F32)], axis=1
    )
    g_in, g_attend, g_merge, g_expand, g_shrink, g_vec, g_abias = run_backward(pgrad, slots, saved, weights)
    share = rows // lax.axis_size("tensor")
    start = lax.axis_index("tensor") * share
    activations = lax.dynamic_slice_in_dim(acts, start, share, 1)[:, None]
    input_grad = lax.dynamic_slice_in_dim(g_in, start, share, 1)[:, None]
    groups = ("dp", "rep")
    attend = jnp.transpose(lax.psum_scatter(g_attend, groups, scatter_dimension=2, tiled=True), (0, 2, 1, 3))
    merge = lax.psum_scatter(g_merge, groups, scatter_dimension=2, tiled=True)
    expand = lax.psum_scatter(g_expand, groups, scatter_dimension=1, tiled=True)
    shrink = lax.psum_scatter(g_shrink, groups, scatter_dimension=2, tiled=True)
    vec = jnp.sum(g_vec, axis=2)
    shared, expand_bias_grad, attend_bias_grad, loss = lax.psum(
        (vec[:, :6], vec[:, 6], jnp.sum(g_abias, axis=2), jnp.sum(per_query)), groups
    )
    size = width // (lax.axis_size("dp") * lax.axis_size("rep"))
    own = lax.dynamic_slice_in_dim(shared, lax.axis_index(groups) * size, size, 2)
    loss = loss / (micro * lax.axis_size("dp") * lax.axis_size("rep"))
    return (
        activations, input_grad, attend, attend_bias_grad, merge, own[:, 5], expand,
        expand_bias_grad, shrink, own[:, 4], own[:, 0:2], own[:, 2:4], loss,
    )


def solution(mesh):
    return jax.shard_map(
        per_device,
        mesh=mesh,
        in_specs=(
            P(None, ("dp", "rep"), None, None),
            P(None, ("dp", "rep"), None),
            P(None, ("dp", "rep")),
            P(None, ("dp", "rep"), None, None),
            P(None, ("dp", "rep"), None),
            P(None, ("dp", "rep")),
            P(("rep", "tensor"), None),
            P(None, None, None, None, "tensor"),
            P(None, None, None, "tensor"),
            P(None, None, "tensor", None),
            P(),
            P(None, None, None, "tensor"),
            P(None, None, "tensor"),
            P(None, None, "tensor", None),
            P(),
            P(),
            P(),
        ),
        out_specs=(
            P(None, ("dp", "rep"), "tensor", None),
            P(None, ("dp", "rep"), "tensor", None),
            P(None, ("dp", "rep"), None, "tensor"),
            P(None, None, "tensor"),
            P(None, "tensor", ("dp", "rep")),
            P(None, ("dp", "rep")),
            P(None, ("dp", "rep"), "tensor"),
            P(None, "tensor"),
            P(None, "tensor", ("dp", "rep")),
            P(None, ("dp", "rep")),
            P(None, None, ("dp", "rep")),
            P(None, None, ("dp", "rep")),
            P(),
        ),
        check_vma=False,
    )
```

time: 1320 us -> 627 us (0.47)
  blocking collectives: 384 us -> 62 us
  waiting for transfers between devices: 512 us -> 200 us
  Pallas kernels: 0 us -> 300 us
  matrix products: 185 us -> 1.4 us
  other arithmetic: 107 us -> 3.63 us
  local copies, waits for them, and re-layouts: 93.8 us -> 43.1 us
    pallas_call x0 -> x2, Pallas kernels: none -> 300 us  [the longest x1 176 us: run_forward(): pl.pallas_call(forward_kernel, out_shape=[jax.ShapeDtypeStruct(*s) for s...]
    all_gather x20 -> x2, blocking collectives: 328 us -> 35.2 us  [the longest x1 30.9 us: contrast(): pieces = lax.all_gather(packed, ('rep', 'tensor'), axis=0, tiled=False)]
    dot_general x90 -> x2, matrix products: 170 us -> 1.4 us  [the longest x1 0.78 us: contrast(): keys = jnp.dot(expo, negatives.astype(F32), precision=TOP_PRECISION)]
    reduce_scatter x25 -> x2, waiting for transfers between devices: 256 us -> 114 us  [the longest x1 58.2 us: per_device(): expand = lax.psum_scatter(g_expand, groups, scatter_dimension=1, tiled=True)]
    unnamed x40 -> x6, waiting for transfers between devices: 176 us -> 85.2 us
    all_gather x1 -> x0, waiting for transfers between devices: 80.2 us -> none  [per_device(): lax.all_gather(negatives, ('rep', 'tensor'), axis=0, tiled=True)]
    reduce_sum x46 -> x8, other arithmetic: 44.6 us -> 1.92 us  [the longest x1 0.89 us: contrast(): keys = jnp.sum(keys * weight[..., None], axis=0) + own[:, None] * key_dir]
    unnamed x555 -> x43, local copies, waits for them, and re-layouts: 49.6 us -> 19.7 us
  transfers between devices with their start and end apart: 33 -> 4, of which waited for: 15 -> 3; matrix products, arithmetic and copies ran while one was open for 23% -> 3% of each run, Pallas kernels for 0% -> 0%
where the time goes in v1:
time: 627 us; the launch traced here: 626 us
  Pallas kernels  300 us (48%)
  waiting for transfers between devices  200 us (32%)
  blocking collectives  62 us (10%)
  local copies, waits for them, and re-layouts  43.1 us (7%)
  between operations  16.5 us (3%)
    pallas_call x1, Pallas kernels, run_forward(): pl.pallas_call(forward_kernel, out_shape=[jax.ShapeDtypeStruct(*s) for s...  176 us
    pallas_call x1, Pallas kernels, run_backward(): pl.pallas_call(backward_kernel, out_shape=[jax.ShapeDtypeStruct(*s) for s...  124 us
    unnamed x6, waiting for transfers between devices  85.2 us
    reduce_scatter x1, waiting for transfers between devices, per_device(): expand = lax.psum_scatter(g_expand, groups, scatter_dimension=1, tiled=True)  58.2 us
    reduce_scatter x1, waiting for transfers between devices, per_device(): lax.psum_scatter(g_attend, groups, scatter_dimension=2, tiled=True)  56.1 us
    all_gather x1, blocking collectives, contrast(): pieces = lax.all_gather(packed, ('rep', 'tensor'), axis=0, tiled=False)  30.9 us
    psum x1, blocking collectives, per_device(): lax.psum((vec[:, :6], vec[:, 6], jnp.sum(g_abias, axis=2), jnp.sum(per_qu...  26.8 us
    unnamed x43, local copies, waits for them, and re-layouts  19.7 us
  transfers between devices with their start and end apart: 4, of which 3 were waited for; matrix products, arithmetic and copies ran while one was open for 3% of the time, Pallas kernels for 0%

profile of v1, /device:TPU:0, one launch (start us, length us, event | category | flops | bytes accessed | tf_op | source)
XLA Modules:
  0.0 626.1 jit_solution(17796512585135955819)
XLA Ops:
  7.2 0.0 reduce-scatter.10.cloned.1.call-start
  7.3 6.4 %copy.82 = bf16[2,2,768,3,192]{4,2,3,1,0:T(8,128)(2,1)} copy(bf16[2,2,768,3,192]{2,4,3,1,0:T(8,128)(2,1)} %param.24) | data formatting | bytes 7077888 | tf_op args[7]
  13.7 0.6 copy.85.mbias
  14.3 0.6 copy.86.ebias
  14.9 0.6 copy.87.sbias
  15.5 0.6 copy.83.q_len
  16.2 0.6 copy.84.k_len
  16.8 175.9 %encoders_forward.1 = (bf16[2,256,768]{2,1,0:T(8,128)(2,1)}, f32[4,8,768]{2,1,0:T(8,128)}, f32[2,8,256]{2,1,0:T(8,128)}, bf16[2,2,256,768]{3,2,1,0:T(8,128)(2,1)...) custom-call(bf16[2,1,256,768]{3,2,1,0:T(8,128)(2,1)} %q_tok.1, ...), custom_call_target="tpu_custom_call" | custom-call | tf_op jit(solution)/shard_map/encoders_forward/pallas_call | solution.py:403
  192.7 0.9 copy.88
  193.7 0.1 multiply_reduce_fusion.3
  193.9 0.2 multiply_reduce_fusion.2
  194.1 4.3 all-gather.1
  198.4 0.6 fusion.14
  199.0 0.8 fusion.1
  199.8 0.2 fusion
  200.0 0.8 slice.77
  200.8 3.4 slice_bitcast_fusion.wqkv
  204.3 1.7 slice_bitcast_fusion.1.ws
  206.0 1.5 copy-done.3
  207.5 1.6 slice_bitcast_fusion.2.we
  209.1 0.1 copy-done.4
  209.2 0.9 slice_bitcast_fusion.3.wm
  210.0 0.6 slice_bitcast_fusion.6.gains
  210.6 0.1 broadcast_in_dim.46
  210.7 0.1 broadcast_in_dim.22
  210.8 30.9 %all-gather.2 = f32[8,4,1024]{2,1,0:T(4,128)S(1)} all-gather(f32[1,4,1024]{2,1,0:T(4,128)S(1)} %maximum_bitcast_fusion), channel_id=2, replica_groups=mesh['dp'=4,'rep'=2,'tensor'=4] {'rep','tensor'}, dimensions={0}, use_global_device_ids=true | all-gather | bytes 147456 | tf_op jit(solution)/shard_map/all_gather | solution.py:663
  241.7 0.2 fusion.13
  241.9 0.1 copy.101
  242.0 0.4 copy.100
  242.5 0.1 exponential_bitcast_fusion
  242.5 0.9 multiply_reduce_fusion
  243.4 0.1 copy.91
  243.6 0.1 copy.102
  243.7 0.2 fusion.9
  243.9 0.6 subtract_reduce_fusion
  244.5 0.2 multiply_reduce_fusion.1
  244.7 0.1 fusion.4
  244.8 0.1 pad.2.clone
  244.9 0.7 maximum_maximum_fusion.pgrad
  245.6 123.8 %encoder_backward.1 = (bf16[2,256,768]{2,1,0:T(8,128)(2,1)}, f32[2,3,768,192]{3,2,1,0:T(8,128)}, f32[2,192,768]{2,1,0:T(8,128)}, f32[2,768,768]{2,1,0:T(8,128)},...) custom-call(f32[2,8,768]{2,1,0:T(8,128)} %maximum_maximum_fusion.pgrad, ...), custom_call_target="tpu_custom_call" | custom-call | tf_op jit(solution)/shard_map/encoder_backward/pallas_call | solution.py:628
  369.4 2.5 copy.95
  371.9 2.3 reshape.81
  374.2 0.0 reduce-scatter.10.cloned.1.call-update
  374.2 0.0 all-reduce.4.cloned.1.call-start
  374.2 8.2 %copy.93 = f32[2,768,768]{1,0,2:T(2,128)} copy(f32[2,768,768]{2,1,0:T(8,128)} %get-tuple-element.54) | data formatting | bytes 9437184 | tf_op jit(solution)/shard_map/encoder_backward/pallas_call | solution.py:628
  382.5 0.0 all-reduce.4.cloned.1.call-update
  382.5 0.0 reduce-scatter.6.cloned.1.call-start
  382.5 0.7 reduce-scatter.6.cloned.1.call-update
  383.2 0.0 reduce-scatter.8.cloned.1.call-start
  383.3 0.5 reduce-scatter.8.cloned.1.call-update
  383.8 0.5 copy-done.5
  384.3 0.1 reduce_sum.98
  384.4 0.6 dynamic-slice.1
  385.7 26.8 %all-reduce.1 = (f32[2,2,192]{2,1,0:T(2,128)}, f32[2,6,768]{2,1,0:T(8,128)S(1)}, f32[2,768]{1,0:T(2,128)}, f32[]{:T(128)}) all-reduce(f32[2,2,192]{2,1,0:T(2,128)S(1)} %reduce_sum.97, f32[2,6,768]{2,1,0:T(8,128)S(1)} %bitcast.75, f32[2,768]{1,0:T(2,128)S(1)} %bitcast.76, ...), channel_id=1, replica_groups=mesh['dp'=4,'rep'=2,'tensor'=4] {'dp','rep'}, use_global_device_ids=true, to_apply=%region_11.0 | all-reduce | flops 11521 | bytes 92168 | tf_op jit(solution)/shard_map/psum | solution.py:715
  413.1 0.7 constant_dynamic-slice_fusion.1
  413.8 0.7 constant_dynamic-slice_fusion.5
  414.4 1.8 dynamic-slice_bitcast_fusion
  416.2 1.1 reshape.82
  417.3 0.8 copy.96
  418.1 84.0 %all-reduce.4.cloned.1.call-done = f32[2,768,768]{1,0,2:T(2,128)} async-done(((f32[2,768,768]{1,0,2:T(2,128)}), f32[2,768,768]{1,0,2:T(2,128)}) %all-reduce.4.cloned.1.call-update) | async-done | bytes 4718608
  502.2 1.1 constant_dynamic-slice_fusion.7
  503.3 0.9 copy.94
  504.2 56.1 %reduce-scatter.6.cloned.1.call-done = f32[2,3,96,192]{3,2,1,0:T(8,128)} async-done(((f32[2,3,768,192]{3,2,1,0:T(8,128)}), f32[2,3,96,192]{3,2,1,0:T(8,128)}) %reduce-scatter.6.cloned.1.call-update) | async-done | bytes 442384 | tf_op jit(solution)/shard_map/reduce_scatter | solution.py:710
  560.2 58.2 %reduce-scatter.8.cloned.1.call-done = f32[2,96,768]{2,1,0:T(8,128)} async-done(((f32[2,768,768]{2,1,0:T(8,128)}), f32[2,96,768]{2,1,0:T(8,128)}) %reduce-scatter.8.cloned.1.call-update) | async-done | bytes 589840 | tf_op jit(solution)/shard_map/reduce_scatter | solution.py:712
  (39 shorter events, 0.2 us)
Async XLA Ops:
  7.2 191.2 %copy-start = (bf16[1024,768]{1,0:T(8,128)(2,1)S(1)}, bf16[1024,768]{1,0:T(8,128)(2,1)}, u32[]{:S(2)}) copy-start(bf16[1024,768]{1,0:T(8,128)(2,1)} %param.23) | copy-start | bytes 4718596
  7.2 6.5 %copy-start.8 = (bf16[2,2,768]{2,1,0:T(2,128)(2,1)S(1)}, bf16[2,2,768]{2,1,0:T(2,128)(2,1)}, u32[]{:S(2)}) copy-start(bf16[2,2,768]{2,1,0:T(2,128)(2,1)} %param.27) | copy-start | bytes 18436
  7.2 7.1 %copy-start.9 = (bf16[2,2,768]{2,1,0:T(2,128)(2,1)S(1)}, bf16[2,2,768]{2,1,0:T(2,128)(2,1)}, u32[]{:S(2)}) copy-start(bf16[2,2,768]{2,1,0:T(2,128)(2,1)} %param.29) | copy-start | bytes 18436
  7.2 7.7 %copy-start.10 = (bf16[2,2,768]{2,1,0:T(2,128)(2,1)S(1)}, bf16[2,2,768]{2,1,0:T(2,128)(2,1)}, u32[]{:S(2)}) copy-start(bf16[2,2,768]{2,1,0:T(2,128)(2,1)} %param.31) | copy-start | bytes 18436
  7.2 8.3 %copy-start.11 = (s32[2,1]{0,1:T(1,128)S(1)}, s32[2,1]{0,1:T(1,128)}, u32[]{:S(2)}) copy-start(s32[2,1]{0,1:T(1,128)} %param.19) | copy-start | bytes 28
  7.2 8.9 %copy-start.12 = (s32[2,1]{0,1:T(1,128)S(1)}, s32[2,1]{0,1:T(1,128)}, u32[]{:S(2)}) copy-start(s32[2,1]{0,1:T(1,128)} %param.22) | copy-start | bytes 28
  7.2 409.0 %reduce-scatter.10.cloned.1.call-start = ((), (), s32[]{:S(2)}) async-start(), calls=%async_computation.5 | async-start | bytes 1327104
  200.8 3.5 copy-start.2
  204.3 3.2 copy-start.3
  207.5 1.7 copy-start.4
  207.5 2.6 copy-start.7
  374.2 128.0 %all-reduce.4.cloned.1.call-start = ((), (), s32[]{:S(2)}) async-start(), calls=%async_computation.6 | async-start | bytes 9437184
  382.5 177.7 %reduce-scatter.6.cloned.1.call-start = ((), (), s32[]{:S(2)}) async-start(), calls=%async_computation.3 | async-start | bytes 5308416 | tf_op jit(solution)/shard_map/reduce_scatter | solution.py:710
  383.2 235.2 %reduce-scatter.8.cloned.1.call-start = ((), (), s32[]{:S(2)}) async-start(), calls=%async_computation.4 | async-start | bytes 5308416 | tf_op jit(solution)/shard_map/reduce_scatter | solution.py:712
  383.3 1.0 copy-start.5
  383.3 1.1 copy-start.6
  383.3 1.2 copy-start.13
  383.8 234.6 %copy-start.1 = (bf16[1024,768]{1,0:T(8,128)(2,1)S(1)}, bf16[1024,768]{1,0:T(8,128)(2,1)}, u32[]{:S(2)}) copy-start(bf16[1024,768]{1,0:T(8,128)(2,1)} %param.23) | copy-start | bytes 4718596
Sparse Core Ops, SparseCore 0:
  374.3 37.4 reduce-scatter.9
  415.5 86.6 all-reduce.3
  506.2 53.9 reduce-scatter.5
  564.5 53.8 reduce-scatter.7

commit v2 on v1

--- a/solution.py
+++ b/solution.py
@@ -1,3 +1,5 @@
+import functools
+
 import jax
 import jax.numpy as jnp
 from jax import lax
@@ -160,9 +162,16 @@
 def forward_kernel(
     q_tok, q_drop, q_len, k_tok, k_drop, k_len,
     wqkv, abias, wm, mbias, we, ebias, ws, sbias, gains, shifts,
-    acts, pooled, slots, xin, proj, probs, mixed, n1, i1, first, slope, active, n2, i2,
-    h, hb, qkv, pb, mx, inner, act, vbias, valid, part, sbuf, tbuf, x1, x2, s_sem, t_sem, r1, r2,
+    acts, pooled, slots, *rest,
 ):
+    kept, rest = rest[:11], rest[11:]
+    saved, rest = rest[:11], rest[11:]
+    loaded, rest = rest[:4], rest[4:]
+    h, hb, qkv, pb, mx, inner, act, vbias, valid, save_sem, load_sem, *line_refs = rest
+    xin, proj, probs, mixed, n1, i1, first, slope, active, n2, i2 = saved
+    part = line_refs[0]
+    stored = (wqkv, wm, we, ws)
+    wqkv, wm, we, ws = loaded
     micro = q_tok.shape[0]
     rows, width = q_tok.shape[2:]
     layers = we.shape[1]
@@ -170,8 +179,20 @@
     heads = local // HEAD_DIM
     streams = 2 * micro
     last = 2 * layers * streams
+
+    def load(k, e, layer):
+        return pltpu.make_async_copy(stored[k].at[e, layer], loaded[k].at[e, layer], load_sem.at[k, e, layer])
+
+    for layer in range(layers):
+        for e in (1, 0):
+            for k in range(4):
+                load(k, e, layer).start()
+
+    def save(k, layer, m):
+        return pltpu.make_async_copy(saved[k].at[layer, m], kept[k].at[layer, m], save_sem.at[k, layer, m])
+
     greet_line()
-    line = Line(part, sbuf, tbuf, x1, x2, s_sem, t_sem, r1, r2)
+    line = Line(*line_refs)
 
     def compact(tok, drop, length, slots_out, s, m):
         pos = lax.broadcasted_iota(jnp.int32, (1, rows), 1)
@@ -243,13 +264,24 @@
 
             tiles(rows, norm)
 
+            @pl.when(is_q)
+            def _():
+                for k in (9, 10):
+                    save(k, lp, m).start()
+
         serve(i, (1, 1))
+
+        @pl.when((layer < layers) & (m == 0))
+        def _():
+            for k in (0, 1):
+                load(k, e, layer).wait()
 
         @pl.when(layer < layers)
         def _():
             @pl.when(is_q)
             def _():
                 xin[layer, m] = hb[...]
+                save(0, layer, m).start()
 
             rows_now = hb[...]
             for j in range(3):
@@ -260,6 +292,7 @@
             def _():
                 for j in range(3):
                     proj[layer, m, j] = qkv[j]
+                save(1, layer, m).start()
 
         serve(i, (1, 2), (2, 0))
         q_masks = head_masks(local, HEAD_DIM**-0.5)
@@ -297,6 +330,8 @@
             @pl.when(is_q)
             def _():
                 mixed[layer, m] = mixed_now
+                for k in (2, 3):
+                    save(k, layer, m).start()
 
             part[s] = nn(mixed_now, wm[e, layer])
             line.begin(s)
@@ -333,6 +368,17 @@
                 first[layer, m, r] = out.astype(BF)
 
         tiles(rows, norm)
+
+        @pl.when(m == 0)
+        def _():
+            for k in (2, 3):
+                load(k, e, layer).wait()
+
+        @pl.when(is_q)
+        def _():
+            for k in (4, 5, 6):
+                save(k, layer, m).start()
+
         serve(i, (1, 1), (2, 0))
         inner[...] = nn(hb[...], we[e, layer])
         serve(i, (1, 2), (2, 1))
@@ -350,6 +396,12 @@
                 slope[layer, m, r] = phi + u * jnp.exp(-0.5 * u * u) * INV_ROOT_TAU
 
         tiles(rows, gelu)
+
+        @pl.when(is_q)
+        def _():
+            for k in (7, 8):
+                save(k, layer, m).start()
+
         serve(i, (1, 3), (2, 2))
         part[s] = nn(act[...], ws[e, layer])
         line.begin(s)
@@ -373,6 +425,13 @@
         return carry
 
     lax.fori_loop(0, layers + 1, layer_step, 0)
+
+    def drain(j, carry):
+        for k in range(len(saved)):
+            save(k, j // micro, j % micro).wait()
+        return carry
+
+    lax.fori_loop(0, layers * micro, drain, 0)
 
 
 def run_forward(q_tok, q_drop, q_len, k_tok, k_drop, k_len, weights):
@@ -399,13 +458,16 @@
         (lm + (rows, 128), F32),
     ]
     vm = pl.BlockSpec(memory_space=pltpu.VMEM)
+    hb = pl.BlockSpec(memory_space=pl.ANY)
     sm = pl.BlockSpec(memory_space=pltpu.SMEM)
     return pl.pallas_call(
         forward_kernel,
         out_shape=[jax.ShapeDtypeStruct(*s) for s in shapes],
-        in_specs=[vm, vm, sm, vm, vm, sm] + [vm] * 10,
-        out_specs=[vm] * len(shapes),
-        scratch_shapes=[
+        in_specs=[vm, vm, sm, vm, vm, sm] + [hb, vm, hb, vm, hb, vm, hb, vm, vm, vm],
+        out_specs=[vm] * 3 + [hb] * 11,
+        scratch_shapes=[pltpu.VMEM(*s) for s in shapes[3:]]
+        + [pltpu.VMEM(w.shape, BF) for w in (wqkv, wm, we, ws)]
+        + [
             pltpu.VMEM((streams, rows, width), F32),
             pltpu.VMEM((rows, width), BF),
             pltpu.VMEM((3, rows, local), BF),
@@ -415,6 +477,8 @@
             pltpu.VMEM((rows, units), BF),
             pltpu.VMEM((streams, 8, rows), F32),
             pltpu.VMEM((streams, 8, rows), F32),
+            pltpu.SemaphoreType.DMA((11,) + lm),
+            pltpu.SemaphoreType.DMA((4, 2, layers)),
         ]
         + line_scratch(streams, rows, width),
         compiler_params=pltpu.CompilerParams(
@@ -437,21 +501,139 @@
     return jnp.sum(x.reshape(x.shape[0] // 8, 8, x.shape[1]), axis=0)
 
 
-def backward_kernel(
-    pgrad, slots, xin, proj, probs, mixed, n1, i1, first, slope, active, n2, i2,
-    wqkv, wm, we, ws, gains,
-    g_in, g_attend, g_merge, g_expand, g_shrink, g_vec, g_abias,
-    dr, low, dinner, tmp, dqkv, dsc, dpart, part, sbuf, tbuf, x1, x2, s_sem, t_sem, r1, r2,
-):
+class Plane:
+    def __init__(self, grads, sends, recvs, out, send_sem, recv_sem, credit):
+        dp, self.x = lax.axis_index("dp"), lax.axis_index("rep")
+        self.y, self.c = dp // 2, dp % 2
+        self.partner = {
+            "c": {"dp": dp + 1 - 2 * self.c},
+            "x": {"rep": 1 - self.x},
+            "y": {"dp": (dp + 2) % 4},
+        }
+        self.grads, self.sends, self.recvs, self.out = grads, sends, recvs, out
+        self.send_sem, self.recv_sem, self.credit = send_sem, recv_sem, credit
+        self.block = grads.shape[2] // 8
+
+    def copy(self, u, stage, half):
+        way = ("c", "xy"[half], "yx"[half])[stage]
+        return pltpu.make_async_remote_copy(
+            src_ref=self.sends[stage].at[u, half], dst_ref=self.recvs[stage].at[u, half],
+            send_sem=self.send_sem.at[u, stage, half], recv_sem=self.recv_sem.at[u, stage, half],
+            device_id=self.partner[way], device_id_type=MESH)
+
+    def spots(self, stage, half, own):
+        pick = (lambda v: v) if own else (lambda v: 1 - v)
+        if stage == 0:
+            return [(4 * y + 2 * pick(self.c), 2 * y, 2) for y in (0, 1)]
+        if stage == 1 and half == 0:
+            return [(4 * y + 2 * self.c + pick(self.x), y, 1) for y in (0, 1)]
+        if stage == 1:
+            return [(4 * pick(self.y) + 2 * self.c, 0, 2)]
+        if half == 0:
+            return [(4 * pick(self.y) + 2 * self.c + self.x, 0, 1)]
+        return [(4 * self.y + 2 * self.c + pick(self.x), 0, 1)]
+
+    def parts(self, stage, half, own):
+        for here, there, blocks in self.spots(stage, half, own):
+            for b in range(blocks):
+                start = (here + b) * self.block
+                yield pl.ds(pl.multiple_of(start, 8), self.block), pl.ds((there + b) * self.block, self.block)
+
+    def send(self, u, stage, live, spend):
+        @pl.when(live)
+        def _():
+            for half in (0, 1):
+                for here, there in self.parts(stage, half, False):
+                    self.sends[stage][u, half, there] = self.grads[u, half, here].astype(BF)
+
+            @pl.when(spend)
+            def _():
+                pl.semaphore_wait(self.credit.at[u, stage], 2)
+
+            for half in (0, 1):
+                self.copy(u, stage, half).start()
+
+    def take(self, u, stage, live, give, layer):
+        @pl.when(live)
+        def _():
+            for half in (0, 1):
+                self.copy(u, stage, half).wait()
+                for here, there in self.parts(stage, half, True):
+                    total = self.grads[u, half, here] + self.recvs[stage][u, half, there].astype(F32)
+                    if stage == 2:
+                        self.out[layer, u, half] = total
+                    else:
+                        self.grads[u, half, here] = total
+
+            @pl.when(give)
+            def _():
+                for half in (0, 1):
+                    way = ("c", "xy"[half], "yx"[half])[stage]
+                    pl.semaphore_signal(
+                        self.credit.at[u, stage], inc=1, device_id=self.partner[way], device_id_type=MESH
+                    )
+
+
+def greet_all():
+    z, dp, rep = lax.axis_index("tensor"), lax.axis_index("dp"), lax.axis_index("rep")
+    sem = pltpu.get_barrier_semaphore()
+    others = [{"tensor": (z + d) % 4} for d in (1, 2, 3)]
+    others += [{"rep": 1 - rep, "tensor": (z + d) % 4} for d in (0, 1, 2, 3)]
+    others += [{"dp": dp + 1 - 2 * (dp % 2)}, {"dp": (dp + 2) % 4}]
+    for other in others:
+        pl.semaphore_signal(sem, inc=1, device_id=other, device_id_type=MESH)
+    pl.semaphore_wait(sem, len(others))
+
+
+def backward_kernel(inside, *refs):
+    seed, slots, negs, gains, *rest = refs
+    kept, rest = rest[:11], rest[11:]
+    stored, rest = rest[:4], rest[4:]
+    g_in, vec, out_big, out_small, *rest = rest
+    saved, rest = rest[:11], rest[11:]
+    loaded, rest = rest[:4], rest[4:]
+    g_vec, g_abias, dr, low, dinner, tmp, dqkv, dsc, pgrad, load_sem, *rest = rest
+    line_refs, rest = rest[:9], rest[9:]
+    xin, proj, probs, mixed, n1, i1, first, slope, active, n2, i2 = saved
+    wqkv, wm, we, ws = loaded
+    part = line_refs[0]
     layers, micro, rows, width = xin.shape
     local = wm.shape[1]
+    half_units = we.shape[2] // 2
     heads = local // HEAD_DIM
     streams = micro
     last = 2 * layers * streams
-    greet_line()
-    line = Line(part, sbuf, tbuf, x1, x2, s_sem, t_sem, r1, r2)
+    order = (9, 10, 7, 8, 6, 4, 5, 3, 2, 1, 0)
+
+    def load_saved(k, layer):
+        return pltpu.make_async_copy(kept[k].at[layer], saved[k].at[layer], load_sem.at[k, layer])
+
+    def load_weight(k, layer):
+        return pltpu.make_async_copy(stored[k].at[0, layer], loaded[k].at[layer], load_sem.at[11 + k, layer])
+
+    for layer in reversed(range(layers)):
+        for k in order[:2]:
+            load_saved(k, layer).start()
+        for k in (3, 2):
+            load_weight(k, layer).start()
+        for k in order[2:]:
+            load_saved(k, layer).start()
+        for k in (1, 0):
+            load_weight(k, layer).start()
     g_vec[...] = jnp.zeros_like(g_vec)
     g_abias[...] = jnp.zeros_like(g_abias)
+    vec[...] = jnp.zeros_like(vec)
+    if inside:
+        (g_big, g_small, b1, b2, b3, e1, e2, e3, s1, s2, s3, t1, t2, t3, big_s, big_r, small_s, small_r,
+         big_c, small_c, v_rcv, v_send, v_recv, ask, asked, reply, heard, ask_sem, reply_sem, heard_sem) = rest
+        greet_all()
+        big = Plane(g_big, (b1, b2, b3), (e1, e2, e3), out_big, big_s, big_r, big_c)
+        small = Plane(g_small, (s1, s2, s3), (t1, t2, t3), out_small, small_s, small_r, small_c)
+        contrast_inside(seed, negs, pgrad, vec, ask, asked, reply, heard, ask_sem, reply_sem, heard_sem)
+    else:
+        greet_line()
+        pgrad[...] = seed[...]
+    line = Line(*line_refs)
 
     def serve(i, *which):
         j = jnp.maximum(i - 1, 0)
@@ -462,7 +644,12 @@
             else:
                 line.outward(s, c, slot, live)
 
-    def add_to(ref, s, value):
+    def add_to(large, u, half, layer, s, value):
+        if inside:
+            ref = (g_big if large else g_small).at[u, half]
+        else:
+            ref = (out_big if large else out_small).at[layer, u, half]
+
         @pl.when(s == 0)
         def _():
             ref[...] = value
@@ -470,21 +657,37 @@
         @pl.when(s > 0)
         def _():
             ref[...] += value
+
+    def plane(what, large, stage, live, step):
+        if inside:
+            group = big if large else small
+            for u in (0, 1):
+                if what == "send":
+                    group.send(u, stage, live, step > 0)
+                else:
+                    group.take(u, stage, live, step < layers - 1, layers - 1 - step)
 
     def mlp_back(step, s):
         layer = layers - 1 - step
         i = step * 2 * streams + s
 
+        @pl.when(s == 0)
+        def _():
+            for k in (4, 6, 7, 8, 9, 10):
+                load_saved(k, layer).wait()
+            for k in (2, 3):
+                load_weight(k, layer).wait()
+
         @pl.when(step == 0)
         def _():
-            def seed(c, carry):
+            def begin(c, carry):
                 r = pl.ds(pl.multiple_of(c * TILE, TILE), TILE)
                 pos = (lax.broadcasted_iota(jnp.int32, (TILE, 1), 0) + c * TILE).astype(F32)
                 part[s, r] = jnp.where(pos < pgrad[s, 1:2, 0:1], pgrad[s, 0:1], 0.0)
                 dr[s, r] = jnp.zeros((TILE, width), F32)
                 return carry
 
-            lax.fori_loop(0, rows // TILE, seed, 0)
+            lax.fori_loop(0, rows // TILE, begin, 0)
 
         @pl.when(step > 0)
         def _():
@@ -516,14 +719,32 @@
         part[s] = nt(dinner[...], we[layer])
         line.begin(s)
         serve(i, (1, 2), (2, 0))
-        add_to(g_shrink.at[layer], s, tn(active[layer, s], low[s]))
+        plane("take", True, 2, (step > 0) & (s == 0), step - 1)
+        plane("take", False, 0, (step > 0) & (s == 0), step - 1)
+        plane("send", False, 1, (step > 0) & (s == 0), step - 1)
+        for half in (0, 1):
+            cols = pl.ds(half * half_units, half_units)
+            add_to(True, 0, half, layer, s, tn(low[s], active[layer, s, :, cols]))
         serve(i, (1, 3), (2, 1))
-        add_to(g_expand.at[layer], s, tn(first[layer, s], dinner[...]))
+        for half in (0, 1):
+            cols = pl.ds(half * half_units, half_units)
+            add_to(True, 1, half, layer, s, tn(first[layer, s], dinner[:, cols]))
+        plane("send", True, 0, s == streams - 1, step)
+        plane("take", False, 1, (step > 0) & (s == streams - 1), step - 1)
+        plane("send", False, 2, (step > 0) & (s == streams - 1), step - 1)
         serve(i, (2, 2), (2, 3))
 
     def attention_back(step, s):
         layer = layers - 1 - step
         i = (step * 2 + 1) * streams + s
+
+        @pl.when(s == 0)
+        def _():
+            for k in (0, 1, 2, 3, 5):
+                load_saved(k, layer).wait()
+            for k in (0, 1):
+                load_weight(k, layer).wait()
+
         line.finish(s, 0)
         gain = gains[layer, 0:1].astype(F32)
 
@@ -571,9 +792,15 @@
         part[s] = nt(dsc[0], wqkv[layer, 0]) + nt(dsc[1], wqkv[layer, 1]) + nt(dsc[2], wqkv[layer, 2])
         line.begin(s)
         serve(i, (2, 2), (2, 3))
-        add_to(g_merge.at[layer], s, tn(mixed[layer, s], low[s]))
+        plane("take", True, 0, s == 0, step)
+        plane("send", True, 1, s == 0, step)
+        plane("take", True, 1, s == streams - 1, step)
+        plane("send", True, 2, s == streams - 1, step)
+        plane("take", False, 2, (step > 0) & (s == 0), step - 1)
         for j in range(3):
-            add_to(g_attend.at[layer, j], s, tn(xin[layer, s], dsc[j]))
+            add_to(False, j // 2, j % 2, layer, s, tn(xin[layer, s], dsc[j]))
+        add_to(False, 1, 1, layer, s, tn(low[s], mixed[layer, s]))
+        plane("send", False, 0, s == streams - 1, step)
 
     def layer_step(step, carry):
         def m_step(s, c):
@@ -590,12 +817,44 @@
 
     lax.fori_loop(0, layers, layer_step, 0)
 
+    for layer in range(layers):
+        for k in range(7):
+            vec[layer * 7 + k : layer * 7 + k + 1] = jnp.sum(g_vec[layer, k], axis=0, keepdims=True)
+        for k in range(2):
+            row = layers * 7 + layer * 2 + k
+            vec[row : row + 1, 0:local] = jnp.sum(g_abias[layer, k], axis=0, keepdims=True)
+
+    def vec_copy(stage):
+        return pltpu.make_async_remote_copy(
+            src_ref=vec, dst_ref=v_rcv.at[stage], send_sem=v_send.at[stage], recv_sem=v_recv.at[stage],
+            device_id=big.partner["cxy"[stage]], device_id_type=MESH)
+
+    def vec_take(stage):
+        if inside:
+            vec_copy(stage).wait()
+            vec[...] += v_rcv[stage]
+
+    def vec_send(stage):
+        if inside:
+            vec_copy(stage).start()
+
+    end = layers - 1
+    vec_send(0)
+    serve(last, (1, 0))
+    plane("take", False, 0, True, end)
+    plane("send", False, 1, True, end)
+    vec_take(0)
+    vec_send(1)
+    serve(last, (1, 1))
+    plane("take", True, 2, True, end)
+    serve(last, (1, 2), (2, 0))
+    plane("take", False, 1, True, end)
+    plane("send", False, 2, True, end)
+    vec_take(1)
+    vec_send(2)
+    serve(last, (1, 3), (2, 1), (2, 2), (2, 3))
+
     def tail(s, carry):
-        @pl.when(s == 0)
-        def _():
-            for c in range(CHUNKS):
-                serve(last, (1, c), (2, c))
-
         line.finish(s, 1)
 
         def back(r):
@@ -608,43 +867,140 @@
         return carry
 
     lax.fori_loop(0, streams, tail, 0)
-
-
-def run_backward(pgrad, slots, saved, weights):
+    plane("take", False, 2, True, end)
+    vec_take(2)
+
+
+def run_backward(inside, seed, slots, negatives, saved, weights):
     wqkv, abias, wm, mbias, we, ebias, ws, sbias, gains, shifts = weights
     layers, micro, rows, width = saved[0].shape
     local, units = wm.shape[2], we.shape[3]
-    heads = local // HEAD_DIM
-    shapes = [
-        ((micro, rows, width), BF),
-        ((layers, 3, width, local), F32),
-        ((layers, local, width), F32),
-        ((layers, width, units), F32),
-        ((layers, units, width), F32),
-        ((layers, 7, 8, width), F32),
-        ((layers, 2, 8, local), F32),
+    tall = 8 * ((9 * layers + 2 + 7) // 8)
+    kinds = ((units // 2, "big"), (local, "small"))
+    high = width // 8 if inside else width
+    shapes = [((micro, rows, width), BF), ((tall, width), F32)]
+    shapes += [((layers, 2, 2, high, w), F32) for w, _ in kinds]
+    vm = pl.BlockSpec(memory_space=pltpu.VMEM)
+    hb = pl.BlockSpec(memory_space=pl.ANY)
+    dma = pltpu.SemaphoreType.DMA
+    scratch = [pltpu.VMEM(v.shape, v.dtype) for v in saved]
+    scratch += [pltpu.VMEM(w.shape[1:], BF) for w in (wqkv, wm, we, ws)]
+    scratch += [
+        pltpu.VMEM((layers, 7, 8, width), F32),
+        pltpu.VMEM((layers, 2, 8, local), F32),
+        pltpu.VMEM((micro, rows, width), F32),
+        pltpu.VMEM((micro, rows, width), BF),
+        pltpu.VMEM((rows, units), BF),
+        pltpu.VMEM((rows, units), F32),
+        pltpu.VMEM((3, rows, local), F32),
+        pltpu.VMEM((3, rows, local), BF),
+        pltpu.VMEM((micro, 8, width), F32),
+        dma((15, layers)),
     ]
-    vm = pl.BlockSpec(memory_space=pltpu.VMEM)
+    scratch += line_scratch(micro, rows, width)
+    if inside:
+        scratch += [pltpu.VMEM((2, 2, width, w), F32) for w, _ in kinds]
+        for w, _ in kinds:
+            for _ in range(2):
+                scratch += [pltpu.VMEM((2, 2, width // n, w), BF) for n in (2, 4, 8)]
+        scratch += [dma((2, 3, 2))] * 4
+        scratch += [pltpu.SemaphoreType.REGULAR((2, 3))] * 2
+        scratch += [pltpu.VMEM((3, tall, width), F32), dma((3,)), dma((3,))]
+        scratch += [
+            pltpu.VMEM((16, width), BF),
+            pltpu.VMEM((16, width), BF),
+            pltpu.VMEM((2, 8, width), F32),
+            pltpu.VMEM((8, 8, width), F32),
+            dma((2,)),
+            dma((8,)),
+            dma((8,)),
+        ]
     return pl.pallas_call(
-        backward_kernel,
+        functools.partial(backward_kernel, inside),
         out_shape=[jax.ShapeDtypeStruct(*s) for s in shapes],
-        in_specs=[vm] * 18,
+        in_specs=[vm] * 4 + [hb] * 15,
         out_specs=[vm] * len(shapes),
-        scratch_shapes=[
-            pltpu.VMEM((micro, rows, width), F32),
-            pltpu.VMEM((micro, rows, width), BF),
-            pltpu.VMEM((rows, units), BF),
-            pltpu.VMEM((rows, units), F32),
-            pltpu.VMEM((3, rows, local), F32),
-            pltpu.VMEM((3, rows, local), BF),
-            pltpu.VMEM((8, 128), F32),
-        ]
-        + line_scratch(micro, rows, width),
+        scratch_shapes=scratch,
         compiler_params=pltpu.CompilerParams(
             collective_id=1, has_side_effects=True, vmem_limit_bytes=VMEM_LIMIT
         ),
         name="encoder_backward",
-    )(pgrad, slots, *saved, wqkv[0], wm[0], we[0], ws[0], gains[0])
+    )(seed, slots, negatives, gains[0], *saved, wqkv, wm, we, ws)
+
+
+def contrast_inside(pooled, negs, pgrad, vec, ask, asked, reply, heard, ask_sem, reply_sem, heard_sem):
+    z, rep = lax.axis_index("tensor"), lax.axis_index("rep")
+    micro = pgrad.shape[0]
+    width = negs.shape[1]
+    scales, counts, dirs, key_dirs, positives = [], [], [], [], []
+    ask[...] = jnp.zeros_like(ask)
+    for m in range(micro):
+        count = pooled[micro + m, 1:2]
+        mean_q = pooled[micro + m, 0:1] / count
+        mean_k = pooled[m, 0:1] / pooled[m, 1:2]
+        scale = lax.rsqrt(jnp.sum(mean_q * mean_q, axis=-1, keepdims=True) + UNIT_EPS)
+        key_dir = mean_k * lax.rsqrt(jnp.sum(mean_k * mean_k, axis=-1, keepdims=True) + UNIT_EPS)
+        direction = mean_q * scale
+        ask[m : m + 1] = direction.astype(BF)
+        positives.append(jnp.sum(direction * key_dir, axis=-1, keepdims=True) / SOFTMAX_WARMTH)
+        scales.append(scale)
+        counts.append(count)
+        dirs.append(direction)
+        key_dirs.append(key_dir)
+    question = pltpu.make_async_remote_copy(
+        src_ref=ask, dst_ref=asked, send_sem=ask_sem.at[0], recv_sem=ask_sem.at[1],
+        device_id={"rep": 1 - rep}, device_id_type=MESH)
+    question.start()
+
+    def answer(which, rows_now):
+        logits = nt(rows_now, negs[...]) / SOFTMAX_WARMTH
+        top = jnp.max(logits, axis=-1, keepdims=True)
+        expo = jnp.exp(logits - top)
+        total = jnp.sum(expo, axis=-1, keepdims=True)
+        high = expo.astype(BF)
+        rest = expo - high.astype(F32)
+        mid = rest.astype(BF)
+        tiny = (rest - mid.astype(F32)).astype(BF)
+        keys = nn(high, negs[...]) + nn(mid, negs[...]) + nn(tiny, negs[...])
+        reply[which, 0:micro] = keys[0:micro]
+        reply[which, micro : 2 * micro] = jnp.broadcast_to(top[0:micro], (micro, width))
+        reply[which, 2 * micro : 3 * micro] = jnp.broadcast_to(total[0:micro], (micro, width))
+
+    def tell(which, d):
+        other = {"tensor": (z + d) % 4} if which == 0 else {"rep": 1 - rep, "tensor": (z + d) % 4}
+        k = which * 4 + d
+        return pltpu.make_async_remote_copy(
+            src_ref=reply.at[which], dst_ref=heard.at[k], send_sem=reply_sem.at[k], recv_sem=heard_sem.at[k],
+            device_id=other, device_id_type=MESH)
+
+    answer(0, ask[...])
+    for d in (1, 2, 3):
+        tell(0, d).start()
+    question.wait()
+    answer(1, asked[...])
+    for d in (0, 1, 2, 3):
+        tell(1, d).start()
+    for k in range(1, 8):
+        tell(k // 4, k % 4).wait()
+    everyone = [reply[0]] + [heard[k] for k in range(1, 8)]
+    loss = 0.0
+    for m in range(micro):
+        positive = positives[m]
+        best = positive
+        for one in everyone:
+            best = jnp.maximum(best, one[micro + m : micro + m + 1, 0:1])
+        own = jnp.exp(positive - best)
+        total, keys = own, own * key_dirs[m]
+        for one in everyone:
+            weight = jnp.exp(one[micro + m : micro + m + 1, 0:1] - best)
+            total = total + weight * one[2 * micro + m : 2 * micro + m + 1, 0:1]
+            keys = keys + weight * one[m : m + 1]
+        loss = loss + best + jnp.log(total) - positive
+        dqn = (keys / total - key_dirs[m]) * (CROP_SLOTS / SOFTMAX_WARMTH)
+        mean_grad = scales[m] * (dqn - dirs[m] * jnp.sum(dirs[m] * dqn, axis=-1, keepdims=True))
+        pgrad[m, 0:1] = mean_grad / counts[m]
+        pgrad[m, 1:2] = counts[m]
+    vec[vec.shape[0] - 1 : vec.shape[0]] = jnp.broadcast_to(loss, (1, width))
 
 
 def contrast(mean_q, mean_k, negatives):
@@ -695,32 +1051,40 @@
     acts, pooled, slots, *saved = run_forward(
         query_tokens, query_drop, query_length, key_tokens, key_drop, key_length, weights
     )
-    counts = pooled[:, 1]
-    means = pooled[:, 0] / counts
-    per_query, mean_grad = contrast(means[micro:], means[:micro], negatives)
-    pgrad = jnp.concatenate(
-        [(mean_grad / counts[micro:])[:, None], counts[micro:, None], jnp.zeros((micro, 6, width), F32)], axis=1
-    )
-    g_in, g_attend, g_merge, g_expand, g_shrink, g_vec, g_abias = run_backward(pgrad, slots, saved, weights)
+    layers = expand_weight.shape[1]
+    groups = ("dp", "rep")
+    inside = lax.axis_size("dp") == 4 and lax.axis_size("rep") == 2
+    if inside:
+        g_in, vec, g_big, g_small = run_backward(inside, pooled, slots, negatives, saved, weights)
+        loss = vec[-1, 0]
+    else:
+        counts = pooled[:, 1]
+        means = pooled[:, 0] / counts
+        per_query, mean_grad = contrast(means[micro:], means[:micro], negatives)
+        pgrad = jnp.concatenate(
+            [(mean_grad / counts[micro:])[:, None], counts[micro:, None], jnp.zeros((micro, 6, width), F32)], axis=1
+        )
+        g_in, vec, g_big, g_small = run_backward(inside, pgrad, slots, negatives, saved, weights)
+        g_big = lax.psum_scatter(g_big, groups, scatter_dimension=3, tiled=True)
+        g_small = lax.psum_scatter(g_small, groups, scatter_dimension=3, tiled=True)
+        vec, loss = lax.psum((vec, jnp.sum(per_query)), groups)
     share = rows // lax.axis_size("tensor")
     start = lax.axis_index("tensor") * share
     activations = lax.dynamic_slice_in_dim(acts, start, share, 1)[:, None]
     input_grad = lax.dynamic_slice_in_dim(g_in, start, share, 1)[:, None]
-    groups = ("dp", "rep")
-    attend = jnp.transpose(lax.psum_scatter(g_attend, groups, scatter_dimension=2, tiled=True), (0, 2, 1, 3))
-    merge = lax.psum_scatter(g_merge, groups, scatter_dimension=2, tiled=True)
-    expand = lax.psum_scatter(g_expand, groups, scatter_dimension=1, tiled=True)
-    shrink = lax.psum_scatter(g_shrink, groups, scatter_dimension=2, tiled=True)
-    vec = jnp.sum(g_vec, axis=2)
-    shared, expand_bias_grad, attend_bias_grad, loss = lax.psum(
-        (vec[:, :6], vec[:, 6], jnp.sum(g_abias, axis=2), jnp.sum(per_query)), groups
-    )
+    shrink = jnp.concatenate([g_big[:, 0, 0], g_big[:, 0, 1]], axis=2).transpose(0, 2, 1)
+    expand = jnp.concatenate([g_big[:, 1, 0], g_big[:, 1, 1]], axis=2)
+    attend = jnp.stack([g_small[:, 0, 0], g_small[:, 0, 1], g_small[:, 1, 0]], axis=2)
+    merge = g_small[:, 1, 1].transpose(0, 2, 1)
+    local = attend_weight.shape[4]
+    rows7 = vec[: 7 * layers].reshape(layers, 7, width)
+    attend_bias_grad = vec[7 * layers : 9 * layers, :local].reshape(layers, 2, local)
     size = width // (lax.axis_size("dp") * lax.axis_size("rep"))
-    own = lax.dynamic_slice_in_dim(shared, lax.axis_index(groups) * size, size, 2)
+    own = lax.dynamic_slice_in_dim(rows7, lax.axis_index(groups) * size, size, 2)
     loss = loss / (micro * lax.axis_size("dp") * lax.axis_size("rep"))
     return (
         activations, input_grad, attend, attend_bias_grad, merge, own[:, 5], expand,
-        expand_bias_grad, shrink, own[:, 4], own[:, 0:2], own[:, 2:4], loss,
+        rows7[:, 6], shrink, own[:, 4], own[:, 0:2], own[:, 2:4], loss,
     )
 
 

time: 627 us -> 318 us (0.51)
  waiting for transfers between devices: 200 us -> 0 us
  blocking collectives: 62 us -> 0 us
  local copies, waits for them, and re-layouts: 43.1 us -> 18.3 us
  between operations: 16.5 us -> 2.57 us
    reduce_scatter x2 -> x0, waiting for transfers between devices: 114 us -> none  [the longest x1 58.2 us: per_device(): expand = lax.psum_scatter(g_expand, groups, scatter_dimension=1, tiled=True)]
    unnamed x6 -> x0, waiting for transfers between devices: 85.2 us -> none
    all_gather x2 -> x0, blocking collectives: 35.2 us -> none  [the longest x1 30.9 us: contrast(): pieces = lax.all_gather(packed, ('rep', 'tensor'), axis=0, tiled=False)]
    psum x1 -> x0, blocking collectives: 26.8 us -> none  [per_device(): lax.psum((vec[:, :6], vec[:, 6], jnp.sum(g_abias, axis=2), jnp.sum(per_qu...]
    unnamed x43 -> x24, local copies, waits for them, and re-layouts: 19.7 us -> 10.3 us
    pallas_call x1, Pallas kernels: 176 us -> 167 us  [run_forward(): pl.pallas_call(forward_kernel, out_shape=[jax.ShapeDtypeStruct(*s) for s...]
    pallas_call x2 -> x0, local copies, waits for them, and re-layouts: 9.14 us -> none  [the longest x1 8.21 us: run_backward(): pl.pallas_call(backward_kernel, out_shape=[jax.ShapeDtypeStruct(*s) for s...]
    squeeze x4 -> x2, local copies, waits for them, and re-layouts: 7.57 us -> 1.23 us  [the longest x1 1.19 us: per_device(): g_big[:, 0, 0]]
  transfers between devices with their start and end apart: 4 -> 0, of which waited for: 3 -> 0; matrix products, arithmetic and copies ran while one was open for 3% -> 0% of each run, Pallas kernels for 0% -> 0%
where the time goes in v2:
time: 318 us; the launch traced here: 317 us
  Pallas kernels  295 us (93%)
  local copies, waits for them, and re-layouts  18.3 us (6%)
    pallas_call x1, Pallas kernels, run_forward(): pl.pallas_call(forward_kernel, out_shape=[jax.ShapeDtypeStruct(*s) for s...  167 us
    pallas_call x1, Pallas kernels, run_backward(): pl.pallas_call(functools.partial(backward_kernel, inside), out_shape=[jax...  129 us
    unnamed x24, local copies, waits for them, and re-layouts  10.3 us

profile of v2, /device:TPU:0, one launch (start us, length us, event | category | flops | bytes accessed | tf_op | source)
XLA Modules:
  0.0 317.4 jit_solution(11197897455342221336)
XLA Ops:
  0.6 0.0 copy-start.4
  0.7 0.0 copy-start.5
  0.7 0.0 copy-start.6
  0.7 0.0 copy-start.7
  0.7 0.0 copy-start.8
  0.7 6.3 %copy.39 = bf16[2,2,768,3,192]{4,2,3,1,0:T(8,128)(2,1)} copy(bf16[2,2,768,3,192]{2,4,3,1,0:T(8,128)(2,1)} %param.24) | data formatting | bytes 7077888 | tf_op args[7]
  7.0 0.0 copy-done.4
  7.0 0.6 copy.42.mbias
  7.6 0.0 copy-done.5
  7.6 0.6 copy.43.ebias
  8.3 0.0 copy-done.6
  8.3 0.6 copy.44.sbias
  8.9 0.0 copy-done.7
  8.9 0.6 copy.40.q_len
  9.5 0.0 copy-done.8
  9.5 0.6 copy.41.k_len
  10.2 0.0 copy-start.3
  10.2 166.7 %encoders_forward.1 = (bf16[2,256,768]{2,1,0:T(8,128)(2,1)}, f32[4,8,768]{2,1,0:T(8,128)}, f32[2,8,256]{2,1,0:T(8,128)}, bf16[2,2,256,768]{3,2,1,0:T(8,128)(2,1)...) custom-call(bf16[2,1,256,768]{3,2,1,0:T(8,128)(2,1)} %q_tok.1, ...), custom_call_target="tpu_custom_call" | custom-call | tf_op jit(solution)/shard_map/encoders_forward/pallas_call | solution.py:463
  176.9 0.0 copy-done.3
  176.9 0.6 slice_bitcast_fusion.8.refs_3_
  177.5 128.6 %encoder_backward.1 = (bf16[2,256,768]{2,1,0:T(8,128)(2,1)}, f32[24,768]{1,0:T(8,128)}, f32[2,2,2,96,384]{4,3,2,1,0:T(8,128)}, f32[2,2,2,96,192]{4,3,2,1,0:T(8,128)}) custom-call(f32[4,8,768]{2,1,0:T(8,128)} %get-tuple-element.32.refs_0_, f32[2,8,256]{2,1,0:T(8,128)} %get-tuple-element.33.refs_1_, bf16[1024,768]{1,0:T(8,128)(2,1)} %refs_2_.1, ...), custom_call_target="tpu_custom_call" | custom-call | tf_op jit(solution)/shard_map/encoder_backward/pallas_call | solution.py:918
  306.1 0.0 copy-start
  306.2 1.2 slice_bitcast_fusion
  307.4 0.2 copy-done
  307.6 0.0 copy-start.1
  307.6 1.1 pad_maximum_fusion.1
  308.8 0.2 copy-done.1
  309.0 0.0 copy-start.2
  309.0 0.1 pad_maximum_fusion
  309.1 0.9 copy.49
  309.9 0.8 copy.50
  310.7 1.8 dynamic-slice_bitcast_fusion
  312.5 0.0 copy-done.2
  312.5 0.7 constant_dynamic-slice_fusion.3
  313.2 0.6 constant_dynamic-slice_fusion.1
  313.9 0.6 copy.57
  314.5 0.6 reshape.34
  315.1 0.5 slice.67
  (7 shorter events, 0.1 us)
Async XLA Ops:
  0.6 6.4 %copy-start.4 = (bf16[2,2,768]{2,1,0:T(2,128)(2,1)S(1)}, bf16[2,2,768]{2,1,0:T(2,128)(2,1)}, u32[]{:S(2)}) copy-start(bf16[2,2,768]{2,1,0:T(2,128)(2,1)} %param.27) | copy-start | bytes 18436
  0.7 7.0 %copy-start.5 = (bf16[2,2,768]{2,1,0:T(2,128)(2,1)S(1)}, bf16[2,2,768]{2,1,0:T(2,128)(2,1)}, u32[]{:S(2)}) copy-start(bf16[2,2,768]{2,1,0:T(2,128)(2,1)} %param.29) | copy-start | bytes 18436
  0.7 7.6 %copy-start.6 = (bf16[2,2,768]{2,1,0:T(2,128)(2,1)S(1)}, bf16[2,2,768]{2,1,0:T(2,128)(2,1)}, u32[]{:S(2)}) copy-start(bf16[2,2,768]{2,1,0:T(2,128)(2,1)} %param.31) | copy-start | bytes 18436
  0.7 8.2 %copy-start.7 = (s32[2,1]{0,1:T(1,128)S(1)}, s32[2,1]{0,1:T(1,128)}, u32[]{:S(2)}) copy-start(s32[2,1]{0,1:T(1,128)} %param.19) | copy-start | bytes 28
  0.7 8.8 %copy-start.8 = (s32[2,1]{0,1:T(1,128)S(1)}, s32[2,1]{0,1:T(1,128)}, u32[]{:S(2)}) copy-start(s32[2,1]{0,1:T(1,128)} %param.22) | copy-start | bytes 28
  10.2 166.7 %copy-start.3 = (bf16[2,2,2,768]{3,2,1,0:T(2,128)(2,1)S(1)}, bf16[2,2,2,768]{3,2,1,0:T(2,128)(2,1)}, u32[]{:S(2)}) copy-start(bf16[2,2,2,768]{3,2,1,0:T(2,128)(2,1)} %gains.1) | copy-start | bytes 36868
  306.1 1.4 copy-start
  307.6 1.3 copy-start.1
  309.0 3.5 %copy-start.2 = (f32[24,768]{1,0:T(8,128)S(1)}, f32[24,768]{1,0:T(8,128)}, u32[]{:S(2)}) copy-start(f32[24,768]{1,0:T(8,128)} %get-tuple-element.47) | copy-start | bytes 221188

commit v3 on v2

--- a/solution.py
+++ b/solution.py
@@ -20,7 +20,8 @@
 MESH = pl.DeviceIdType.MESH
 BF = jnp.bfloat16
 F32 = jnp.float32
-CHUNKS = 4
+CHUNKS = 8
+LAG = 3
 TILE = 64
 VMEM_LIMIT = 62 * 1024 * 1024
 
@@ -167,7 +168,7 @@
     kept, rest = rest[:11], rest[11:]
     saved, rest = rest[:11], rest[11:]
     loaded, rest = rest[:4], rest[4:]
-    h, hb, qkv, pb, mx, inner, act, vbias, valid, save_sem, load_sem, *line_refs = rest
+    h, hb, qkv, pb, mx, inner, act, vbias, valid, vecs, save_sem, load_sem, *line_refs = rest
     xin, proj, probs, mixed, n1, i1, first, slope, active, n2, i2 = saved
     part = line_refs[0]
     stored = (wqkv, wm, we, ws)
@@ -191,6 +192,12 @@
     def save(k, layer, m):
         return pltpu.make_async_copy(saved[k].at[layer, m], kept[k].at[layer, m], save_sem.at[k, layer, m])
 
+    for e in range(2):
+        for layer in range(layers):
+            for row, ref in enumerate((mbias, ebias, sbias)):
+                vecs[e, layer, row : row + 1] = ref[e, layer : layer + 1].astype(F32)
+            vecs[e, layer, 3:5] = gains[e, layer].astype(F32)
+            vecs[e, layer, 5:7] = shifts[e, layer].astype(F32)
     greet_line()
     line = Line(*line_refs)
 
@@ -219,38 +226,35 @@
         j = jnp.maximum(i, 0)
         return j % streams, (j // streams) % 2, (i >= 0) & (i < last)
 
-    def serve(i, *which):
-        s1, slot1, live1 = at(i - 1)
-        s2, slot2, live2 = at(i - 2)
-        for kind, c in which:
-            if kind == 1:
-                line.inward(s1, c, slot1, live1)
-            else:
-                line.outward(s2, c, slot2, live2)
+    def tick(i, *which):
+        for c in which:
+            s, slot, live = at(i - 1)
+            line.inward(s, c, slot, live)
+            if c < LAG:
+                s, slot, live = at(i - 2)
+            line.outward(s, (c - LAG) % CHUNKS, slot, live)
 
     def attention_pass(layer, s):
         i = layer * 2 * streams + s
         e, m = 1 - s // micro, s % micro
         is_q = s >= micro
-        serve(i, (1, 0))
+        tick(i, 0)
 
         @pl.when(layer == 0)
         def _():
             @pl.when(s < micro)
             def _():
-                compact(k_tok, k_drop, k_len[m, 0], False, s, m)
+                compact(k_tok, k_drop, k_len[m], False, s, m)
 
             @pl.when(is_q)
             def _():
-                compact(q_tok, q_drop, q_len[m, 0], True, s, m)
+                compact(q_tok, q_drop, q_len[m], True, s, m)
 
         @pl.when(layer > 0)
         def _():
             line.finish(s, 1)
             lp = layer - 1
-            bias = sbias[e, lp].astype(F32)
-            gain = gains[e, lp, 1:2].astype(F32)
-            shift = shifts[e, lp, 1:2].astype(F32)
+            bias, gain, shift = vecs[e, lp, 2:3], vecs[e, lp, 4:5], vecs[e, lp, 6:7]
 
             def norm(r):
                 out, normed, inverse = normalize(h[s, r] + part[s, r] + bias, gain, shift)
@@ -269,7 +273,7 @@
                 for k in (9, 10):
                     save(k, lp, m).start()
 
-        serve(i, (1, 1))
+        tick(i, 1, 2)
 
         @pl.when((layer < layers) & (m == 0))
         def _():
@@ -286,7 +290,7 @@
             rows_now = hb[...]
             for j in range(3):
                 bias = 0.0 if j == 1 else abias[e, layer, j // 2 : j // 2 + 1].astype(F32)
-                qkv[j] = (nn(rows_now, wqkv[e, layer, j]) + bias).astype(BF)
+                qkv[j] = (nt(rows_now, wqkv[e, layer, j]) + bias).astype(BF)
 
             @pl.when(is_q)
             def _():
@@ -294,7 +298,7 @@
                     proj[layer, m, j] = qkv[j]
                 save(1, layer, m).start()
 
-        serve(i, (1, 2), (2, 0))
+        tick(i, 3)
         q_masks = head_masks(local, HEAD_DIM**-0.5)
         v_masks = head_masks(local, 1.0)
 
@@ -318,10 +322,7 @@
 
         for hd in range(heads):
             one_head(hd)
-            if hd == 0:
-                serve(i, (1, 3), (2, 1))
-            elif hd == 1:
-                serve(i, (2, 2))
+            tick(i, 4 + hd)
 
         @pl.when(layer < layers)
         def _():
@@ -336,7 +337,7 @@
             part[s] = nn(mixed_now, wm[e, layer])
             line.begin(s)
 
-        serve(i, (2, 3))
+        tick(i, *range(4 + heads, CHUNKS))
 
         @pl.when(layer == layers)
         def _():
@@ -344,17 +345,17 @@
 
             @pl.when(is_q)
             def _():
-                acts[m] = hb[...]
+                share = rows // lax.axis_size("tensor")
+                start = pl.multiple_of(lax.axis_index("tensor") * share, 16)
+                acts[m] = hb[pl.ds(start, share)]
 
     def forward_pass(layer, s):
         i = (layer * 2 + 1) * streams + s
         e, m = 1 - s // micro, s % micro
         is_q = s >= micro
-        serve(i, (1, 0))
+        tick(i, 0, 1)
         line.finish(s, 0)
-        bias = mbias[e, layer].astype(F32)
-        gain = gains[e, layer, 0:1].astype(F32)
-        shift = shifts[e, layer, 0:1].astype(F32)
+        bias, gain, shift = vecs[e, layer, 0:1], vecs[e, layer, 3:4], vecs[e, layer, 5:6]
 
         def norm(r):
             out, normed, inverse = normalize(h[s, r] + part[s, r] + bias, gain, shift)
@@ -379,10 +380,10 @@
             for k in (4, 5, 6):
                 save(k, layer, m).start()
 
-        serve(i, (1, 1), (2, 0))
+        tick(i, 2, 3)
         inner[...] = nn(hb[...], we[e, layer])
-        serve(i, (1, 2), (2, 1))
-        bias_e = ebias[e, layer].astype(F32)
+        tick(i, 4)
+        bias_e = vecs[e, layer, 1:2]
 
         def gelu(r):
             u = inner[r] + bias_e
@@ -402,10 +403,10 @@
             for k in (7, 8):
                 save(k, layer, m).start()
 
-        serve(i, (1, 3), (2, 2))
+        tick(i, 5, 6)
         part[s] = nn(act[...], ws[e, layer])
         line.begin(s)
-        serve(i, (2, 3))
+        tick(i, 7)
 
     def layer_step(layer, carry):
         def a_step(s, c):
@@ -442,7 +443,7 @@
     streams = 2 * micro
     lm = (layers, micro)
     shapes = [
-        ((micro, rows, width), BF),
+        ((micro, rows // lax.axis_size("tensor"), width), BF),
         ((streams, 8, width), F32),
         ((micro, 8, rows), F32),
         (lm + (rows, width), BF),
@@ -477,6 +478,7 @@
             pltpu.VMEM((rows, units), BF),
             pltpu.VMEM((streams, 8, rows), F32),
             pltpu.VMEM((streams, 8, rows), F32),
+            pltpu.VMEM((2, layers, 8, width), F32),
             pltpu.SemaphoreType.DMA((11,) + lm),
             pltpu.SemaphoreType.DMA((4, 2, layers)),
         ]
@@ -635,14 +637,14 @@
         pgrad[...] = seed[...]
     line = Line(*line_refs)
 
-    def serve(i, *which):
+    def tick(i, *which):
         j = jnp.maximum(i - 1, 0)
         s, slot, live = j % streams, (j // streams) % 2, (i >= 1) & (i <= last)
-        for kind, c in which:
-            if kind == 1:
+        for c in which:
+            if c < CHUNKS:
                 line.inward(s, c, slot, live)
-            else:
-                line.outward(s, c, slot, live)
+            if c >= LAG:
+                line.outward(s, c - LAG, slot, live)
 
     def add_to(large, u, half, layer, s, value):
         if inside:
@@ -693,7 +695,7 @@
         def _():
             line.finish(s, 1)
 
-        gain = gains[layer, 1:2].astype(F32)
+        gain = gains[0, layer, 1:2].astype(F32)
 
         def back(r):
             g = part[s, r] + dr[s, r]
@@ -706,9 +708,9 @@
             g_vec[layer, 4] += fold(out)
 
         tiles(rows, back)
-        serve(i, (1, 0))
+        tick(i, 0)
         tmp[...] = nt(low[s], ws[layer])
-        serve(i, (1, 1))
+        tick(i, 1)
 
         def slopes(r):
             out = tmp[r] * slope[layer, s, r]
@@ -716,23 +718,25 @@
             g_vec[layer, 6] += fold(out)
 
         tiles(rows, slopes)
+        tick(i, 2)
         part[s] = nt(dinner[...], we[layer])
         line.begin(s)
-        serve(i, (1, 2), (2, 0))
+        tick(i, 3)
         plane("take", True, 2, (step > 0) & (s == 0), step - 1)
         plane("take", False, 0, (step > 0) & (s == 0), step - 1)
         plane("send", False, 1, (step > 0) & (s == 0), step - 1)
         for half in (0, 1):
             cols = pl.ds(half * half_units, half_units)
             add_to(True, 0, half, layer, s, tn(low[s], active[layer, s, :, cols]))
-        serve(i, (1, 3), (2, 1))
+            tick(i, 4 + half)
         for half in (0, 1):
             cols = pl.ds(half * half_units, half_units)
             add_to(True, 1, half, layer, s, tn(first[layer, s], dinner[:, cols]))
+            tick(i, 6 + half)
         plane("send", True, 0, s == streams - 1, step)
         plane("take", False, 1, (step > 0) & (s == streams - 1), step - 1)
         plane("send", False, 2, (step > 0) & (s == streams - 1), step - 1)
-        serve(i, (2, 2), (2, 3))
+        tick(i, *range(CHUNKS, CHUNKS + LAG))
 
     def attention_back(step, s):
         layer = layers - 1 - step
@@ -746,7 +750,7 @@
                 load_weight(k, layer).wait()
 
         line.finish(s, 0)
-        gain = gains[layer, 0:1].astype(F32)
+        gain = gains[0, layer, 0:1].astype(F32)
 
         def back(r):
             g = part[s, r] + dr[s, r]
@@ -759,9 +763,9 @@
             g_vec[layer, 5] += fold(out)
 
         tiles(rows, back)
-        serve(i, (1, 0))
+        tick(i, 0)
         dmix = nt(low[s], wm[layer]).astype(BF)
-        serve(i, (1, 1))
+        tick(i, 1)
         masks = head_masks(local, 1.0)
         for hd in range(heads):
             chance_b = probs[layer, s, hd]
@@ -781,17 +785,14 @@
                 dqkv[0] += dq
                 dqkv[1] += dk
                 dqkv[2] += dv
-            if hd == 0:
-                serve(i, (1, 2), (2, 0))
-            elif hd == 1:
-                serve(i, (1, 3), (2, 1))
+            tick(i, 2 + hd)
         g_abias[layer, 0] += fold(dqkv[0])
         g_abias[layer, 1] += fold(dqkv[2])
         for j in range(3):
             dsc[j] = dqkv[j].astype(BF)
-        part[s] = nt(dsc[0], wqkv[layer, 0]) + nt(dsc[1], wqkv[layer, 1]) + nt(dsc[2], wqkv[layer, 2])
+        part[s] = nn(dsc[0], wqkv[layer, 0]) + nn(dsc[1], wqkv[layer, 1]) + nn(dsc[2], wqkv[layer, 2])
         line.begin(s)
-        serve(i, (2, 2), (2, 3))
+        tick(i, *range(2 + heads, 6))
         plane("take", True, 0, s == 0, step)
         plane("send", True, 1, s == 0, step)
         plane("take", True, 1, s == streams - 1, step)
@@ -799,7 +800,9 @@
         plane("take", False, 2, (step > 0) & (s == 0), step - 1)
         for j in range(3):
             add_to(False, j // 2, j % 2, layer, s, tn(xin[layer, s], dsc[j]))
+        tick(i, 6)
         add_to(False, 1, 1, layer, s, tn(low[s], mixed[layer, s]))
+        tick(i, *range(7, CHUNKS + LAG))
         plane("send", False, 0, s == streams - 1, step)
 
     def layer_step(step, carry):
@@ -840,19 +843,19 @@
 
     end = layers - 1
     vec_send(0)
-    serve(last, (1, 0))
+    tick(last, 0, 1)
     plane("take", False, 0, True, end)
     plane("send", False, 1, True, end)
     vec_take(0)
     vec_send(1)
-    serve(last, (1, 1))
+    tick(last, 2, 3, 4)
     plane("take", True, 2, True, end)
-    serve(last, (1, 2), (2, 0))
+    tick(last, 5, 6)
     plane("take", False, 1, True, end)
     plane("send", False, 2, True, end)
     vec_take(1)
     vec_send(2)
-    serve(last, (1, 3), (2, 1), (2, 2), (2, 3))
+    tick(last, *range(7, CHUNKS + LAG))
 
     def tail(s, carry):
         line.finish(s, 1)
@@ -863,7 +866,10 @@
         tiles(rows, back)
         down = lax.broadcasted_iota(jnp.int32, (rows, rows), 0).astype(F32)
         pick = jnp.where(slots[s, 0:1] == down, 1.0, 0.0).astype(BF)
-        g_in[s] = tn(pick, low[s]).astype(BF)
+        low[s] = tn(pick, low[s]).astype(BF)
+        share = rows // lax.axis_size("tensor")
+        start = pl.multiple_of(lax.axis_index("tensor") * share, 16)
+        g_in[s] = low[s, pl.ds(start, share)]
         return carry
 
     lax.fori_loop(0, streams, tail, 0)
@@ -878,7 +884,7 @@
     tall = 8 * ((9 * layers + 2 + 7) // 8)
     kinds = ((units // 2, "big"), (local, "small"))
     high = width // 8 if inside else width
-    shapes = [((micro, rows, width), BF), ((tall, width), F32)]
+    shapes = [((micro, rows // lax.axis_size("tensor"), width), BF), ((tall, width), F32)]
     shapes += [((layers, 2, 2, high, w), F32) for w, _ in kinds]
     vm = pl.BlockSpec(memory_space=pltpu.VMEM)
     hb = pl.BlockSpec(memory_space=pl.ANY)
@@ -925,7 +931,7 @@
             collective_id=1, has_side_effects=True, vmem_limit_bytes=VMEM_LIMIT
         ),
         name="encoder_backward",
-    )(seed, slots, negatives, gains[0], *saved, wqkv, wm, we, ws)
+    )(seed, slots, negatives, gains, *saved, wqkv, wm, we, ws)
 
 
 def contrast_inside(pooled, negs, pgrad, vec, ask, asked, reply, heard, ask_sem, reply_sem, heard_sem):
@@ -1003,6 +1009,64 @@
     vec[vec.shape[0] - 1 : vec.shape[0]] = jnp.broadcast_to(loss, (1, width))
 
 
+def outputs_kernel(layers, size, acts, g_in, vec, big, small, o_acts, o_in, o_attend, o_abias, o_merge, o_mbias,
+                   o_expand, o_ebias, o_shrink, o_sbias, o_gain, o_shift, o_loss):
+    width = vec.shape[1]
+    local = small.shape[4]
+    half = big.shape[4]
+    group = lax.axis_index("dp") * lax.axis_size("rep") + lax.axis_index("rep")
+    blocks = width // size
+    own = pltpu.roll(vec[...], ((blocks - group) % blocks) * size, axis=1)[:, :size]
+    o_acts[:, 0] = acts[...]
+    o_in[:, 0] = g_in[...]
+    for l in range(layers):
+        for h in (0, 1):
+            cols = slice(h * half, (h + 1) * half)
+            o_shrink[l, :, cols] = big[l, 0, h]
+            o_expand[l, :, cols] = big[l, 1, h]
+        for j in range(3):
+            o_attend[l, j] = small[l, j // 2, j % 2]
+        o_merge[l] = small[l, 1, 1].T
+        row = 7 * l
+        o_gain[l] = own[row : row + 2]
+        o_shift[l] = own[row + 2 : row + 4]
+        o_sbias[l : l + 1] = own[row + 4 : row + 5]
+        o_mbias[l : l + 1] = own[row + 5 : row + 6]
+        o_ebias[l : l + 1] = vec[row + 6 : row + 7]
+        o_abias[l] = vec[7 * layers + 2 * l : 7 * layers + 2 * l + 2, :local]
+    o_loss[...] = vec[vec.shape[0] - 1 :, 0:1]
+
+
+def run_outputs(acts, g_in, vec, big, small):
+    micro, share, width = acts.shape
+    layers, _, _, size, half = big.shape
+    local = small.shape[4]
+    shapes = [
+        ((micro, 1, share, width), BF),
+        ((micro, 1, share, width), BF),
+        ((layers, 3, size, local), F32),
+        ((layers, 2, local), F32),
+        ((layers, local, size), F32),
+        ((layers, size), F32),
+        ((layers, size, 2 * half), F32),
+        ((layers, width), F32),
+        ((layers, size, 2 * half), F32),
+        ((layers, size), F32),
+        ((layers, 2, size), F32),
+        ((layers, 2, size), F32),
+        ((1, 1), F32),
+    ]
+    vm = pl.BlockSpec(memory_space=pltpu.VMEM)
+    return pl.pallas_call(
+        functools.partial(outputs_kernel, layers, size),
+        out_shape=[jax.ShapeDtypeStruct(*s) for s in shapes],
+        in_specs=[vm] * 5,
+        out_specs=[vm] * len(shapes),
+        compiler_params=pltpu.CompilerParams(vmem_limit_bytes=VMEM_LIMIT),
+        name="outputs",
+    )(acts, g_in, vec, big, small)
+
+
 def contrast(mean_q, mean_k, negatives):
     key_dir = mean_k * lax.rsqrt(jnp.sum(mean_k * mean_k, axis=-1, keepdims=True) + UNIT_EPS)
     scale = lax.rsqrt(jnp.sum(mean_q * mean_q, axis=-1, keepdims=True) + UNIT_EPS)
@@ -1037,26 +1101,24 @@
 ):
     micro, _, rows, width = query_tokens.shape
     weights = (
-        jnp.transpose(attend_weight, (0, 1, 3, 2, 4)),
+        jnp.transpose(attend_weight, (0, 1, 3, 4, 2)),
         attend_bias,
         merge_weight,
-        merge_bias[:, :, None],
+        merge_bias,
         expand_weight,
-        expand_bias[:, :, None],
+        expand_bias,
         shrink_weight,
-        shrink_bias[:, :, None],
+        shrink_bias,
         norm_gain,
         norm_shift,
     )
     acts, pooled, slots, *saved = run_forward(
-        query_tokens, query_drop, query_length, key_tokens, key_drop, key_length, weights
+        query_tokens, query_drop, query_length.reshape(micro), key_tokens, key_drop, key_length.reshape(micro), weights
     )
-    layers = expand_weight.shape[1]
     groups = ("dp", "rep")
     inside = lax.axis_size("dp") == 4 and lax.axis_size("rep") == 2
     if inside:
         g_in, vec, g_big, g_small = run_backward(inside, pooled, slots, negatives, saved, weights)
-        loss = vec[-1, 0]
     else:
         counts = pooled[:, 1]
         means = pooled[:, 0] / counts
@@ -1067,24 +1129,12 @@
         g_in, vec, g_big, g_small = run_backward(inside, pgrad, slots, negatives, saved, weights)
         g_big = lax.psum_scatter(g_big, groups, scatter_dimension=3, tiled=True)
         g_small = lax.psum_scatter(g_small, groups, scatter_dimension=3, tiled=True)
-        vec, loss = lax.psum((vec, jnp.sum(per_query)), groups)
-    share = rows // lax.axis_size("tensor")
-    start = lax.axis_index("tensor") * share
-    activations = lax.dynamic_slice_in_dim(acts, start, share, 1)[:, None]
-    input_grad = lax.dynamic_slice_in_dim(g_in, start, share, 1)[:, None]
-    shrink = jnp.concatenate([g_big[:, 0, 0], g_big[:, 0, 1]], axis=2).transpose(0, 2, 1)
-    expand = jnp.concatenate([g_big[:, 1, 0], g_big[:, 1, 1]], axis=2)
-    attend = jnp.stack([g_small[:, 0, 0], g_small[:, 0, 1], g_small[:, 1, 0]], axis=2)
-    merge = g_small[:, 1, 1].transpose(0, 2, 1)
-    local = attend_weight.shape[4]
-    rows7 = vec[: 7 * layers].reshape(layers, 7, width)
-    attend_bias_grad = vec[7 * layers : 9 * layers, :local].reshape(layers, 2, local)
-    size = width // (lax.axis_size("dp") * lax.axis_size("rep"))
-    own = lax.dynamic_slice_in_dim(rows7, lax.axis_index(groups) * size, size, 2)
-    loss = loss / (micro * lax.axis_size("dp") * lax.axis_size("rep"))
+        vec = lax.psum(vec.at[-1].add(jnp.sum(per_query)), groups)
+    outs = run_outputs(acts, g_in, vec, g_big, g_small)
+    loss = outs[12].reshape(()) / (micro * lax.axis_size("dp") * lax.axis_size("rep"))
     return (
-        activations, input_grad, attend, attend_bias_grad, merge, own[:, 5], expand,
-        rows7[:, 6], shrink, own[:, 4], own[:, 0:2], own[:, 2:4], loss,
+        outs[0], outs[1], jnp.transpose(outs[2], (0, 2, 1, 3)), *outs[3:8],
+        jnp.transpose(outs[8], (0, 2, 1)), *outs[9:12], loss,
     )
 
 

time: 318 us -> 292 us (0.918)
  local copies, waits for them, and re-layouts: 18.3 us -> 0 us
  Pallas kernels: 295 us -> 289 us
    unnamed x24 -> x0, local copies, waits for them, and re-layouts: 10.3 us -> none
    pallas_call x1, Pallas kernels: 167 us -> 158 us  [run_forward(): pl.pallas_call(forward_kernel, out_shape=[jax.ShapeDtypeStruct(*s) for s...]
    broadcast_in_dim x4 -> x0, local copies, waits for them, and re-layouts: 3.62 us -> none  [the longest x1 1.79 us: per_device(): input_grad = lax.dynamic_slice_in_dim(g_in, start, share, 1)[:, None]]
where the time goes in v3:
time: 292 us; the launch traced here: 291 us
  Pallas kernels  289 us (99%)
    pallas_call x1, Pallas kernels, run_forward(): pl.pallas_call(forward_kernel, out_shape=[jax.ShapeDtypeStruct(*s) for s...  158 us
    pallas_call x1, Pallas kernels, run_backward(): pl.pallas_call(functools.partial(backward_kernel, inside), out_shape=[jax...  128 us

profile of v3, /device:TPU:0, one launch (start us, length us, event | category | flops | bytes accessed | tf_op | source)
XLA Modules:
  0.0 291.4 jit_solution(17211703809411001664)
XLA Ops:
  0.6 157.7 %encoders_forward.1 = (bf16[2,64,768]{2,1,0:T(8,128)(2,1)}, f32[4,8,768]{2,1,0:T(8,128)}, f32[2,8,256]{2,1,0:T(8,128)}, bf16[2,2,256,768]{3,2,1,0:T(8,128)(2,1)}...) custom-call(bf16[2,1,256,768]{3,2,1,0:T(8,128)(2,1)} %q_tok.1, ...), custom_call_target="tpu_custom_call" | custom-call | tf_op jit(solution)/shard_map/encoders_forward/pallas_call | solution.py:464
  158.3 128.2 %encoder_backward.1 = (bf16[2,64,768]{2,1,0:T(8,128)(2,1)}, f32[24,768]{1,0:T(8,128)}, f32[2,2,2,96,384]{4,3,2,1,0:T(8,128)}, f32[2,2,2,96,192]{4,3,2,1,0:T(8,128)}) custom-call(f32[4,8,768]{2,1,0:T(8,128)} %get-tuple-element.45.refs_0_, f32[2,8,256]{2,1,0:T(8,128)} %get-tuple-element.46.refs_1_, bf16[1024,768]{1,0:T(8,128)(2,1)} %refs_2_.1, ...), custom_call_target="tpu_custom_call" | custom-call | tf_op jit(solution)/shard_map/encoder_backward/pallas_call | solution.py:924
  286.5 3.2 %outputs.1 = (bf16[2,1,64,768]{3,2,1,0:T(8,128)(2,1)}, bf16[2,1,64,768]{3,2,1,0:T(8,128)(2,1)}, f32[2,3,96,192]{3,2,1,0:T(8,128)}, f32[2,2,192]{2,1,0:T(2,128)},...) custom-call(bf16[2,64,768]{2,1,0:T(8,128)(2,1)} %get-tuple-element.4, ...), custom_call_target="tpu_custom_call" | custom-call | tf_op jit(solution)/shard_map/outputs/pallas_call | solution.py:1060

commit v4 on v3

--- a/solution.py
+++ b/solution.py
@@ -22,6 +22,7 @@
 F32 = jnp.float32
 CHUNKS = 8
 LAG = 3
+EARLY = 2
 TILE = 64
 VMEM_LIMIT = 62 * 1024 * 1024
 
@@ -59,7 +60,7 @@
         self.size = part.shape[1] // CHUNKS
 
     def rows(self, c):
-        return pl.ds(c * self.size, self.size)
+        return pl.ds(pl.multiple_of(c * self.size, self.size), self.size)
 
     def to_inner(self, s, c):
         return pltpu.make_async_remote_copy(
@@ -105,13 +106,20 @@
             self.tbuf[s, rows] = joint.astype(BF)
             self.to_outer(s, c, slot).start()
 
-    def finish(self, s, slot):
+    def settle(self, s, slot, tile):
+        per = TILE // self.size
+
         @pl.when(self.end)
         def _():
-            for c in range(CHUNKS):
+            for d in range(per):
+                c = tile * per + d
                 rows = self.rows(c)
                 self.to_outer(s, c, slot).wait_recv()
                 self.part[s, rows] = self.part[s, rows] + self.x1[slot, s, rows].astype(F32)
+
+    def release(self, s, slot):
+        @pl.when(self.end)
+        def _():
             for c in range(CHUNKS):
                 self.to_inner(s, c).wait_send()
 
@@ -136,8 +144,10 @@
     ]
 
 
-def tiles(rows, body):
+def tiles(rows, body, ready=None):
     def step(c, carry):
+        if ready is not None:
+            ready(c)
         body(pl.ds(pl.multiple_of(c * TILE, TILE), TILE))
         return carry
 
@@ -252,7 +262,6 @@
 
         @pl.when(layer > 0)
         def _():
-            line.finish(s, 1)
             lp = layer - 1
             bias, gain, shift = vecs[e, lp, 2:3], vecs[e, lp, 4:5], vecs[e, lp, 6:7]
 
@@ -266,7 +275,8 @@
                     n2[lp, m, r] = normed
                     i2[lp, m, r] = jnp.broadcast_to(inverse, (TILE, 128))
 
-            tiles(rows, norm)
+            tiles(rows, norm, lambda t: line.settle(s, 1, t))
+            line.release(s, 1)
 
             @pl.when(is_q)
             def _():
@@ -354,7 +364,6 @@
         e, m = 1 - s // micro, s % micro
         is_q = s >= micro
         tick(i, 0, 1)
-        line.finish(s, 0)
         bias, gain, shift = vecs[e, layer, 0:1], vecs[e, layer, 3:4], vecs[e, layer, 5:6]
 
         def norm(r):
@@ -368,7 +377,8 @@
                 i1[layer, m, r] = jnp.broadcast_to(inverse, (TILE, 128))
                 first[layer, m, r] = out.astype(BF)
 
-        tiles(rows, norm)
+        tiles(rows, norm, lambda t: line.settle(s, 0, t))
+        line.release(s, 0)
 
         @pl.when(m == 0)
         def _():
@@ -637,14 +647,22 @@
         pgrad[...] = seed[...]
     line = Line(*line_refs)
 
+    def at(j):
+        return jnp.maximum(j, 0) % streams, (jnp.maximum(j, 0) // streams) % 2, (j >= 0) & (j < last)
+
     def tick(i, *which):
-        j = jnp.maximum(i - 1, 0)
-        s, slot, live = j % streams, (j // streams) % 2, (i >= 1) & (i <= last)
-        for c in which:
-            if c < CHUNKS:
+        for g in which:
+            s, slot, live = at(i - 1)
+            if g >= 1 and g - 1 < CHUNKS:
+                line.outward(s, g - 1, slot, live)
+            c = g + EARLY
+            if c >= CHUNKS + 1:
+                s, slot, live = at(i)
+                c -= CHUNKS + 1
+                if c < EARLY:
+                    line.inward(s, c, slot, live)
+            elif c < CHUNKS:
                 line.inward(s, c, slot, live)
-            if c >= LAG:
-                line.outward(s, c - LAG, slot, live)
 
     def add_to(large, u, half, layer, s, value):
         if inside:
@@ -690,10 +708,6 @@
                 return carry
 
             lax.fori_loop(0, rows // TILE, begin, 0)
-
-        @pl.when(step > 0)
-        def _():
-            line.finish(s, 1)
 
         gain = gains[0, layer, 1:2].astype(F32)
 
@@ -707,7 +721,17 @@
             g_vec[layer, 3] += fold(g)
             g_vec[layer, 4] += fold(out)
 
-        tiles(rows, back)
+        def ready(t):
+            @pl.when(step > 0)
+            def _():
+                line.settle(s, 1, t)
+
+        tiles(rows, back, ready)
+
+        @pl.when(step > 0)
+        def _():
+            line.release(s, 1)
+
         tick(i, 0)
         tmp[...] = nt(low[s], ws[layer])
         tick(i, 1)
@@ -736,7 +760,7 @@
         plane("send", True, 0, s == streams - 1, step)
         plane("take", False, 1, (step > 0) & (s == streams - 1), step - 1)
         plane("send", False, 2, (step > 0) & (s == streams - 1), step - 1)
-        tick(i, *range(CHUNKS, CHUNKS + LAG))
+        tick(i, CHUNKS)
 
     def attention_back(step, s):
         layer = layers - 1 - step
@@ -749,7 +773,6 @@
             for k in (0, 1):
                 load_weight(k, layer).wait()
 
-        line.finish(s, 0)
         gain = gains[0, layer, 0:1].astype(F32)
 
         def back(r):
@@ -762,7 +785,8 @@
             g_vec[layer, 2] += fold(g)
             g_vec[layer, 5] += fold(out)
 
-        tiles(rows, back)
+        tiles(rows, back, lambda t: line.settle(s, 0, t))
+        line.release(s, 0)
         tick(i, 0)
         dmix = nt(low[s], wm[layer]).astype(BF)
         tick(i, 1)
@@ -802,7 +826,7 @@
             add_to(False, j // 2, j % 2, layer, s, tn(xin[layer, s], dsc[j]))
         tick(i, 6)
         add_to(False, 1, 1, layer, s, tn(low[s], mixed[layer, s]))
-        tick(i, *range(7, CHUNKS + LAG))
+        tick(i, 7, CHUNKS)
         plane("send", False, 0, s == streams - 1, step)
 
     def layer_step(step, carry):
@@ -855,15 +879,14 @@
     plane("send", False, 2, True, end)
     vec_take(1)
     vec_send(2)
-    tick(last, *range(7, CHUNKS + LAG))
+    tick(last, 7, CHUNKS)
 
     def tail(s, carry):
-        line.finish(s, 1)
-
         def back(r):
             low[s, r] = (part[s, r] + dr[s, r]).astype(BF)
 
-        tiles(rows, back)
+        tiles(rows, back, lambda t: line.settle(s, 1, t))
+        line.release(s, 1)
         down = lax.broadcasted_iota(jnp.int32, (rows, rows), 0).astype(F32)
         pick = jnp.where(slots[s, 0:1] == down, 1.0, 0.0).astype(BF)
         low[s] = tn(pick, low[s]).astype(BF)

time: 292 us -> 276 us (0.945)
  Pallas kernels: 289 us -> 273 us
    pallas_call x1, Pallas kernels: 128 us -> 113 us  [run_backward(): pl.pallas_call(functools.partial(backward_kernel, inside), out_shape=[jax...]
where the time goes in v4:
time: 276 us
  Pallas kernels  273 us (99%)
    pallas_call x1, Pallas kernels, run_forward(): pl.pallas_call(forward_kernel, out_shape=[jax.ShapeDtypeStruct(*s) for s...  157 us
    pallas_call x1, Pallas kernels, run_backward(): pl.pallas_call(functools.partial(backward_kernel, inside), out_shape=[jax...  113 us

profile of v4, /device:TPU:0, one launch (start us, length us, event | category | flops | bytes accessed | tf_op | source)
XLA Modules:
  0.0 275.5 jit_solution(10471048117982890556)
XLA Ops:
  0.6 157.0 %encoders_forward.1 = (bf16[2,64,768]{2,1,0:T(8,128)(2,1)}, f32[4,8,768]{2,1,0:T(8,128)}, f32[2,8,256]{2,1,0:T(8,128)}, bf16[2,2,256,768]{3,2,1,0:T(8,128)(2,1)}...) custom-call(bf16[2,1,256,768]{3,2,1,0:T(8,128)(2,1)} %q_tok.1, ...), custom_call_target="tpu_custom_call" | custom-call | tf_op jit(solution)/shard_map/encoders_forward/pallas_call | solution.py:474
  157.7 112.9 %encoder_backward.1 = (bf16[2,64,768]{2,1,0:T(8,128)(2,1)}, f32[24,768]{1,0:T(8,128)}, f32[2,2,2,96,384]{4,3,2,1,0:T(8,128)}, f32[2,2,2,96,192]{4,3,2,1,0:T(8,128)}) custom-call(f32[4,8,768]{2,1,0:T(8,128)} %get-tuple-element.45.refs_0_, f32[2,8,256]{2,1,0:T(8,128)} %get-tuple-element.46.refs_1_, bf16[1024,768]{1,0:T(8,128)(2,1)} %refs_2_.1, ...), custom_call_target="tpu_custom_call" | custom-call | tf_op jit(solution)/shard_map/encoder_backward/pallas_call | solution.py:947
  270.6 3.2 %outputs.1 = (bf16[2,1,64,768]{3,2,1,0:T(8,128)(2,1)}, bf16[2,1,64,768]{3,2,1,0:T(8,128)(2,1)}, f32[2,3,96,192]{3,2,1,0:T(8,128)}, f32[2,2,192]{2,1,0:T(2,128)},...) custom-call(bf16[2,64,768]{2,1,0:T(8,128)(2,1)} %get-tuple-element.4, ...), custom_call_target="tpu_custom_call" | custom-call | tf_op jit(solution)/shard_map/outputs/pallas_call | solution.py:1083

commit v5 on v4

v5 whole, which is shorter than its diff:
```python
import functools

import jax
import jax.numpy as jnp
from jax import lax
from jax.experimental import pallas as pl
from jax.experimental.pallas import tpu as pltpu
from jax.sharding import PartitionSpec as P

HEAD_DIM = 64
CROP_SLOTS = 256
SOFTMAX_WARMTH = 0.05
NORM_EPS = 1e-12
UNIT_EPS = 1e-06
MASKED = -1e30
TOP_PRECISION = lax.Precision.HIGHEST
ROOT_HALF = 0.7071067811865476
INV_ROOT_TAU = 0.3989422804014327

MESH = pl.DeviceIdType.MESH
BF = jnp.bfloat16
F32 = jnp.float32
CHUNKS = 8
LAG = 5
EARLY = 3
TILE = 64
VMEM_LIMIT = 62 * 1024 * 1024


def nn(a, b):
    return jnp.dot(a, b, preferred_element_type=F32)


def nt(a, b):
    return lax.dot_general(a, b, (((1,), (1,)), ((), ())), preferred_element_type=F32)


def tn(a, b):
    return lax.dot_general(a, b, (((0,), (0,)), ((), ())), preferred_element_type=F32)


class Line:
    def __init__(self, part, sbuf, tbuf, x1, x2, s_sem, t_sem, r1, r2):
        z = lax.axis_index("tensor")
        self.mid = (z + 1) // 2 == 1
        self.end = (z + 1) // 2 != 1
        self.lower = z // 2 == 0
        self.inner = 1 + z // 2
        self.outer = 3 * (z // 2)
        self.cross = 3 - z
        self.part, self.sbuf, self.tbuf, self.x1, self.x2 = part, sbuf, tbuf, x1, x2
        self.s_sem, self.t_sem, self.r1, self.r2 = s_sem, t_sem, r1, r2
        self.size = part.shape[1] // CHUNKS

    def rows(self, c):
        return pl.ds(pl.multiple_of(c * self.size, self.size), self.size)

    def near(self, c):
        return (c < CHUNKS // 2) == self.lower

    def outbound(self, c, narrow):
        return (c >= 0) if narrow is False else jnp.logical_not(narrow & self.near(c))

    def homebound(self, c, narrow):
        return (c >= 0) if narrow is False else jnp.logical_not(narrow) | self.near(c)

    def to_inner(self, s, c):
        return pltpu.make_async_remote_copy(
            src_ref=self.sbuf.at[s, self.rows(c)], dst_ref=self.x2.at[s, self.rows(c)],
            send_sem=self.s_sem.at[s, c], recv_sem=self.r2.at[s, c],
            device_id={"tensor": self.inner}, device_id_type=MESH)

    def to_cross(self, s, c, slot):
        return pltpu.make_async_remote_copy(
            src_ref=self.sbuf.at[s, self.rows(c)], dst_ref=self.x1.at[slot, s, self.rows(c)],
            send_sem=self.s_sem.at[s, c], recv_sem=self.r1.at[slot, s, c],
            device_id={"tensor": self.cross}, device_id_type=MESH)

    def to_outer(self, s, c, slot):
        return pltpu.make_async_remote_copy(
            src_ref=self.tbuf.at[s, self.rows(c)], dst_ref=self.x1.at[slot, s, self.rows(c)],
            send_sem=self.t_sem.at[s, c], recv_sem=self.r1.at[slot, s, c],
            device_id={"tensor": self.outer}, device_id_type=MESH)

    def begin(self, s, narrow=False):
        for c in range(CHUNKS):
            @pl.when(self.end & self.outbound(c, narrow))
            def _():
                rows = self.rows(c)
                self.sbuf[s, rows] = self.part[s, rows].astype(BF)
                self.to_inner(s, c).start()

    def inward(self, s, c, slot, live, narrow=False):
        @pl.when(self.mid & live & self.outbound(c, narrow))
        def _():
            rows = self.rows(c)
            self.to_inner(s, c).wait_recv()
            self.sbuf[s, rows] = (self.part[s, rows] + self.x2[s, rows].astype(F32)).astype(BF)
            self.to_cross(s, c, slot).start()

    def outward(self, s, c, slot, live, narrow=False):
        @pl.when(self.mid & live & self.homebound(c, narrow))
        def _():
            rows = self.rows(c)
            self.to_cross(s, c, slot).wait_recv()
            joint = self.part[s, rows] + self.x1[slot, s, rows].astype(F32)
            self.part[s, rows] = joint + self.x2[s, rows].astype(F32)
            self.tbuf[s, rows] = joint.astype(BF)
            self.to_outer(s, c, slot).start()

    def settle(self, s, slot, tile, narrow=False):
        per = TILE // self.size
        for d in range(per):
            c = tile * per + d

            @pl.when(self.end & self.homebound(c, narrow))
            def _():
                rows = self.rows(c)
                self.to_outer(s, c, slot).wait_recv()
                self.part[s, rows] = self.part[s, rows] + self.x1[slot, s, rows].astype(F32)

    def release(self, s, slot, narrow=False):
        for c in range(CHUNKS):
            @pl.when(self.end & self.outbound(c, narrow))
            def _():
                self.to_inner(s, c).wait_send()

            @pl.when(self.mid & self.outbound(c, narrow))
            def _():
                self.to_cross(s, c, slot).wait_send()

            @pl.when(self.mid & self.homebound(c, narrow))
            def _():
                self.to_outer(s, c, slot).wait_send()


def line_scratch(streams, rows, width):
    return [
        pltpu.VMEM((streams, rows, width), F32),
        pltpu.VMEM((streams, rows, width), BF),
        pltpu.VMEM((streams, rows, width), BF),
        pltpu.VMEM((2, streams, rows, width), BF),
        pltpu.VMEM((streams, rows, width), BF),
        pltpu.SemaphoreType.DMA((streams, CHUNKS)),
        pltpu.SemaphoreType.DMA((streams, CHUNKS)),
        pltpu.SemaphoreType.DMA((2, streams, CHUNKS)),
        pltpu.SemaphoreType.DMA((streams, CHUNKS)),
    ]


def tiles(rows, body, ready=None):
    def step(c, carry):
        if ready is not None:
            ready(c)
        body(pl.ds(pl.multiple_of(c * TILE, TILE), TILE))
        return carry

    lax.fori_loop(0, rows // TILE, step, 0)


def normalize(total, gain, shift):
    mean = jnp.mean(total, axis=-1, keepdims=True)
    centered = total - mean
    inverse = lax.rsqrt(jnp.mean(centered * centered, axis=-1, keepdims=True) + NORM_EPS)
    normed = centered * inverse
    return normed * gain + shift, normed, inverse


def head_masks(width, scale):
    lane = lax.broadcasted_iota(jnp.int32, (1, width), 1)
    return [
        jnp.where((lane >= h * HEAD_DIM) & (lane < (h + 1) * HEAD_DIM), scale, 0.0).astype(BF)
        for h in range(width // HEAD_DIM)
    ]


def norm_back(g, normed, inverse, gain):
    scaled = g * gain
    return inverse * (
        scaled
        - jnp.mean(scaled, axis=-1, keepdims=True)
        - normed * jnp.mean(scaled * normed, axis=-1, keepdims=True)
    )


def fold(x):
    return jnp.sum(x.reshape(x.shape[0] // 8, 8, x.shape[1]), axis=0)


class Plane:
    def __init__(self, grads, sends, spots, recvs, out, send_sem, recv_sem, credit):
        dp, self.x = lax.axis_index("dp"), lax.axis_index("rep")
        self.y, self.c = dp // 2, dp % 2
        self.partner = {
            "c": {"dp": dp + 1 - 2 * self.c},
            "x": {"rep": 1 - self.x},
            "y": {"dp": (dp + 2) % 4},
        }
        self.grads, self.sends, self.places, self.recvs, self.out = grads, sends, spots, recvs, out
        self.send_sem, self.recv_sem, self.credit = send_sem, recv_sem, credit
        self.block = grads.shape[2] // 8

    def message(self, u, stage, half, rows):
        if self.places is None:
            return self.sends[stage].at[u, half, rows]
        row, lane = self.places[stage]
        start = half * (self.grads.shape[2] // 2) + row
        return self.sends.at[u, pl.ds(start + rows.start, rows.size), pl.ds(lane, self.grads.shape[3])]

    def copy(self, u, stage, half):
        way = ("c", "xy"[half], "yx"[half])[stage]
        return pltpu.make_async_remote_copy(
            src_ref=self.message(u, stage, half, pl.ds(0, self.recvs[stage].shape[2])), dst_ref=self.recvs[stage].at[u, half],
            send_sem=self.send_sem.at[u, stage, half], recv_sem=self.recv_sem.at[u, stage, half],
            device_id=self.partner[way], device_id_type=MESH)

    def spots(self, stage, half, own):
        pick = (lambda v: v) if own else (lambda v: 1 - v)
        if stage == 0:
            return [(4 * y + 2 * pick(self.c), 2 * y, 2) for y in (0, 1)]
        if stage == 1 and half == 0:
            return [(4 * y + 2 * self.c + pick(self.x), y, 1) for y in (0, 1)]
        if stage == 1:
            return [(4 * pick(self.y) + 2 * self.c, 0, 2)]
        if half == 0:
            return [(4 * pick(self.y) + 2 * self.c + self.x, 0, 1)]
        return [(4 * self.y + 2 * self.c + pick(self.x), 0, 1)]

    def parts(self, stage, half, own):
        for here, there, blocks in self.spots(stage, half, own):
            for b in range(blocks):
                start = (here + b) * self.block
                yield pl.ds(pl.multiple_of(start, 8), self.block), pl.ds((there + b) * self.block, self.block)

    def send(self, u, stage, live, spend):
        @pl.when(live)
        def _():
            for half in (0, 1):
                for here, there in self.parts(stage, half, False):
                    self.message(u, stage, half, there)[...] = self.grads[u, half, here].astype(BF)

            @pl.when(spend)
            def _():
                pl.semaphore_wait(self.credit.at[u, stage], 2)

            for half in (0, 1):
                self.copy(u, stage, half).start()

    def take(self, u, stage, live, give, layer):
        @pl.when(live)
        def _():
            for half in (0, 1):
                self.copy(u, stage, half).wait()
                for here, there in self.parts(stage, half, True):
                    total = self.grads[u, half, here] + self.recvs[stage][u, half, there].astype(F32)
                    if stage == 2:
                        self.out[layer, u, half] = total
                    else:
                        self.grads[u, half, here] = total

            @pl.when(give)
            def _():
                for half in (0, 1):
                    way = ("c", "xy"[half], "yx"[half])[stage]
                    pl.semaphore_signal(
                        self.credit.at[u, stage], inc=1, device_id=self.partner[way], device_id_type=MESH
                    )


def greet(inside):
    z, dp, rep = lax.axis_index("tensor"), lax.axis_index("dp"), lax.axis_index("rep")
    sem = pltpu.get_barrier_semaphore()
    others = [{"tensor": (z + d) % 4} for d in (1, 2, 3)]
    if inside:
        others += [{"rep": 1 - rep, "tensor": (z + d) % 4} for d in (0, 1, 2, 3)]
        others += [{"dp": dp + 1 - 2 * (dp % 2)}, {"dp": (dp + 2) % 4}]
    for other in others:
        pl.semaphore_signal(sem, inc=1, device_id=other, device_id_type=MESH)
    pl.semaphore_wait(sem, len(others))


class Contrast:
    def __init__(self, inside, micro, pooled, keys, pgrad, vec, state, bufs):
        self.inside, self.micro, self.pooled, self.keys = inside, micro, pooled, keys
        self.pgrad, self.vec, self.state = pgrad, vec, state
        self.z, self.rep = lax.axis_index("tensor"), lax.axis_index("rep")
        if inside:
            (self.asks, self.asked, self.reply, self.heard, self.ask_sem, self.reply_sem, self.heard_sem) = bufs
        else:
            (self.source, self.key_sem) = bufs

    def question(self, m):
        return pltpu.make_async_remote_copy(
            src_ref=self.asks.at[m], dst_ref=self.asked.at[m], send_sem=self.ask_sem.at[m, 0],
            recv_sem=self.ask_sem.at[m, 1], device_id={"rep": 1 - self.rep}, device_id_type=MESH)

    def tell(self, m, which, d):
        other = {"tensor": (self.z + d) % 4}
        if which == 1:
            other["rep"] = 1 - self.rep
        k = which * 4 + d
        return pltpu.make_async_remote_copy(
            src_ref=self.reply.at[m, which], dst_ref=self.heard.at[m, k], send_sem=self.reply_sem.at[m, k],
            recv_sem=self.heard_sem.at[m, k], device_id=other, device_id_type=MESH)

    def score(self, rows_now):
        keys = self.keys[...]
        logits = nt(rows_now, keys) / SOFTMAX_WARMTH
        top = jnp.max(logits, axis=-1, keepdims=True)
        expo = jnp.exp(logits - top)
        total = jnp.sum(expo, axis=-1, keepdims=True)
        high = expo.astype(BF)
        rest = expo - high.astype(F32)
        mid = rest.astype(BF)
        tiny = (rest - mid.astype(F32)).astype(BF)
        weighted = nn(high, keys) + nn(mid, keys) + nn(tiny, keys)
        return weighted[0:1], top[0:1], total[0:1]

    def answer(self, m, which, rows_now):
        weighted, top, total = self.score(rows_now)
        width = weighted.shape[1]
        self.reply[m, which, 0:1] = weighted
        self.reply[m, which, 1:2] = jnp.broadcast_to(top, (1, width))
        self.reply[m, which, 2:3] = jnp.broadcast_to(total, (1, width))

    def ask(self, m):
        count = self.pooled[self.micro + m, 1:2]
        mean = self.pooled[self.micro + m, 0:1] / count
        scale = lax.rsqrt(jnp.sum(mean * mean, axis=-1, keepdims=True) + UNIT_EPS)
        direction = mean * scale
        self.state[m, 0:1] = direction
        self.state[m, 1:2] = jnp.broadcast_to(scale, count.shape)
        self.state[m, 2:3] = count
        if self.inside:
            self.asks[m] = jnp.broadcast_to(direction, self.asks.shape[1:]).astype(BF)
            self.question(m).start()
            self.answer(m, 0, self.asks[m])
            for d in (1, 2, 3):
                self.tell(m, 0, d).start()

    def respond(self, m):
        if self.inside:
            self.question(m).wait()
            self.answer(m, 1, self.asked[m])
            for d in (0, 1, 2, 3):
                self.tell(m, 1, d).start()

    def close(self, m, pooled_key):
        direction, scale, count = self.state[m, 0:1], self.state[m, 1:2, 0:1], self.state[m, 2:3]
        mean = pooled_key / self.pooled[m, 1:2]
        key_dir = mean * lax.rsqrt(jnp.sum(mean * mean, axis=-1, keepdims=True) + UNIT_EPS)
        positive = jnp.sum(direction * key_dir, axis=-1, keepdims=True) / SOFTMAX_WARMTH
        if self.inside:
            for k in range(1, 8):
                self.tell(m, k // 4, k % 4).wait()
            everyone = [self.reply[m, 0]] + [self.heard[m, k] for k in range(1, 8)]
            best = positive
            for one in everyone:
                best = jnp.maximum(best, one[1:2, 0:1])
            own = jnp.exp(positive - best)
            total, keys = own, own * key_dir
            for one in everyone:
                weight = jnp.exp(one[1:2, 0:1] - best)
                total = total + weight * one[2:3, 0:1]
                keys = keys + weight * one[0:1]
        else:
            rows_now = jnp.broadcast_to(direction, (16, direction.shape[1])).astype(BF)

            def piece(c, carry):
                best, total, keys = carry
                size = self.keys.shape[0]
                copy = pltpu.make_async_copy(
                    self.source.at[pl.ds(pl.multiple_of(c * size, size), size)], self.keys, self.key_sem)
                copy.start()
                copy.wait()
                weighted, top, part = self.score(rows_now)
                now = jnp.maximum(best, top)
                old, new = jnp.exp(best - now), jnp.exp(top - now)
                return now, total * old + part * new, keys * old + weighted * new

            start = (positive, jnp.ones_like(positive), key_dir)
            best, total, keys = lax.fori_loop(0, self.source.shape[0] // self.keys.shape[0], piece, start)
        loss = best + jnp.log(total) - positive
        last = self.vec.shape[0] - 1
        self.vec[last : last + 1] += jnp.broadcast_to(loss, direction.shape)
        dqn = (keys / total - key_dir) * (CROP_SLOTS / SOFTMAX_WARMTH)
        mean_grad = scale * (dqn - direction * jnp.sum(direction * dqn, axis=-1, keepdims=True))
        self.pgrad[m, 0:1] = mean_grad / count
        self.pgrad[m, 1:2] = count


def step_kernel(inside, *refs):
    q_tok, q_drop, q_len, k_tok, k_drop, k_len, negs, *refs = refs
    wqkv_in, abias, wm_in, mbias, we_in, ebias, ws_in, sbias, gains, shifts, *refs = refs
    acts, g_in, vec, out_big, out_small, *refs = refs
    xin, proj, probs, mixed, n1, first, slope, active, n2, inv, *refs = refs
    wqkv, wm, we, ws, tok, h, hb, qkv, mx, inner, *refs = refs
    vbias, valid, vecs, slots, pooled, state, pgrad, g_vec, g_abias, g_big, g_small, *refs = refs
    load_sem, tok_sem, kpart, kheard, kp_sem, kh_sem, *refs = refs
    line = Line(*refs[:9])
    part, sbuf, tbuf = refs[:3]
    refs = refs[9:]
    stored, loaded = (wqkv_in, wm_in, we_in, ws_in), (wqkv, wm, we, ws)
    micro = q_tok.shape[0]
    rows, width = q_tok.shape[2:]
    layers = we.shape[1]
    local = wm.shape[2]
    half_units = we.shape[3] // 2
    heads = local // HEAD_DIM
    streams = 2 * micro
    third = width // 3
    z = lax.axis_index("tensor")
    share = rows // lax.axis_size("tensor")
    own_rows = pl.ds(pl.multiple_of(z * share, 16), share)

    def load(k, e, layer):
        return pltpu.make_async_copy(stored[k].at[e, layer], loaded[k].at[e, layer], load_sem.at[k, e, layer])

    def load_tokens(s):
        source = k_tok if s < micro else q_tok
        return pltpu.make_async_copy(source.at[s % micro, 0], tok.at[pl.ds(s * rows, rows)], tok_sem.at[s])

    def load_keys():
        return pltpu.make_async_copy(negs, tok, tok_sem.at[streams])

    for layer in range(layers):
        for e in (1, 0):
            for k in (0, 1):
                load(k, e, layer).start()
            if layer == 0:
                for s in range((1 - e) * micro, (2 - e) * micro):
                    load_tokens(s).start()
            for k in (2, 3):
                load(k, e, layer).start()
    vec[...] = jnp.zeros_like(vec)
    g_vec[...] = jnp.zeros_like(g_vec)
    g_abias[...] = jnp.zeros_like(g_abias)
    for e in range(2):
        for layer in range(layers):
            for row, ref in enumerate((mbias, ebias, sbias)):
                vecs[e, layer, row : row + 1] = ref[e, layer : layer + 1].astype(F32)
            vecs[e, layer, 3:5] = gains[e, layer].astype(F32)
            vecs[e, layer, 5:7] = shifts[e, layer].astype(F32)
    greet(inside)

    last_f = 2 * layers * streams

    def at_f(i):
        j = jnp.maximum(i, 0)
        s, stage = j % streams, j // streams
        return s, stage % 2, (i >= 0) & (i < last_f), (stage == 2 * layers - 1) & (s < micro)

    def tick_f(i, *which):
        for c in which:
            s, slot, live, narrow = at_f(i - 1)
            line.inward(s, c, slot, live, narrow)
            if c < LAG:
                s, slot, live, narrow = at_f(i - 2)
            line.outward(s, (c - LAG) % CHUNKS, slot, live, narrow)

    def compact(drop, length, is_q, s, m):
        pos = lax.broadcasted_iota(jnp.int32, (1, rows), 1)
        kept = (pos < length) & ((drop[m] == 0) | (pos == 0))
        kept_f = jnp.broadcast_to(jnp.where(kept, 1.0, 0.0), (16, rows))
        down = lax.broadcasted_iota(jnp.int32, (rows, rows), 0)
        along = lax.broadcasted_iota(jnp.int32, (rows, rows), 1)
        tri = jnp.where(down <= along, 1.0, 0.0).astype(BF)
        order = nn(kept_f.astype(BF), tri)[0:1] - 1.0
        order = jnp.where(kept, order, -1.0)
        count = jnp.sum(kept_f[0:1], axis=-1, keepdims=True)
        pick = jnp.where(order == down.astype(F32), 1.0, 0.0).astype(BF)
        rows_now = nn(pick, tok[pl.ds(pl.multiple_of(s * rows, rows), rows)])
        h[s] = rows_now
        hb[...] = rows_now.astype(BF)
        fits = pos.astype(F32) < count
        vbias[s] = jnp.broadcast_to(jnp.where(fits, 0.0, MASKED), (8, rows))
        if not is_q:
            fits = fits & line.end & ((pos < rows // 2) == line.lower)
        valid[s] = jnp.broadcast_to(jnp.where(fits, 1.0, 0.0), (8, rows))
        pooled[s, 1:2] = jnp.broadcast_to(count, (1, width))
        if is_q:
            slots[m] = jnp.broadcast_to(order, (8, rows))

    def second_norm(lp, e, s, narrow):
        m, is_q = s % micro, s >= micro
        bias, gain, shift = vecs[e, lp, 2:3], vecs[e, lp, 4:5], vecs[e, lp, 6:7]

        def norm(r):
            out, normed, inverse = normalize(h[s, r] + part[s, r] + bias, gain, shift)
            h[s, r] = out
            hb[r] = out.astype(BF)

            @pl.when(is_q)
            def _():
                n2[lp, m, r] = normed.astype(BF)
                inv[lp, m, r, 64:128] = jnp.broadcast_to(inverse, (TILE, 64))

        tiles(rows, norm, lambda t: line.settle(s, 1, t, narrow))
        line.release(s, 1, narrow)

    def attention_pass(layer, s):
        i = layer * 2 * streams + s
        e, m = 1 - s // micro, s % micro
        is_q = s >= micro
        tick_f(i, 0)

        @pl.when(layer == 0)
        def _():
            @pl.when(s < micro)
            def _():
                pltpu.make_async_copy(k_tok.at[m, 0], tok.at[pl.ds(0, rows)], tok_sem.at[s]).wait()
                compact(k_drop, k_len[m], False, s, m)

            @pl.when(is_q)
            def _():
                pltpu.make_async_copy(q_tok.at[m, 0], tok.at[pl.ds(0, rows)], tok_sem.at[s]).wait()
                compact(q_drop, q_len[m], True, s, m)

        @pl.when(layer > 0)
        def _():
            second_norm(layer - 1, e, s, False)

        tick_f(i, 1, 2)

        @pl.when(m == 0)
        def _():
            for k in (0, 1):
                load(k, e, layer).wait()

        @pl.when(is_q)
        def _():
            xin[layer, m] = hb[...]

        rows_now = hb[...]
        for j in range(3):
            bias = 0.0 if j == 1 else abias[e, layer, j // 2 : j // 2 + 1].astype(F32)
            qkv[j] = (nt(rows_now, wqkv[e, layer, j]) + bias).astype(BF)

        @pl.when(is_q)
        def _():
            for j in range(3):
                proj[layer, m, j] = qkv[j]

        tick_f(i, 3)
        q_masks = head_masks(local, HEAD_DIM**-0.5)
        v_masks = head_masks(local, 1.0)
        for hd in range(heads):
            scores = nt(qkv[0] * q_masks[hd], qkv[1]) + vbias[s, 0:1]
            expo = jnp.exp(scores - jnp.max(scores, axis=-1, keepdims=True))
            chance = (expo / jnp.sum(expo, axis=-1, keepdims=True)).astype(BF)

            @pl.when(is_q)
            def _():
                probs[layer, m, hd] = chance

            out = nn(chance, qkv[2] * v_masks[hd])
            if hd == 0:
                mx[...] = out
            else:
                mx[...] += out
            tick_f(i, 4 + hd)
        mixed_now = mx[...].astype(BF)

        @pl.when(is_q)
        def _():
            mixed[layer, m] = mixed_now

        part[s] = nn(mixed_now, wm[e, layer])
        line.begin(s)
        tick_f(i, *range(4 + heads, CHUNKS))

    def forward_pass(layer, s):
        i = (layer * 2 + 1) * streams + s
        e, m = 1 - s // micro, s % micro
        is_q = s >= micro
        tick_f(i, 0, 1)
        bias, gain, shift = vecs[e, layer, 0:1], vecs[e, layer, 3:4], vecs[e, layer, 5:6]

        def norm(r):
            out, normed, inverse = normalize(h[s, r] + part[s, r] + bias, gain, shift)
            h[s, r] = out
            hb[r] = out.astype(BF)

            @pl.when(is_q)
            def _():
                n1[layer, m, r] = normed.astype(BF)
                inv[layer, m, r, 0:64] = jnp.broadcast_to(inverse, (TILE, 64))
                first[layer, m, r] = out.astype(BF)

        tiles(rows, norm, lambda t: line.settle(s, 0, t))
        line.release(s, 0)

        @pl.when(m == 0)
        def _():
            for k in (2, 3):
                load(k, e, layer).wait()

        tick_f(i, 2, 3)
        inner[...] = nn(hb[...], we[e, layer])
        tick_f(i, 4)
        bias_e = vecs[e, layer, 1:2]

        def gelu(r):
            u = inner[r] + bias_e
            phi = 0.5 * (1.0 + lax.erf(u * ROOT_HALF))
            out = (u * phi).astype(BF)
            tbuf[s, r] = out

            @pl.when(is_q)
            def _():
                active[layer, m, r] = out
                slope[layer, m, r] = (phi + u * jnp.exp(-0.5 * u * u) * INV_ROOT_TAU).astype(BF)

        tiles(rows, gelu)
        tick_f(i, 5, 6)
        part[s] = nn(tbuf[s], ws[e, layer])
        line.begin(s, (layer == layers - 1) & (s < micro))
        tick_f(i, 7)

    def layer_step(layer, carry):
        def a_step(s, c):
            attention_pass(layer, s)
            return c

        def f_step(s, c):
            forward_pass(layer, s)
            return c

        lax.fori_loop(0, streams, a_step, 0)
        if inside:
            @pl.when(layer == 0)
            def _():
                load_keys().start()

        lax.fori_loop(0, streams, f_step, 0)
        return carry

    lax.fori_loop(0, layers, layer_step, 0)

    def pool(s):
        return jnp.dot(valid[s], h[s], precision=TOP_PRECISION, preferred_element_type=F32)

    def kshare(m, d):
        return pltpu.make_async_remote_copy(
            src_ref=kpart.at[m], dst_ref=kheard.at[z // 3, m], send_sem=kp_sem.at[m, d - 1],
            recv_sem=kh_sem.at[z // 3, m], device_id={"tensor": (z + d) % 4}, device_id_type=MESH)

    def last_key(m):
        second_norm(layers - 1, 1, m, line.part.shape[0] > 0)
        kpart[m] = pool(m)

        @pl.when(line.end)
        def _():
            for d in (1, 2, 3):
                kshare(m, d).start()

    def last_query(m):
        second_norm(layers - 1, 0, micro + m, False)
        pooled[micro + m, 0:1] = pool(micro + m)[0:1]
        acts[m] = hb[own_rows]

    def pooled_key(m):
        @pl.when(line.end)
        def _():
            for d in (1, 2, 3):
                kshare(m, d).wait_send()

        total = kpart[m, 0:1]
        for e in (0, 1):
            @pl.when(z != 3 * e)
            def _():
                pltpu.make_async_remote_copy(
                    src_ref=kpart.at[m], dst_ref=kheard.at[e, m], send_sem=kp_sem.at[m, 0],
                    recv_sem=kh_sem.at[e, m], device_id={"tensor": 3 - z}, device_id_type=MESH).wait_recv()

            total = total + jnp.where(z != 3 * e, kheard[e, m, 0:1], 0.0)
        return total

    if inside:
        e1, e2, e3, t1, t2, t3, d1, d2, d3, big_s, big_r, small_s, small_r, big_c, small_c, v_rcv, v_send, v_recv, *bufs = refs
        w_big, quarter = half_units, width // 4
        big = Plane(g_big, we.at[1], ((0, 0), (0, w_big), (quarter, w_big)), (e1, e2, e3), out_big, big_s, big_r, big_c)
        small = Plane(g_small, (d1, d2, d3), None, (t1, t2, t3), out_small, small_s, small_r, small_c)
    else:
        g_sem, key_sem = refs
        bufs = (negs, key_sem)
    queue = Contrast(inside, micro, pooled, tok, pgrad, vec, state, bufs)
    tick_f(last_f, 0, 1, 2)
    for m in range(micro):
        last_key(m)
        tick_f(last_f, 3 + m)
    if inside:
        load_keys().wait()
    for m in range(micro):
        if m == micro - 1:
            tick_f(last_f, *range(3 + micro, CHUNKS))
            tick_f(last_f + 1, *range(LAG))
        if m > 0:
            queue.respond(m - 1)
        last_query(m)
        queue.ask(m)

    last_b = 2 * layers * micro
    dinner = tbuf.at[1]
    heads_f = [h.at[0, :, pl.ds(j * third, local)] for j in range(3)]
    heads_b = [tbuf.at[0, :, pl.ds(j * third, local)] for j in range(3)]

    def at_b(i):
        j = jnp.maximum(i, 0)
        return micro + j % micro, (j // micro) % 2, (i >= 0) & (i < last_b)

    def tick(i, *which):
        for g in which:
            s, slot, live = at_b(i - 1)
            if g >= 1 and g - 1 < CHUNKS:
                line.outward(s, g - 1, slot, live)
            c = g + EARLY
            if c >= CHUNKS + 1:
                s, slot, live = at_b(i)
                c -= CHUNKS + 1
                if c < EARLY:
                    line.inward(s, c, slot, live)
            elif c < CHUNKS:
                line.inward(s, c, slot, live)

    def drained(large, layer, u, half):
        source, target = (g_big, out_big) if large else (g_small, out_small)
        return pltpu.make_async_copy(source.at[u, half], target.at[layer, u, half], g_sem.at[0 if large else 1, u, half])

    def add_to(large, u, half, s, value):
        ref = (g_big if large else g_small).at[u, half]

        @pl.when(s == 0)
        def _():
            ref[...] = value

        @pl.when(s > 0)
        def _():
            ref[...] += value

    def plane(what, large, stage, live, step):
        for u in (0, 1):
            if inside:
                group = big if large else small
                if what == "send":
                    group.send(u, stage, live, step > 0)
                else:
                    group.take(u, stage, live, step < layers - 1, layers - 1 - step)
            elif (what, stage) in (("send", 0), ("take", 2)):
                @pl.when(live)
                def _():
                    for half in (0, 1):
                        copy = drained(large, layers - 1 - step, u, half)
                        copy.start() if what == "send" else copy.wait()

    def mlp_back(step, m):
        layer = layers - 1 - step
        i = step * 2 * micro + m
        s = micro + m
        low = sbuf.at[m]

        @pl.when(step == 0)
        def _():
            queue.close(m, pooled_key(m))

            def begin(c, carry):
                r = pl.ds(pl.multiple_of(c * TILE, TILE), TILE)
                pos = (lax.broadcasted_iota(jnp.int32, (TILE, 1), 0) + c * TILE).astype(F32)
                part[s, r] = jnp.where(pos < pgrad[m, 1:2, 0:1], pgrad[m, 0:1], 0.0)
                h[s, r] = jnp.zeros((TILE, width), F32)
                return carry

            lax.fori_loop(0, rows // TILE, begin, 0)

        gain = vecs[0, layer, 4:5]

        def back(r):
            g = part[s, r] + h[s, r]
            normed = n2[layer, m, r].astype(F32)
            out = norm_back(g, normed, inv[layer, m, r][:, 64:65], gain)
            h[s, r] = out
            low[r] = out.astype(BF)
            g_vec[layer, 1] += fold(g * normed)
            g_vec[layer, 3] += fold(g)
            g_vec[layer, 4] += fold(out)

        def ready(t):
            @pl.when(step > 0)
            def _():
                line.settle(s, 1, t)

        tiles(rows, back, ready)

        @pl.when(step > 0)
        def _():
            line.release(s, 1)

        tick(i, 0)
        inner[...] = nt(low[...], ws[0, layer])
        tick(i, 1)

        def slopes(r):
            out = inner[r] * slope[layer, m, r].astype(F32)
            dinner[r] = out.astype(BF)
            g_vec[layer, 6] += fold(out)

        tiles(rows, slopes)
        tick(i, 2)
        part[s] = nt(dinner[...], we[0, layer])
        line.begin(s)
        tick(i, 3)

        @pl.when((step == 0) & (m == 0))
        def _():
            queue.respond(micro - 1)

        plane("take", True, 2, (step > 0) & (m == 0), step - 1)
        plane("take", False, 0, (step > 0) & (m == 0), step - 1)
        plane("send", False, 1, (step > 0) & (m == 0), step - 1)
        for half in (0, 1):
            cols = pl.ds(half * half_units, half_units)
            add_to(True, 0, half, m, tn(low[...], active[layer, m, :, cols]))
            tick(i, 4 + half)
        for half in (0, 1):
            cols = pl.ds(half * half_units, half_units)
            add_to(True, 1, half, m, tn(first[layer, m], dinner[:, cols]))
            tick(i, 6 + half)
        plane("send", True, 0, m == micro - 1, step)
        plane("take", False, 1, (step > 0) & (m == micro - 1), step - 1)
        plane("send", False, 2, (step > 0) & (m == micro - 1), step - 1)
        tick(i, CHUNKS)

    def attention_back(step, m):
        layer = layers - 1 - step
        i = (step * 2 + 1) * micro + m
        s = micro + m
        low = sbuf.at[m]
        gain = vecs[0, layer, 3:4]

        def back(r):
            g = part[s, r] + h[s, r]
            normed = n1[layer, m, r].astype(F32)
            out = norm_back(g, normed, inv[layer, m, r][:, 0:1], gain)
            h[s, r] = out
            low[r] = out.astype(BF)
            g_vec[layer, 0] += fold(g * normed)
            g_vec[layer, 2] += fold(g)
            g_vec[layer, 5] += fold(out)

        tiles(rows, back, lambda t: line.settle(s, 0, t))
        line.release(s, 0)
        tick(i, 0)
        dmix = nt(low[...], wm[0, layer]).astype(BF)
        tick(i, 1)
        masks = head_masks(local, 1.0)
        for hd in range(heads):
            chance_b = probs[layer, m, hd]
            chance = chance_b.astype(F32)
            dm = dmix * masks[hd]
            dch = nt(dm, proj[layer, m, 2])
            ds = chance * (dch - jnp.sum(chance * dch, axis=-1, keepdims=True))
            draw = (ds * HEAD_DIM**-0.5).astype(BF)
            dq = nn(draw, proj[layer, m, 1] * masks[hd])
            dk = tn(draw, proj[layer, m, 0] * masks[hd])
            dv = tn(chance_b, dm)
            for ref, value in zip(heads_f, (dq, dk, dv)):
                if hd == 0:
                    ref[...] = value
                else:
                    ref[...] += value
            tick(i, 2 + hd)
        g_abias[layer, 0] += fold(heads_f[0][...])
        g_abias[layer, 1] += fold(heads_f[2][...])
        for j in range(3):
            heads_b[j][...] = heads_f[j][...].astype(BF)
        part[s] = sum(nn(heads_b[j][...], wqkv[0, layer, j]) for j in range(3))
        line.begin(s)
        tick(i, *range(2 + heads, 6))
        plane("take", True, 0, m == 0, step)
        plane("send", True, 1, m == 0, step)
        plane("take", True, 1, m == micro - 1, step)
        plane("send", True, 2, m == micro - 1, step)
        plane("take", False, 2, (step > 0) & (m == 0), step - 1)
        for j in range(3):
            add_to(False, j // 2, j % 2, m, tn(xin[layer, m], heads_b[j][...]))
        tick(i, 6)
        add_to(False, 1, 1, m, tn(low[...], mixed[layer, m]))
        tick(i, 7, CHUNKS)
        plane("send", False, 0, m == micro - 1, step)

    def back_step(step, carry):
        def m_step(m, c):
            mlp_back(step, m)
            return c

        def a_step(m, c):
            attention_back(step, m)
            return c

        lax.fori_loop(0, micro, m_step, 0)
        lax.fori_loop(0, micro, a_step, 0)
        return carry

    lax.fori_loop(0, layers, back_step, 0)

    for layer in range(layers):
        for k in range(7):
            vec[layer * 7 + k : layer * 7 + k + 1] = jnp.sum(g_vec[layer, k], axis=0, keepdims=True)
        for k in range(2):
            row = layers * 7 + layer * 2 + k
            vec[row : row + 1, 0:local] = jnp.sum(g_abias[layer, k], axis=0, keepdims=True)

    def vec_copy(stage):
        return pltpu.make_async_remote_copy(
            src_ref=vec, dst_ref=v_rcv.at[stage], send_sem=v_send.at[stage], recv_sem=v_recv.at[stage],
            device_id=big.partner["cxy"[stage]], device_id_type=MESH)

    def vec_take(stage):
        if inside:
            vec_copy(stage).wait()
            vec[...] += v_rcv[stage]

    def vec_send(stage):
        if inside:
            vec_copy(stage).start()

    final = layers - 1
    vec_send(0)
    tick(last_b, 0, 1)
    plane("take", False, 0, True, final)
    plane("send", False, 1, True, final)
    vec_take(0)
    vec_send(1)
    tick(last_b, 2, 3, 4)
    plane("take", True, 2, True, final)
    tick(last_b, 5, 6)
    plane("take", False, 1, True, final)
    plane("send", False, 2, True, final)
    vec_take(1)
    vec_send(2)
    tick(last_b, 7, CHUNKS)

    def finish(m, carry):
        s = micro + m
        low = sbuf.at[m]

        def back(r):
            low[r] = (part[s, r] + h[s, r]).astype(BF)

        tiles(rows, back, lambda t: line.settle(s, 1, t))
        line.release(s, 1)
        down = lax.broadcasted_iota(jnp.int32, (rows, rows), 0).astype(F32)
        pick = jnp.where(slots[m, 0:1] == down, 1.0, 0.0).astype(BF)
        low[...] = tn(pick, low[...]).astype(BF)
        g_in[m] = low[own_rows]
        return carry

    lax.fori_loop(0, micro, finish, 0)
    plane("take", False, 2, True, final)
    vec_take(2)


def run_step(inside, tokens, negatives, weights):
    q_tok = tokens[0]
    micro, _, rows, width = q_tok.shape
    wqkv, abias, wm, mbias, we, ebias, ws, sbias, gains, shifts = weights
    layers, local, units = we.shape[1], wm.shape[2], we.shape[3]
    heads = local // HEAD_DIM
    streams = 2 * micro
    share = rows // lax.axis_size("tensor")
    lm = (layers, micro)
    tall = 8 * ((9 * layers + 2 + 7) // 8)
    kinds = (units // 2, local)
    high = width // 8 if inside else width
    shapes = [((micro, share, width), BF), ((micro, share, width), BF), ((tall, width), F32)]
    shapes += [((layers, 2, 2, high, w), F32) for w in kinds]
    vm = pl.BlockSpec(memory_space=pltpu.VMEM)
    hb = pl.BlockSpec(memory_space=pl.ANY)
    sm = pl.BlockSpec(memory_space=pltpu.SMEM)
    dma = pltpu.SemaphoreType.DMA
    v = pltpu.VMEM
    scratch = [
        v(lm + (rows, width), BF),
        v(lm + (3, rows, local), BF),
        v(lm + (heads, rows, rows), BF),
        v(lm + (rows, local), BF),
        v(lm + (rows, width), BF),
        v(lm + (rows, width), BF),
        v(lm + (rows, units), BF),
        v(lm + (rows, units), BF),
        v(lm + (rows, width), BF),
        v(lm + (rows, 128), F32),
    ]
    scratch += [v(w.shape, BF) for w in (wqkv, wm, we, ws)]
    scratch += [
        v((streams * rows, width), BF),
        v((streams, rows, width), F32),
        v((rows, width), BF),
        v((3, rows, local), BF),
        v((rows, local), F32),
        v((rows, units), F32),
        v((streams, 8, rows), F32),
        v((streams, 8, rows), F32),
        v((2, layers, 8, width), F32),
        v((micro, 8, rows), F32),
        v((streams, 8, width), F32),
        v((micro, 8, width), F32),
        v((micro, 8, width), F32),
        v((layers, 7, 8, width), F32),
        v((layers, 2, 8, local), F32),
    ]
    scratch += [v((2, 2, width, w), F32) for w in kinds]
    scratch += [
        dma((4, 2, layers)),
        dma((streams + 1,)),
        v((micro, 8, width), F32),
        v((2, micro, 8, width), F32),
        dma((micro, 3)),
        dma((2, micro)),
    ]
    scratch += line_scratch(streams, rows, width)
    if inside:
        for w in kinds + kinds[1:]:
            scratch += [v((2, 2, width // n, w), BF) for n in (2, 4, 8)]
        scratch += [dma((2, 3, 2))] * 4
        scratch += [pltpu.SemaphoreType.REGULAR((2, 3))] * 2
        scratch += [v((3, tall, width), F32), dma((3,)), dma((3,))]
        scratch += [
            v((micro, 16, width), BF),
            v((micro, 16, width), BF),
            v((micro, 2, 8, width), F32),
            v((micro, 8, 8, width), F32),
            dma((micro, 2)),
            dma((micro, 8)),
            dma((micro, 8)),
        ]
    else:
        scratch += [dma((2, 2, 2)), dma(())]
    return pl.pallas_call(
        functools.partial(step_kernel, inside),
        out_shape=[jax.ShapeDtypeStruct(*s) for s in shapes],
        in_specs=[hb, vm, sm, hb, vm, sm, hb] + [hb, vm, hb, vm, hb, vm, hb, vm, vm, vm],
        out_specs=[vm] * 3 + [vm if inside else hb] * 2,
        scratch_shapes=scratch,
        compiler_params=pltpu.CompilerParams(
            collective_id=0, has_side_effects=True, vmem_limit_bytes=VMEM_LIMIT
        ),
        name="training_step",
    )(*tokens, negatives, *weights)


def outputs_kernel(layers, size, acts, g_in, vec, big, small, o_acts, o_in, o_attend, o_abias, o_merge, o_mbias,
                   o_expand, o_ebias, o_shrink, o_sbias, o_gain, o_shift, o_loss):
    width = vec.shape[1]
    local = small.shape[4]
    half = big.shape[4]
    group = lax.axis_index("dp") * lax.axis_size("rep") + lax.axis_index("rep")
    blocks = width // size
    own = pltpu.roll(vec[...], ((blocks - group) % blocks) * size, axis=1)[:, :size]
    o_acts[:, 0] = acts[...]
    o_in[:, 0] = g_in[...]
    for l in range(layers):
        for h in (0, 1):
            cols = slice(h * half, (h + 1) * half)
            o_shrink[l, :, cols] = big[l, 0, h]
            o_expand[l, :, cols] = big[l, 1, h]
        for j in range(3):
            o_attend[l, j] = small[l, j // 2, j % 2]
        o_merge[l] = small[l, 1, 1].T
        row = 7 * l
        o_gain[l] = own[row : row + 2]
        o_shift[l] = own[row + 2 : row + 4]
        o_sbias[l : l + 1] = own[row + 4 : row + 5]
        o_mbias[l : l + 1] = own[row + 5 : row + 6]
        o_ebias[l : l + 1] = vec[row + 6 : row + 7]
        o_abias[l] = vec[7 * layers + 2 * l : 7 * layers + 2 * l + 2, :local]
    o_loss[...] = vec[vec.shape[0] - 1 :, 0:1]


def run_outputs(acts, g_in, vec, big, small):
    micro, share, width = acts.shape
    layers, _, _, size, half = big.shape
    local = small.shape[4]
    shapes = [
        ((micro, 1, share, width), BF),
        ((micro, 1, share, width), BF),
        ((layers, 3, size, local), F32),
        ((layers, 2, local), F32),
        ((layers, local, size), F32),
        ((layers, size), F32),
        ((layers, size, 2 * half), F32),
        ((layers, width), F32),
        ((layers, size, 2 * half), F32),
        ((layers, size), F32),
        ((layers, 2, size), F32),
        ((layers, 2, size), F32),
        ((1, 1), F32),
    ]
    vm = pl.BlockSpec(memory_space=pltpu.VMEM)
    return pl.pallas_call(
        functools.partial(outputs_kernel, layers, size),
        out_shape=[jax.ShapeDtypeStruct(*s) for s in shapes],
        in_specs=[vm] * 5,
        out_specs=[vm] * len(shapes),
        compiler_params=pltpu.CompilerParams(vmem_limit_bytes=VMEM_LIMIT),
        name="outputs",
    )(acts, g_in, vec, big, small)


def per_device(
    query_tokens, query_drop, query_length, key_tokens, key_drop, key_length, negatives,
    attend_weight, attend_bias, merge_weight, merge_bias, expand_weight, expand_bias,
    shrink_weight, shrink_bias, norm_gain, norm_shift,
):
    micro = query_tokens.shape[0]
    weights = (
        jnp.transpose(attend_weight, (0, 1, 3, 4, 2)),
        attend_bias,
        merge_weight,
        merge_bias,
        expand_weight,
        expand_bias,
        shrink_weight,
        shrink_bias,
        norm_gain,
        norm_shift,
    )
    tokens = (query_tokens, query_drop, query_length.reshape(micro), key_tokens, key_drop, key_length.reshape(micro))
    groups = ("dp", "rep")
    inside = lax.axis_size("dp") == 4 and lax.axis_size("rep") == 2
    if not inside:
        negatives = lax.all_gather(negatives, ("rep", "tensor"), axis=0, tiled=True)
    acts, g_in, vec, g_big, g_small = run_step(inside, tokens, negatives, weights)
    if not inside:
        g_big = lax.psum_scatter(g_big, groups, scatter_dimension=3, tiled=True)
        g_small = lax.psum_scatter(g_small, groups, scatter_dimension=3, tiled=True)
        vec = lax.psum(vec, groups)
    outs = run_outputs(acts, g_in, vec, g_big, g_small)
    loss = outs[12].reshape(()) / (micro * lax.axis_size("dp") * lax.axis_size("rep"))
    return (
        outs[0], outs[1], jnp.transpose(outs[2], (0, 2, 1, 3)), *outs[3:8],
        jnp.transpose(outs[8], (0, 2, 1)), *outs[9:12], loss,
    )


def solution(mesh):
    return jax.shard_map(
        per_device,
        mesh=mesh,
        in_specs=(
            P(None, ("dp", "rep"), None, None),
            P(None, ("dp", "rep"), None),
            P(None, ("dp", "rep")),
            P(None, ("dp", "rep"), None, None),
            P(None, ("dp", "rep"), None),
            P(None, ("dp", "rep")),
            P(("rep", "tensor"), None),
            P(None, None, None, None, "tensor"),
            P(None, None, None, "tensor"),
            P(None, None, "tensor", None),
            P(),
            P(None, None, None, "tensor"),
            P(None, None, "tensor"),
            P(None, None, "tensor", None),
            P(),
            P(),
            P(),
        ),
        out_specs=(
            P(None, ("dp", "rep"), "tensor", None),
            P(None, ("dp", "rep"), "tensor", None),
            P(None, ("dp", "rep"), None, "tensor"),
            P(None, None, "tensor"),
            P(None, "tensor", ("dp", "rep")),
            P(None, ("dp", "rep")),
            P(None, ("dp", "rep"), "tensor"),
            P(None, "tensor"),
            P(None, "tensor", ("dp", "rep")),
            P(None, ("dp", "rep")),
            P(None, None, ("dp", "rep")),
            P(None, None, ("dp", "rep")),
            P(),
        ),
        check_vma=False,
    )
```

time: 276 us -> 264 us (0.957)
  Pallas kernels: 273 us -> 261 us
    pallas_call x2 -> x1, Pallas kernels: 270 us -> 258 us  [run_step(): pl.pallas_call(functools.partial(step_kernel, inside), out_shape=[jax.Sha...]
where the time goes in v5:
time: 264 us
  Pallas kernels  261 us (99%)
    pallas_call x1, Pallas kernels, run_step(): pl.pallas_call(functools.partial(step_kernel, inside), out_shape=[jax.Sha...  258 us

profile of v5, /device:TPU:0, one launch (start us, length us, event | category | flops | bytes accessed | tf_op | source)
XLA Modules:
  0.0 263.9 jit_solution(8070375334922018703)
XLA Ops:
  0.7 258.3 %training_step.1 = (bf16[2,64,768]{2,1,0:T(8,128)(2,1)}, bf16[2,64,768]{2,1,0:T(8,128)(2,1)}, f32[24,768]{1,0:T(8,128)}, f32[2,2,2,96,384]{4,3,2,1,0:T(8,128)}, f32[2,2,2,96,192]{4,3,2,1,0:T(8,128)}) custom-call(bf16[2,1,256,768]{3,2,1,0:T(8,128)(2,1)} %refs_0_.1, s32[2,1,256]{2,1,0:T(1,128)} %refs_1_.1, s32[2]{0:T(128)} %bitcast.7, ...), custom_call_target="tpu_custom_call" | custom-call | tf_op jit(solution)/shard_map/training_step/pallas_call | solution.py:1039
  258.9 3.2 %outputs.1 = (bf16[2,1,64,768]{3,2,1,0:T(8,128)(2,1)}, bf16[2,1,64,768]{3,2,1,0:T(8,128)(2,1)}, f32[2,3,96,192]{3,2,1,0:T(8,128)}, f32[2,2,192]{2,1,0:T(2,128)},...) custom-call(bf16[2,64,768]{2,1,0:T(8,128)(2,1)} %get-tuple-element.3, ...), custom_call_target="tpu_custom_call" | custom-call | tf_op jit(solution)/shard_map/outputs/pallas_call | solution.py:1100

commit v6 on v5

--- a/solution.py
+++ b/solution.py
@@ -313,15 +313,9 @@
         rest = expo - high.astype(F32)
         mid = rest.astype(BF)
         tiny = (rest - mid.astype(F32)).astype(BF)
-        weighted = nn(high, keys) + nn(mid, keys) + nn(tiny, keys)
-        return weighted[0:1], top[0:1], total[0:1]
-
-    def answer(self, m, which, rows_now):
-        weighted, top, total = self.score(rows_now)
-        width = weighted.shape[1]
-        self.reply[m, which, 0:1] = weighted
-        self.reply[m, which, 1:2] = jnp.broadcast_to(top, (1, width))
-        self.reply[m, which, 2:3] = jnp.broadcast_to(total, (1, width))
+        weighted = nn(jnp.concatenate([high, mid, tiny], axis=0), keys)
+        n = rows_now.shape[0]
+        return weighted[:n] + weighted[n : 2 * n] + weighted[2 * n :], top, total
 
     def ask(self, m):
         count = self.pooled[self.micro + m, 1:2]
@@ -334,16 +328,22 @@
         if self.inside:
             self.asks[m] = jnp.broadcast_to(direction, self.asks.shape[1:]).astype(BF)
             self.question(m).start()
-            self.answer(m, 0, self.asks[m])
-            for d in (1, 2, 3):
-                self.tell(m, 0, d).start()
 
     def respond(self, m):
         if self.inside:
             self.question(m).wait()
-            self.answer(m, 1, self.asked[m])
+            half = lax.broadcasted_iota(jnp.int32, self.asks.shape[1:], 0) < 8
+            weighted, top, total = self.score(jnp.where(half, self.asks[m], self.asked[m]))
+            wide = (1, weighted.shape[1])
+            for which in (0, 1):
+                row = slice(8 * which, 8 * which + 1)
+                self.reply[m, which, 0:1] = weighted[row]
+                self.reply[m, which, 1:2] = jnp.broadcast_to(top[row], wide)
+                self.reply[m, which, 2:3] = jnp.broadcast_to(total[row], wide)
             for d in (0, 1, 2, 3):
                 self.tell(m, 1, d).start()
+            for d in (1, 2, 3):
+                self.tell(m, 0, d).start()
 
     def close(self, m, pooled_key):
         direction, scale, count = self.state[m, 0:1], self.state[m, 1:2, 0:1], self.state[m, 2:3]
@@ -373,7 +373,7 @@
                     self.source.at[pl.ds(pl.multiple_of(c * size, size), size)], self.keys, self.key_sem)
                 copy.start()
                 copy.wait()
-                weighted, top, part = self.score(rows_now)
+                weighted, top, part = (v[0:1] for v in self.score(rows_now))
                 now = jnp.maximum(best, top)
                 old, new = jnp.exp(best - now), jnp.exp(top - now)
                 return now, total * old + part * new, keys * old + weighted * new
@@ -443,6 +443,14 @@
             vecs[e, layer, 5:7] = shifts[e, layer].astype(F32)
     greet(inside)
 
+    if inside:
+        turn, e1, e2, e3, t1, t2, t3, d1, d2, d3, big_s, big_r, small_s, small_r, big_c, small_c, v_rcv, v_send, v_recv, *bufs = refs
+        w_big, quarter = half_units, width // 4
+        big = Plane(g_big, we.at[1], ((0, 0), (0, w_big), (quarter, w_big)), (e1, e2, e3), out_big, big_s, big_r, big_c)
+        small = Plane(g_small, (d1, d2, d3), None, (t1, t2, t3), out_small, small_s, small_r, small_c)
+    else:
+        g_sem, key_sem = refs
+        bufs = (negs, key_sem)
     last_f = 2 * layers * streams
 
     def at_f(i):
@@ -559,6 +567,11 @@
             else:
                 mx[...] += out
             tick_f(i, 4 + hd)
+        if inside:
+            @pl.when((i == 1) & (big.c == 0) & line.end)
+            def _():
+                pl.semaphore_signal(turn, inc=1, device_id=big.partner["c"], device_id_type=MESH)
+
         mixed_now = mx[...].astype(BF)
 
         @pl.when(is_q)
@@ -566,6 +579,11 @@
             mixed[layer, m] = mixed_now
 
         part[s] = nn(mixed_now, wm[e, layer])
+        if inside:
+            @pl.when((i == 0) & (big.c == 1) & line.end)
+            def _():
+                pl.semaphore_wait(turn, 1)
+
         line.begin(s)
         tick_f(i, *range(4 + heads, CHUNKS))
 
@@ -676,14 +694,6 @@
             total = total + jnp.where(z != 3 * e, kheard[e, m, 0:1], 0.0)
         return total
 
-    if inside:
-        e1, e2, e3, t1, t2, t3, d1, d2, d3, big_s, big_r, small_s, small_r, big_c, small_c, v_rcv, v_send, v_recv, *bufs = refs
-        w_big, quarter = half_units, width // 4
-        big = Plane(g_big, we.at[1], ((0, 0), (0, w_big), (quarter, w_big)), (e1, e2, e3), out_big, big_s, big_r, big_c)
-        small = Plane(g_small, (d1, d2, d3), None, (t1, t2, t3), out_small, small_s, small_r, small_c)
-    else:
-        g_sem, key_sem = refs
-        bufs = (negs, key_sem)
     queue = Contrast(inside, micro, pooled, tok, pgrad, vec, state, bufs)
     tick_f(last_f, 0, 1, 2)
     for m in range(micro):
@@ -797,6 +807,11 @@
 
         tick(i, 0)
         inner[...] = nt(low[...], ws[0, layer])
+
+        @pl.when((step == 0) & (m == 0))
+        def _():
+            queue.respond(micro - 1)
+
         tick(i, 1)
 
         def slopes(r):
@@ -809,10 +824,6 @@
         part[s] = nt(dinner[...], we[0, layer])
         line.begin(s)
         tick(i, 3)
-
-        @pl.when((step == 0) & (m == 0))
-        def _():
-            queue.respond(micro - 1)
 
         plane("take", True, 2, (step > 0) & (m == 0), step - 1)
         plane("take", False, 0, (step > 0) & (m == 0), step - 1)
@@ -1020,6 +1031,7 @@
     ]
     scratch += line_scratch(streams, rows, width)
     if inside:
+        scratch += [pltpu.SemaphoreType.REGULAR(())]
         for w in kinds + kinds[1:]:
             scratch += [v((2, 2, width // n, w), BF) for n in (2, 4, 8)]
         scratch += [dma((2, 3, 2))] * 4

time: 264 us -> 259 us (0.981)
  Pallas kernels: 261 us -> 256 us
    pallas_call x1, Pallas kernels: 258 us -> 253 us  [run_step(): pl.pallas_call(functools.partial(step_kernel, inside), out_shape=[jax.Sha...]
where the time goes in v6:
time: 259 us
  Pallas kernels  256 us (99%)
    pallas_call x1, Pallas kernels, run_step(): pl.pallas_call(functools.partial(step_kernel, inside), out_shape=[jax.Sha...  253 us

profile of v6, /device:TPU:0, one launch (start us, length us, event | category | flops | bytes accessed | tf_op | source)
XLA Modules:
  0.0 258.7 jit_solution(14302396159165876871)
XLA Ops:
  0.7 253.1 %training_step.1 = (bf16[2,64,768]{2,1,0:T(8,128)(2,1)}, bf16[2,64,768]{2,1,0:T(8,128)(2,1)}, f32[24,768]{1,0:T(8,128)}, f32[2,2,2,96,384]{4,3,2,1,0:T(8,128)}, f32[2,2,2,96,192]{4,3,2,1,0:T(8,128)}) custom-call(bf16[2,1,256,768]{3,2,1,0:T(8,128)(2,1)} %refs_0_.1, s32[2,1,256]{2,1,0:T(1,128)} %refs_1_.1, s32[2]{0:T(128)} %bitcast.7, ...), custom_call_target="tpu_custom_call" | custom-call | tf_op jit(solution)/shard_map/training_step/pallas_call | solution.py:1051
  253.8 3.2 %outputs.1 = (bf16[2,1,64,768]{3,2,1,0:T(8,128)(2,1)}, bf16[2,1,64,768]{3,2,1,0:T(8,128)(2,1)}, f32[2,3,96,192]{3,2,1,0:T(8,128)}, f32[2,2,192]{2,1,0:T(2,128)},...) custom-call(bf16[2,64,768]{2,1,0:T(8,128)(2,1)} %get-tuple-element.3, ...), custom_call_target="tpu_custom_call" | custom-call | tf_op jit(solution)/shard_map/outputs/pallas_call | solution.py:1112

commit v7 on v6

--- a/solution.py
+++ b/solution.py
@@ -82,8 +82,8 @@
             send_sem=self.t_sem.at[s, c], recv_sem=self.r1.at[slot, s, c],
             device_id={"tensor": self.outer}, device_id_type=MESH)
 
-    def begin(self, s, narrow=False):
-        for c in range(CHUNKS):
+    def begin(self, s, narrow=False, chunks=range(CHUNKS)):
+        for c in chunks:
             @pl.when(self.end & self.outbound(c, narrow))
             def _():
                 rows = self.rows(c)
@@ -120,11 +120,17 @@
                 self.part[s, rows] = self.part[s, rows] + self.x1[slot, s, rows].astype(F32)
 
     def release(self, s, slot, narrow=False):
+        self.release_end(s, narrow)
+        self.release_mid(s, slot, narrow)
+
+    def release_end(self, s, narrow=False):
         for c in range(CHUNKS):
             @pl.when(self.end & self.outbound(c, narrow))
             def _():
                 self.to_inner(s, c).wait_send()
 
+    def release_mid(self, s, slot, narrow=False):
+        for c in range(CHUNKS):
             @pl.when(self.mid & self.outbound(c, narrow))
             def _():
                 self.to_cross(s, c, slot).wait_send()
@@ -148,14 +154,14 @@
     ]
 
 
-def tiles(rows, body, ready=None):
+def tiles(rows, body, ready=None, first=0):
     def step(c, carry):
         if ready is not None:
             ready(c)
         body(pl.ds(pl.multiple_of(c * TILE, TILE), TILE))
         return carry
 
-    lax.fori_loop(0, rows // TILE, step, 0)
+    lax.fori_loop(first // TILE, rows // TILE, step, 0)
 
 
 def normalize(total, gain, shift):
@@ -199,6 +205,7 @@
         self.grads, self.sends, self.places, self.recvs, self.out = grads, sends, spots, recvs, out
         self.send_sem, self.recv_sem, self.credit = send_sem, recv_sem, credit
         self.block = grads.shape[2] // 8
+        self.wide = len(out.shape) == 4
 
     def message(self, u, stage, half, rows):
         if self.places is None:
@@ -253,7 +260,10 @@
                 self.copy(u, stage, half).wait()
                 for here, there in self.parts(stage, half, True):
                     total = self.grads[u, half, here] + self.recvs[stage][u, half, there].astype(F32)
-                    if stage == 2:
+                    if stage == 2 and self.wide:
+                        cols = self.grads.shape[3]
+                        self.out[layer, u, :, half * cols : (half + 1) * cols] = total
+                    elif stage == 2:
                         self.out[layer, u, half] = total
                     else:
                         self.grads[u, half, here] = total
@@ -267,7 +277,7 @@
                     )
 
 
-def greet(inside):
+def greet(inside, ahead):
     z, dp, rep = lax.axis_index("tensor"), lax.axis_index("dp"), lax.axis_index("rep")
     sem = pltpu.get_barrier_semaphore()
     others = [{"tensor": (z + d) % 4} for d in (1, 2, 3)]
@@ -276,6 +286,7 @@
         others += [{"dp": dp + 1 - 2 * (dp % 2)}, {"dp": (dp + 2) % 4}]
     for other in others:
         pl.semaphore_signal(sem, inc=1, device_id=other, device_id_type=MESH)
+    ahead()
     pl.semaphore_wait(sem, len(others))
 
 
@@ -423,49 +434,6 @@
     def load_keys():
         return pltpu.make_async_copy(negs, tok, tok_sem.at[streams])
 
-    for layer in range(layers):
-        for e in (1, 0):
-            for k in (0, 1):
-                load(k, e, layer).start()
-            if layer == 0:
-                for s in range((1 - e) * micro, (2 - e) * micro):
-                    load_tokens(s).start()
-            for k in (2, 3):
-                load(k, e, layer).start()
-    vec[...] = jnp.zeros_like(vec)
-    g_vec[...] = jnp.zeros_like(g_vec)
-    g_abias[...] = jnp.zeros_like(g_abias)
-    for e in range(2):
-        for layer in range(layers):
-            for row, ref in enumerate((mbias, ebias, sbias)):
-                vecs[e, layer, row : row + 1] = ref[e, layer : layer + 1].astype(F32)
-            vecs[e, layer, 3:5] = gains[e, layer].astype(F32)
-            vecs[e, layer, 5:7] = shifts[e, layer].astype(F32)
-    greet(inside)
-
-    if inside:
-        turn, e1, e2, e3, t1, t2, t3, d1, d2, d3, big_s, big_r, small_s, small_r, big_c, small_c, v_rcv, v_send, v_recv, *bufs = refs
-        w_big, quarter = half_units, width // 4
-        big = Plane(g_big, we.at[1], ((0, 0), (0, w_big), (quarter, w_big)), (e1, e2, e3), out_big, big_s, big_r, big_c)
-        small = Plane(g_small, (d1, d2, d3), None, (t1, t2, t3), out_small, small_s, small_r, small_c)
-    else:
-        g_sem, key_sem = refs
-        bufs = (negs, key_sem)
-    last_f = 2 * layers * streams
-
-    def at_f(i):
-        j = jnp.maximum(i, 0)
-        s, stage = j % streams, j // streams
-        return s, stage % 2, (i >= 0) & (i < last_f), (stage == 2 * layers - 1) & (s < micro)
-
-    def tick_f(i, *which):
-        for c in which:
-            s, slot, live, narrow = at_f(i - 1)
-            line.inward(s, c, slot, live, narrow)
-            if c < LAG:
-                s, slot, live, narrow = at_f(i - 2)
-            line.outward(s, (c - LAG) % CHUNKS, slot, live, narrow)
-
     def compact(drop, length, is_q, s, m):
         pos = lax.broadcasted_iota(jnp.int32, (1, rows), 1)
         kept = (pos < length) & ((drop[m] == 0) | (pos == 0))
@@ -477,7 +445,7 @@
         order = jnp.where(kept, order, -1.0)
         count = jnp.sum(kept_f[0:1], axis=-1, keepdims=True)
         pick = jnp.where(order == down.astype(F32), 1.0, 0.0).astype(BF)
-        rows_now = nn(pick, tok[pl.ds(pl.multiple_of(s * rows, rows), rows)])
+        rows_now = nn(pick, tok[pl.ds(s * rows if isinstance(s, int) else pl.multiple_of(s * rows, rows), rows)])
         h[s] = rows_now
         hb[...] = rows_now.astype(BF)
         fits = pos.astype(F32) < count
@@ -489,6 +457,53 @@
         if is_q:
             slots[m] = jnp.broadcast_to(order, (8, rows))
 
+    def prepare():
+        for layer in range(layers):
+            for e in (1, 0):
+                for k in (0, 1):
+                    load(k, e, layer).start()
+                if layer == 0:
+                    for s in range((1 - e) * micro, (2 - e) * micro):
+                        load_tokens(s).start()
+                for k in (2, 3):
+                    load(k, e, layer).start()
+        vec[...] = jnp.zeros_like(vec)
+        g_vec[...] = jnp.zeros_like(g_vec)
+        g_abias[...] = jnp.zeros_like(g_abias)
+        for e in range(2):
+            for layer in range(layers):
+                for row, ref in enumerate((mbias, ebias, sbias)):
+                    vecs[e, layer, row : row + 1] = ref[e, layer : layer + 1].astype(F32)
+                vecs[e, layer, 3:5] = gains[e, layer].astype(F32)
+                vecs[e, layer, 5:7] = shifts[e, layer].astype(F32)
+        load_tokens(0).wait()
+        compact(k_drop, k_len[0], False, 0, 0)
+
+    greet(inside, prepare)
+
+    if inside:
+        turn, red_big, red_small, red_sem, e1, e2, e3, t1, t2, t3, d1, d2, d3, big_s, big_r, small_s, small_r, big_c, small_c, v_rcv, v_send, v_recv, *bufs = refs
+        w_big, quarter = half_units, width // 4
+        big = Plane(g_big, we.at[1], ((0, 0), (0, w_big), (quarter, w_big)), (e1, e2, e3), red_big, big_s, big_r, big_c)
+        small = Plane(g_small, (d1, d2, d3), None, (t1, t2, t3), red_small, small_s, small_r, small_c)
+    else:
+        g_sem, key_sem = refs
+        bufs = (negs, key_sem)
+    last_f = 2 * layers * streams
+
+    def at_f(i):
+        j = jnp.maximum(i, 0)
+        s, stage = j % streams, j // streams
+        return s, stage % 2, (i >= 0) & (i < last_f), (stage == 2 * layers - 1) & (s < micro)
+
+    def tick_f(i, *which):
+        for c in which:
+            s, slot, live, narrow = at_f(i - 1)
+            line.inward(s, c, slot, live, narrow)
+            if c < LAG:
+                s, slot, live, narrow = at_f(i - 2)
+            line.outward(s, (c - LAG) % CHUNKS, slot, live, narrow)
+
     def second_norm(lp, e, s, narrow):
         m, is_q = s % micro, s >= micro
         bias, gain, shift = vecs[e, lp, 2:3], vecs[e, lp, 4:5], vecs[e, lp, 6:7]
@@ -514,7 +529,7 @@
 
         @pl.when(layer == 0)
         def _():
-            @pl.when(s < micro)
+            @pl.when((s > 0) & (s < micro))
             def _():
                 pltpu.make_async_copy(k_tok.at[m, 0], tok.at[pl.ds(0, rows)], tok_sem.at[s]).wait()
                 compact(k_drop, k_len[m], False, s, m)
@@ -748,6 +763,10 @@
         def _():
             ref[...] += value
 
+    def leave(large, layer):
+        source, target = (red_big, out_big) if large else (red_small, out_small)
+        return pltpu.make_async_copy(source.at[layer], target.at[layer], red_sem.at[0 if large else 1, layer])
+
     def plane(what, large, stage, live, step):
         for u in (0, 1):
             if inside:
@@ -762,6 +781,10 @@
                     for half in (0, 1):
                         copy = drained(large, layers - 1 - step, u, half)
                         copy.start() if what == "send" else copy.wait()
+        if inside and (what, stage) == ("take", 2):
+            @pl.when(live)
+            def _():
+                leave(large, layers - 1 - step).start()
 
     def mlp_back(step, m):
         layer = layers - 1 - step
@@ -799,35 +822,38 @@
             def _():
                 line.settle(s, 1, t)
 
-        tiles(rows, back, ready)
-
-        @pl.when(step > 0)
-        def _():
-            line.release(s, 1)
-
-        tick(i, 0)
-        inner[...] = nt(low[...], ws[0, layer])
-
-        @pl.when((step == 0) & (m == 0))
-        def _():
-            queue.respond(micro - 1)
-
-        tick(i, 1)
-
         def slopes(r):
             out = inner[r] * slope[layer, m, r].astype(F32)
             dinner[r] = out.astype(BF)
             g_vec[layer, 6] += fold(out)
 
-        tiles(rows, slopes)
-        tick(i, 2)
-        part[s] = nt(dinner[...], we[0, layer])
-        line.begin(s)
-        tick(i, 3)
+        for half in (0, 1):
+            first_row, last_row = half * rows // 2, (half + 1) * rows // 2
+            span = pl.ds(first_row, rows // 2)
+            tiles(last_row, back, ready, first_row)
+            if half == 0:
+                @pl.when(step > 0)
+                def _():
+                    line.release_end(s)
+
+            tick(i, 2 * half)
+            inner[span] = nt(low[span], ws[0, layer])
+
+            if half == 1:
+                @pl.when((step == 0) & (m == 0))
+                def _():
+                    queue.respond(micro - 1)
+
+            tick(i, 2 * half + 1)
+            tiles(last_row, slopes, None, first_row)
+            part[s, span] = nt(dinner[span], we[0, layer])
+            line.begin(s, False, range(half * CHUNKS // 2, (half + 1) * CHUNKS // 2))
+
+        @pl.when(step > 0)
+        def _():
+            line.release_mid(s, 1)
 
         plane("take", True, 2, (step > 0) & (m == 0), step - 1)
-        plane("take", False, 0, (step > 0) & (m == 0), step - 1)
-        plane("send", False, 1, (step > 0) & (m == 0), step - 1)
         for half in (0, 1):
             cols = pl.ds(half * half_units, half_units)
             add_to(True, 0, half, m, tn(low[...], active[layer, m, :, cols]))
@@ -836,6 +862,8 @@
             cols = pl.ds(half * half_units, half_units)
             add_to(True, 1, half, m, tn(first[layer, m], dinner[:, cols]))
             tick(i, 6 + half)
+        plane("take", False, 0, (step > 0) & (m == 0), step - 1)
+        plane("send", False, 1, (step > 0) & (m == 0), step - 1)
         plane("send", True, 0, m == micro - 1, step)
         plane("take", False, 1, (step > 0) & (m == micro - 1), step - 1)
         plane("send", False, 2, (step > 0) & (m == micro - 1), step - 1)
@@ -884,8 +912,10 @@
         g_abias[layer, 1] += fold(heads_f[2][...])
         for j in range(3):
             heads_b[j][...] = heads_f[j][...].astype(BF)
-        part[s] = sum(nn(heads_b[j][...], wqkv[0, layer, j]) for j in range(3))
-        line.begin(s)
+        for half in (0, 1):
+            span = pl.ds(half * rows // 2, rows // 2)
+            part[s, span] = sum(nn(tbuf[0, span, j * third : j * third + local], wqkv[0, layer, j]) for j in range(3))
+            line.begin(s, False, range(half * CHUNKS // 2, (half + 1) * CHUNKS // 2))
         tick(i, *range(2 + heads, 6))
         plane("take", True, 0, m == 0, step)
         plane("send", True, 1, m == 0, step)
@@ -966,9 +996,13 @@
         g_in[m] = low[own_rows]
         return carry
 
-    lax.fori_loop(0, micro, finish, 0)
     plane("take", False, 2, True, final)
     vec_take(2)
+    lax.fori_loop(0, micro, finish, 0)
+    if inside:
+        for layer in range(layers):
+            leave(True, layer).wait()
+            leave(False, layer).wait()
 
 
 def run_step(inside, tokens, negatives, weights):
@@ -984,7 +1018,10 @@
     kinds = (units // 2, local)
     high = width // 8 if inside else width
     shapes = [((micro, share, width), BF), ((micro, share, width), BF), ((tall, width), F32)]
-    shapes += [((layers, 2, 2, high, w), F32) for w in kinds]
+    if inside:
+        shapes += [((layers, 2, high, units), F32), ((layers, 2, 2, high, local), F32)]
+    else:
+        shapes += [((layers, 2, 2, high, w), F32) for w in kinds]
     vm = pl.BlockSpec(memory_space=pltpu.VMEM)
     hb = pl.BlockSpec(memory_space=pl.ANY)
     sm = pl.BlockSpec(memory_space=pltpu.SMEM)
@@ -1031,7 +1068,7 @@
     ]
     scratch += line_scratch(streams, rows, width)
     if inside:
-        scratch += [pltpu.SemaphoreType.REGULAR(())]
+        scratch += [pltpu.SemaphoreType.REGULAR(()), v(*shapes[3]), v(*shapes[4]), dma((2, layers))]
         for w in kinds + kinds[1:]:
             scratch += [v((2, 2, width // n, w), BF) for n in (2, 4, 8)]
         scratch += [dma((2, 3, 2))] * 4
@@ -1052,7 +1089,7 @@
         functools.partial(step_kernel, inside),
         out_shape=[jax.ShapeDtypeStruct(*s) for s in shapes],
         in_specs=[hb, vm, sm, hb, vm, sm, hb] + [hb, vm, hb, vm, hb, vm, hb, vm, vm, vm],
-        out_specs=[vm] * 3 + [vm if inside else hb] * 2,
+        out_specs=[vm] * 3 + [hb] * 2,
         scratch_shapes=scratch,
         compiler_params=pltpu.CompilerParams(
             collective_id=0, has_side_effects=True, vmem_limit_bytes=VMEM_LIMIT
@@ -1065,20 +1102,18 @@
                    o_expand, o_ebias, o_shrink, o_sbias, o_gain, o_shift, o_loss):
     width = vec.shape[1]
     local = small.shape[4]
-    half = big.shape[4]
+    o_acts[:, 0] = acts[...]
+    o_in[:, 0] = g_in[...]
+    for l in range(layers):
+        o_shrink[l] = big[l, 0]
+        o_expand[l] = big[l, 1]
+        for j in range(3):
+            o_attend[l, j] = small[l, j // 2, j % 2]
+        o_merge[l] = small[l, 1, 1].T
     group = lax.axis_index("dp") * lax.axis_size("rep") + lax.axis_index("rep")
     blocks = width // size
     own = pltpu.roll(vec[...], ((blocks - group) % blocks) * size, axis=1)[:, :size]
-    o_acts[:, 0] = acts[...]
-    o_in[:, 0] = g_in[...]
     for l in range(layers):
-        for h in (0, 1):
-            cols = slice(h * half, (h + 1) * half)
-            o_shrink[l, :, cols] = big[l, 0, h]
-            o_expand[l, :, cols] = big[l, 1, h]
-        for j in range(3):
-            o_attend[l, j] = small[l, j // 2, j % 2]
-        o_merge[l] = small[l, 1, 1].T
         row = 7 * l
         o_gain[l] = own[row : row + 2]
         o_shift[l] = own[row + 2 : row + 4]
@@ -1091,7 +1126,7 @@
 
 def run_outputs(acts, g_in, vec, big, small):
     micro, share, width = acts.shape
-    layers, _, _, size, half = big.shape
+    layers, _, size, units = big.shape
     local = small.shape[4]
     shapes = [
         ((micro, 1, share, width), BF),
@@ -1100,9 +1135,9 @@
         ((layers, 2, local), F32),
         ((layers, local, size), F32),
         ((layers, size), F32),
-        ((layers, size, 2 * half), F32),
+        ((layers, size, units), F32),
         ((layers, width), F32),
-        ((layers, size, 2 * half), F32),
+        ((layers, size, units), F32),
         ((layers, size), F32),
         ((layers, 2, size), F32),
         ((layers, 2, size), F32),
@@ -1147,6 +1182,7 @@
         g_big = lax.psum_scatter(g_big, groups, scatter_dimension=3, tiled=True)
         g_small = lax.psum_scatter(g_small, groups, scatter_dimension=3, tiled=True)
         vec = lax.psum(vec, groups)
+        g_big = g_big.transpose(0, 1, 3, 2, 4).reshape(g_big.shape[:2] + (g_big.shape[3], -1))
     outs = run_outputs(acts, g_in, vec, g_big, g_small)
     loss = outs[12].reshape(()) / (micro * lax.axis_size("dp") * lax.axis_size("rep"))
     return (

time: 259 us -> 257 us (level)
  no operation moved by 1% of the time
where the time goes in v7:
time: 257 us
  Pallas kernels  254 us (99%)
    pallas_call x1, Pallas kernels, run_step(): pl.pallas_call(functools.partial(step_kernel, inside), out_shape=[jax.Sha...  251 us

profile of v7, /device:TPU:0, one launch (start us, length us, event | category | flops | bytes accessed | tf_op | source)
XLA Modules:
  0.0 256.7 jit_solution(1948629049923883456)
XLA Ops:
  0.7 251.1 %training_step.1 = (bf16[2,64,768]{2,1,0:T(8,128)(2,1)}, bf16[2,64,768]{2,1,0:T(8,128)(2,1)}, f32[24,768]{1,0:T(8,128)}, f32[2,2,96,768]{3,2,1,0:T(8,128)}, f32[2,2,2,96,192]{4,3,2,1,0:T(8,128)}) custom-call(bf16[2,1,256,768]{3,2,1,0:T(8,128)(2,1)} %refs_0_.1, s32[2,1,256]{2,1,0:T(1,128)} %refs_1_.1, s32[2]{0:T(128)} %bitcast.7, ...), custom_call_target="tpu_custom_call" | custom-call | tf_op jit(solution)/shard_map/training_step/pallas_call | solution.py:1088
  251.8 3.1 %outputs.1 = (bf16[2,1,64,768]{3,2,1,0:T(8,128)(2,1)}, bf16[2,1,64,768]{3,2,1,0:T(8,128)(2,1)}, f32[2,3,96,192]{3,2,1,0:T(8,128)}, f32[2,2,192]{2,1,0:T(2,128)},...) custom-call(bf16[2,64,768]{2,1,0:T(8,128)(2,1)} %get-tuple-element.3, ...), custom_call_target="tpu_custom_call" | custom-call | tf_op jit(solution)/shard_map/outputs/pallas_call | solution.py:1147

commit v8 on v7

--- a/solution.py
+++ b/solution.py
@@ -839,15 +839,14 @@
             tick(i, 2 * half)
             inner[span] = nt(low[span], ws[0, layer])
 
-            if half == 1:
-                @pl.when((step == 0) & (m == 0))
-                def _():
-                    queue.respond(micro - 1)
-
             tick(i, 2 * half + 1)
             tiles(last_row, slopes, None, first_row)
             part[s, span] = nt(dinner[span], we[0, layer])
             line.begin(s, False, range(half * CHUNKS // 2, (half + 1) * CHUNKS // 2))
+            if half == 0:
+                @pl.when((step == 0) & (m == 0))
+                def _():
+                    queue.respond(micro - 1)
 
         @pl.when(step > 0)
         def _():

time: 257 us -> 256 us (level)
  no operation moved by 1% of the time
where the time goes in v8:
time: 256 us
  Pallas kernels  254 us (99%)
    pallas_call x1, Pallas kernels, run_step(): pl.pallas_call(functools.partial(step_kernel, inside), out_shape=[jax.Sha...  250 us

profile of v8, /device:TPU:0, one launch (start us, length us, event | category | flops | bytes accessed | tf_op | source)
XLA Modules:
  0.0 256.0 jit_solution(8548931902223514559)
XLA Ops:
  0.7 250.4 %training_step.1 = (bf16[2,64,768]{2,1,0:T(8,128)(2,1)}, bf16[2,64,768]{2,1,0:T(8,128)(2,1)}, f32[24,768]{1,0:T(8,128)}, f32[2,2,96,768]{3,2,1,0:T(8,128)}, f32[2,2,2,96,192]{4,3,2,1,0:T(8,128)}) custom-call(bf16[2,1,256,768]{3,2,1,0:T(8,128)(2,1)} %refs_0_.1, s32[2,1,256]{2,1,0:T(1,128)} %refs_1_.1, s32[2]{0:T(128)} %bitcast.7, ...), custom_call_target="tpu_custom_call" | custom-call | tf_op jit(solution)/shard_map/training_step/pallas_call | solution.py:1087
  251.0 3.1 %outputs.1 = (bf16[2,1,64,768]{3,2,1,0:T(8,128)(2,1)}, bf16[2,1,64,768]{3,2,1,0:T(8,128)(2,1)}, f32[2,3,96,192]{3,2,1,0:T(8,128)}, f32[2,2,192]{2,1,0:T(2,128)},...) custom-call(bf16[2,64,768]{2,1,0:T(8,128)(2,1)} %get-tuple-element.3, ...), custom_call_target="tpu_custom_call" | custom-call | tf_op jit(solution)/shard_map/outputs/pallas_call | solution.py:1146

commit v9 on v8

--- a/solution.py
+++ b/solution.py
@@ -518,7 +518,12 @@
                 n2[lp, m, r] = normed.astype(BF)
                 inv[lp, m, r, 64:128] = jnp.broadcast_to(inverse, (TILE, 64))
 
-        tiles(rows, norm, lambda t: line.settle(s, 1, t, narrow))
+        def own_half(r):
+            @pl.when(line.end & ((r.start < rows // 2) == line.lower))
+            def _():
+                norm(r)
+
+        tiles(rows, norm if narrow is False else own_half, lambda t: line.settle(s, 1, t, narrow))
         line.release(s, 1, narrow)
 
     def attention_pass(layer, s):
@@ -680,10 +685,14 @@
 
     def last_key(m):
         second_norm(layers - 1, 1, m, line.part.shape[0] > 0)
-        kpart[m] = pool(m)
+
+        @pl.when(line.mid)
+        def _():
+            kpart[m] = jnp.zeros_like(kpart[m])
 
         @pl.when(line.end)
         def _():
+            kpart[m] = pool(m)
             for d in (1, 2, 3):
                 kshare(m, d).start()
 

time: 256 us -> 257 us (level)
  no operation moved by 1% of the time
where the time goes in v9:
time: 257 us; the launch traced here: 256 us
  Pallas kernels  254 us (99%)
    pallas_call x1, Pallas kernels, run_step(): pl.pallas_call(functools.partial(step_kernel, inside), out_shape=[jax.Sha...  251 us

profile of v9, /device:TPU:0, one launch (start us, length us, event | category | flops | bytes accessed | tf_op | source)
XLA Modules:
  0.0 256.5 jit_solution(2297017300622712319)
XLA Ops:
  0.7 250.9 %training_step.1 = (bf16[2,64,768]{2,1,0:T(8,128)(2,1)}, bf16[2,64,768]{2,1,0:T(8,128)(2,1)}, f32[24,768]{1,0:T(8,128)}, f32[2,2,96,768]{3,2,1,0:T(8,128)}, f32[2,2,2,96,192]{4,3,2,1,0:T(8,128)}) custom-call(bf16[2,1,256,768]{3,2,1,0:T(8,128)(2,1)} %refs_0_.1, s32[2,1,256]{2,1,0:T(1,128)} %refs_1_.1, s32[2]{0:T(128)} %bitcast.7, ...), custom_call_target="tpu_custom_call" | custom-call | tf_op jit(solution)/shard_map/training_step/pallas_call | solution.py:1096
  251.5 3.1 %outputs.1 = (bf16[2,1,64,768]{3,2,1,0:T(8,128)(2,1)}, bf16[2,1,64,768]{3,2,1,0:T(8,128)(2,1)}, f32[2,3,96,192]{3,2,1,0:T(8,128)}, f32[2,2,192]{2,1,0:T(2,128)},...) custom-call(bf16[2,64,768]{2,1,0:T(8,128)(2,1)} %get-tuple-element.3, ...), custom_call_target="tpu_custom_call" | custom-call | tf_op jit(solution)/shard_map/outputs/pallas_call | solution.py:1155
